TPU v7x, 512 devices: a whole 4x8x8 slice. The times are simulated.
512 devices in a mesh: section: 16 (over y, core), lat: 32 (over z, x).
Axes of the slice: x: 4, y: 8, z: 8, core: 2. Of those that a mesh axis runs over, the one named last changes fastest.
Arguments:
- section_input: bfloat16 [16, 64, 128, 1024], P('section', 'lat'), may hold values from -6 to 6
- handoff: bfloat16 [16, 64, 128, 1024], P('section', 'lat'), may hold values from -6 to 6
- loss_grad: bfloat16 [64, 128, 1024], P('lat'), may hold values from -6 to 6
- w_first: bfloat16 [16, 2, 2, 1024, 128], P('section'), may hold values from -0.375 to 0.375
- w_second: bfloat16 [16, 2, 2, 1024, 128], P('section'), may hold values from -0.375 to 0.375
- bias: float32 [16, 2, 2, 2, 1024], P('section'), may hold values from -3 to 3
- kept: int32 [16, 2, 8], P('section'), may hold values from 1 to 32, as said below
Outputs:
- handed_on: bfloat16 [16, 64, 128, 1024], P('section', 'lat')
- grad_first: float32 [16, 2, 2, 1024, 128], P('section', None, None, 'lat')
- grad_second: float32 [16, 2, 2, 1024, 128], P('section', None, None, 'lat')
- grad_bias: float32 [16, 2, 2, 2, 1024], P('section', None, None, None, 'lat')
Inputs may be any that keep to these rules, and one draw needn't show every extreme that they name: `kept`: in every section and block layer one channel block keeps 32 modes and another keeps 1.
All inputs are finite; a program needn't handle non-finite values.
Results may differ from a plain program's by a relative error of at most 0.025.
Values may be sent and summed in bfloat16 or wider, within the bound.
No kernel may reach another device: no remote copies, remote signals or barrier semaphores. Data moves between devices by JAX's collectives and lax.ppermute only.
A program may use at most 64 MiB of HBM per device.

v0:
```python
import math

import jax
import jax.numpy as jnp
from jax import lax
from jax.sharding import PartitionSpec as P

LAYERS = 2


def passed_along(value, axis, steps):
    count = lax.axis_size(axis)
    leading, last = (max(0, -steps), min(count, count - steps))
    return lax.ppermute(value, axis, [(source, source + steps) for source in range(leading, last)])


def lon_tables(lon, freqs):
    cells = jnp.arange(lon, dtype=jnp.int32)
    phase = (freqs[:, None] * cells[None, :] % lon).astype(jnp.float32) * (2.0 * math.pi / lon)
    scale = 1.0 / math.sqrt(lon)
    forward = jnp.stack([jnp.cos(phase) * scale, -jnp.sin(phase) * scale])
    weights = jnp.where(freqs == 0, 1.0, 2.0).astype(jnp.float32)
    inverse = forward * weights[None, :, None]
    return (forward.astype(jnp.bfloat16), inverse.astype(jnp.bfloat16))


def lat_table(lat):
    rows = jnp.arange(lat, dtype=jnp.int32)
    phase = (rows[:, None] * rows[None, :] % lat).astype(jnp.float32) * (2.0 * math.pi / lat)
    scale = 1.0 / math.sqrt(lat)
    cosine = jnp.cos(phase) * scale
    sine = jnp.sin(phase) * scale
    upper = jnp.concatenate([cosine, sine], axis=1)
    lower = jnp.concatenate([-sine, cosine], axis=1)
    return jnp.concatenate([upper, lower], axis=0).astype(jnp.bfloat16)


def complex_mix(real, imag, weight):

    def prod(left, right):
        return jnp.einsum("rnb,nbh->rnh", left, right, preferred_element_type=jnp.float32)

    return (
        prod(real, weight[0]) - prod(imag, weight[1]),
        prod(real, weight[1]) + prod(imag, weight[0]),
    )


def complex_adjoint(real, imag, weight):

    def prod(left, right):
        return jnp.einsum("rnh,nbh->rnb", left, right, preferred_element_type=jnp.float32)

    return (
        prod(real, weight[0]) + prod(imag, weight[1]),
        prod(imag, weight[0]) - prod(real, weight[1]),
    )


def outer_sum(left, right):

    def prod(first, second):
        return jnp.einsum("rnb,rnh->nbh", first, second, preferred_element_type=jnp.float32)

    return jnp.stack(
        [
            prod(left[0], right[0]) + prod(left[1], right[1]),
            prod(left[0], right[1]) - prod(left[1], right[0]),
        ]
    )


def to_modes(grid_part):
    return lax.all_to_all(grid_part, "lat", split_axis=2, concat_axis=1, tiled=True)


def to_grid(mode_part):
    return lax.all_to_all(mode_part, "lat", split_axis=1, concat_axis=2, tiled=True)


def on_device(section_input, handoff, loss_grad, w_first, w_second, bias, kept):
    lat_count = lax.axis_size("lat")
    section_count = lax.axis_size("section")
    lon = section_input.shape[2]
    channels = section_input.shape[3]
    width = w_first.shape[-1]
    blocks = channels // width
    lat_all = section_input.shape[1] * lat_count
    per_dev = lon // 2 // lat_count
    slots = jnp.arange(per_dev * lat_count, dtype=jnp.int32)
    freqs = slots % per_dev * lat_count + slots // per_dev
    tab_fwd, tab_inv = lon_tables(lon, freqs)
    mixer = lat_table(lat_all)
    mixer_back = mixer.T
    own_modes = jnp.arange(per_dev, dtype=jnp.int32) * lat_count + lax.axis_index("lat")
    own_rows = jnp.tile(own_modes, lat_all)
    row_count = lat_all * per_dev
    received = passed_along(handoff[0], "section", -1)
    cotangent = jnp.where(lax.axis_index("section") == section_count - 1, loss_grad, received)

    def params_of(layer):
        w_one = w_first[0, layer].reshape(2, blocks, width, width)
        w_two = w_second[0, layer].reshape(2, blocks, width, width)
        b_one = bias[0, layer, 0].reshape(2, blocks, width)
        b_two = bias[0, layer, 1].reshape(2, blocks, width)
        mask = (own_rows[:, None] < kept[0, layer][None, :]).astype(jnp.float32)[:, :, None]
        return (w_one, w_two, b_one, b_two, mask)

    def layer_backward(grad, z, pre, params):
        hidden = jax.nn.silu(pre).astype(jnp.bfloat16)
        du = jnp.einsum("rqj,ijc->riqc", tab_inv, grad, preferred_element_type=jnp.float32).astype(
            jnp.bfloat16
        )
        du_modes = to_modes(du)
        dout = jnp.dot(mixer, du_modes.reshape(2 * lat_all, -1), preferred_element_type=jnp.float32)
        dout = (dout.reshape(2, row_count, blocks, width) * params[4]).astype(jnp.bfloat16)
        dhid_r, dhid_i = complex_adjoint(dout[0], dout[1], params[1])
        sig = jax.nn.sigmoid(pre)
        dpre = (jnp.stack([dhid_r, dhid_i]) * (sig * (1.0 + pre * (1.0 - sig)))).astype(
            jnp.bfloat16
        )
        dz_r, dz_i = complex_adjoint(dpre[0], dpre[1], params[0])
        dz = jnp.stack([dz_r, dz_i]).astype(jnp.bfloat16)
        da = jnp.dot(mixer_back, dz.reshape(2 * lat_all, -1), preferred_element_type=jnp.float32)
        da = da.astype(jnp.bfloat16).reshape(2, lat_all, per_dev, channels)
        da_grid = to_grid(da)
        spatial = jnp.einsum("rqj,riqc->ijc", tab_fwd, da_grid, preferred_element_type=jnp.float32)
        dx = (grad.astype(jnp.float32) + spatial).astype(jnp.bfloat16)
        g_one = outer_sum(z, dpre).reshape(2, channels, width)
        g_two = outer_sum(hidden, dout).reshape(2, channels, width)
        g_bias = jnp.stack(
            [
                jnp.sum(dpre.astype(jnp.float32), axis=1).reshape(2, channels),
                jnp.sum(dout.astype(jnp.float32), axis=1).reshape(2, channels),
            ]
        )
        return (dx, g_one, g_two, g_bias)

    params = [params_of(layer) for layer in range(LAYERS)]
    inputs, states = ([section_input[0]], [])
    for layer in range(LAYERS):
        spectral_params = params[layer]
        spec = jnp.einsum(
            "rqj,ijc->riqc", tab_fwd, inputs[layer], preferred_element_type=jnp.float32
        ).astype(jnp.bfloat16)
        gathered = to_modes(spec)
        spectral_z = jnp.dot(
            mixer, gathered.reshape(2 * lat_all, -1), preferred_element_type=jnp.float32
        )
        spectral_z = spectral_z.astype(jnp.bfloat16).reshape(2, row_count, blocks, width)
        pre_r, pre_i = complex_mix(spectral_z[0], spectral_z[1], spectral_params[0])
        z = spectral_z
        pre = jnp.stack([pre_r, pre_i]) + spectral_params[2][:, None]
        states.append((z, pre))
        if layer + 1 < LAYERS:
            layer_params = params[layer]
            layer_hidden = jax.nn.silu(pre).astype(jnp.bfloat16)
            out_r, out_i = complex_mix(layer_hidden[0], layer_hidden[1], layer_params[1])
            out = ((jnp.stack([out_r, out_i]) + layer_params[3][:, None]) * layer_params[4]).astype(
                jnp.bfloat16
            )
            u = jnp.dot(
                mixer_back, out.reshape(2 * lat_all, -1), preferred_element_type=jnp.float32
            )
            u = u.astype(jnp.bfloat16).reshape(2, lat_all, per_dev, channels)
            back = to_grid(u)
            y = jnp.einsum("rqj,riqc->ijc", tab_inv, back, preferred_element_type=jnp.float32)
            inputs.append((inputs[layer].astype(jnp.float32) + y).astype(jnp.bfloat16))
    grad = cotangent
    ones, twos, biases = ([None] * LAYERS, [None] * LAYERS, [None] * LAYERS)
    for layer in reversed(range(LAYERS)):
        z, pre = states[layer]
        grad, g_one, g_two, g_bias = layer_backward(grad, z, pre, params[layer])
        ones[layer], twos[layer], biases[layer] = (g_one, g_two, g_bias)
    grad_first, grad_second, grad_bias = (
        lax.psum_scatter(
            jnp.stack(ones).astype(jnp.bfloat16), "lat", scatter_dimension=2, tiled=True
        ).astype(jnp.float32),
        lax.psum_scatter(
            jnp.stack(twos).astype(jnp.bfloat16), "lat", scatter_dimension=2, tiled=True
        ).astype(jnp.float32),
        lax.psum_scatter(
            jnp.stack(biases).astype(jnp.bfloat16), "lat", scatter_dimension=3, tiled=True
        ).astype(jnp.float32),
    )
    return (grad[None], grad_first[None], grad_second[None], grad_bias[None])


def solution(mesh):
    return jax.shard_map(
        on_device,
        mesh=mesh,
        in_specs=(
            P("section", "lat", None, None),
            P("section", "lat", None, None),
            P("lat", None, None),
            P("section", None, None, None, None),
            P("section", None, None, None, None),
            P("section", None, None, None, None),
            P("section", None, None),
        ),
        out_specs=(
            P("section", "lat", None, None),
            P("section", None, None, "lat", None),
            P("section", None, None, "lat", None),
            P("section", None, None, None, "lat"),
        ),
        check_vma=False,
    )
```

profile of v0, /device:TPU:56, one launch (start us, length us, event | category | flops | bytes accessed | tf_op | source)
XLA Modules:
  0.0 878.3 jit_solution(9506510881458931162)
XLA Ops:
  10.1 13.3 %all-to-all-start.1 = ((bf16[2,2,64,1024]{3,1,0,2:T(2,128)(2,1)}), bf16[2,2,64,1024]{3,1,0,2:T(2,128)(2,1)S(1)}, u32[]{:S(2)}, u32[]{:S(2)}) async-start(bf16[2,2,64,1024]{3,1,0,2:T(2,128)(2,1)} %copy.136), calls=%async_computation.1 | async-start | bytes 1048576 | tf_op jit(solution)/shard_map/all_to_all | solution.py:74
  24.4 2.4 collective-permute-start
  31.1 2.7 collective-permute-done
  36.5 4.6 all-to-all-done.1
  41.1 5.1 all-to-all-start
  54.8 2.2 copy.143
  57.0 5.8 all-to-all-done
  62.8 4.8 all-to-all-start.2
  71.6 2.4 reshape.334
  73.9 10.1 %all-to-all-done.2 = bf16[2,64,2,1024]{3,2,0,1:T(2,128)(2,1)} async-done(((bf16[2,64,2,1024]{3,2,0,1:T(2,128)(2,1)}), bf16[2,64,2,1024]{3,2,0,1:T(2,128)(2,1)}, u32[]{:S(2)}, u32[]{:S(2)}) %all-to-all-start.2) | async-done | bytes 524320 | tf_op jit(solution)/shard_map/all_to_all | solution.py:78
  84.1 2.3 copy.145
  86.4 2.6 fusion.4
  88.9 2.4 copy.148
  91.3 4.6 all-to-all-start.3
  100.3 12.1 %all-to-all-done.3 = bf16[2,2,64,1024]{3,0,1,2:T(2,128)(2,1)} async-done(((bf16[2,2,64,1024]{3,0,1,2:T(2,128)(2,1)}), bf16[2,2,64,1024]{3,0,1,2:T(2,128)(2,1)}, u32[]{:S(2)}, u32[]{:S(2)}) %all-to-all-start.3) | async-done | bytes 524320 | tf_op jit(solution)/shard_map/all_to_all | solution.py:74
  120.8 2.1 convert_element_type.180
  122.9 2.1 convolution_convert_fusion.1
  125.1 2.2 reshape.338
  127.3 2.2 copy.155
  129.5 4.8 all-to-all-start.4
  137.9 12.4 %all-to-all-done.4 = bf16[2,64,2,1024]{3,2,0,1:T(2,128)(2,1)} async-done(((bf16[2,64,2,1024]{3,2,0,1:T(2,128)(2,1)}), bf16[2,64,2,1024]{3,2,0,1:T(2,128)(2,1)}, u32[]{:S(2)}, u32[]{:S(2)}) %all-to-all-start.4) | async-done | bytes 524320 | tf_op jit(solution)/shard_map/all_to_all | solution.py:78
  150.3 2.2 copy.231
  158.5 4.6 all-to-all-start.5
  167.6 11.2 %all-to-all-done.5 = bf16[2,2,64,1024]{3,0,1,2:T(2,128)(2,1)} async-done(((bf16[2,2,64,1024]{3,0,1,2:T(2,128)(2,1)}), bf16[2,2,64,1024]{3,0,1,2:T(2,128)(2,1)}, u32[]{:S(2)}, u32[]{:S(2)}) %all-to-all-start.5) | async-done | bytes 524320 | tf_op jit(solution)/shard_map/all_to_all | solution.py:74
  181.7 2.4 reshape.340
  193.9 2.0 copy.205
  195.9 3.6 reshape.354
  200.4 2.0 maximum_maximum_fusion
  210.7 4.4 all-to-all-start.6
  215.1 206.7 %reduce-scatter.10.cloned.1.call-done = bf16[32,8]{1,0:T(8,128)(2,1)} async-done(((bf16[1024,8]{1,0:T(8,128)(2,1)}), bf16[32,8]{1,0:T(8,128)(2,1)}) %reduce-scatter.10.cloned.1.call-update) | async-done | bytes 528
  426.0 220.0 %reduce-scatter.6.cloned.1.call-done = bf16[2,2,32,128]{3,2,1,0:T(8,128)(2,1)} async-done(((bf16[2,2,1024,128]{3,2,1,0:T(8,128)(2,1)}), bf16[2,2,32,128]{3,2,1,0:T(8,128)(2,1)}) %reduce-scatter.6.cloned.1.call-update) | async-done | bytes 32784 | tf_op jit(solution)/shard_map/reduce_scatter | solution.py:176
  647.4 223.0 %reduce-scatter.8.cloned.1.call-done = bf16[2,2,32,128]{3,2,1,0:T(8,128)(2,1)} async-done(((bf16[2,2,1024,128]{3,2,1,0:T(8,128)(2,1)}), bf16[2,2,32,128]{3,2,1,0:T(8,128)(2,1)}) %reduce-scatter.8.cloned.1.call-update) | async-done | bytes 32784 | tf_op jit(solution)/shard_map/reduce_scatter | solution.py:179
  (210 shorter events, 78.3 us)
Async XLA Ops:
  10.1 13.3 %copy-start.31 = (bf16[1,2,128,1024]{3,2,1,0:T(8,128)(2,1)S(1)}, bf16[1,2,128,1024]{3,2,1,0:T(8,128)(2,1)}, u32[]{:S(2)}) copy-start(bf16[1,2,128,1024]{3,2,1,0:T(8,128)(2,1)} %param.8) | copy-start | bytes 1572868
  10.1 31.0 %all-to-all-start.1 = ((bf16[2,2,64,1024]{3,1,0,2:T(2,128)(2,1)}), bf16[2,2,64,1024]{3,1,0,2:T(2,128)(2,1)S(1)}, u32[]{:S(2)}, u32[]{:S(2)}) async-start(bf16[2,2,64,1024]{3,1,0,2:T(2,128)(2,1)} %copy.136), calls=%async_computation.1 | async-start | bytes 1048576 | tf_op jit(solution)/shard_map/all_to_all | solution.py:74
  23.4 4.2 copy-start.34
  23.4 4.9 copy-start.32
  24.4 9.4 %collective-permute-start = (bf16[2,128,1024]{1,2,0:T(8,128)(2,1)}, bf16[2,128,1024]{1,2,0:T(8,128)(2,1)}, u32[]{:S(2)}, u32[]{:S(2)}) collective-permute-start(bf16[2,128,1024]{1,2,0:T(8,128)(2,1)} %bitcast), channel_id=1, source_target_pairs={{32,0},{64,32},{96,64},{128,96},{160,128},{192,160},{224,192},{256... | collective-permute-start | bytes 1572872 | tf_op jit(solution)/shard_map/ppermute | solution.py:14
  28.6 5.3 copy-start.18
  28.6 1.7 copy-start.26
  30.3 85.3 %copy-start.4 = (bf16[1,1,1,1024,128]{4,3,2,1,0:T(8,128)(2,1)}, bf16[1,1,1,1024,128]{4,3,2,1,0:T(8,128)(2,1)S(1)}, u32[]{:S(2)}) copy-start(bf16[1,1,1,1024,128]{4,3,2,1,0:T(8,128)(2,1)S(1)} %get-tuple-element.35) | copy-start | bytes 786436
  31.1 19.1 %copy-start.2 = (bf16[1,1,1,1024,128]{4,3,2,1,0:T(8,128)(2,1)}, bf16[1,1,1,1024,128]{4,3,2,1,0:T(8,128)(2,1)S(1)}, u32[]{:S(2)}) copy-start(bf16[1,1,1,1024,128]{4,3,2,1,0:T(8,128)(2,1)S(1)} %get-tuple-element.31) | copy-start | bytes 786436
  31.1 19.3 %copy-start = (bf16[1,1,1,1024,128]{4,3,2,1,0:T(8,128)(2,1)}, bf16[1,1,1,1024,128]{4,3,2,1,0:T(8,128)(2,1)S(1)}, u32[]{:S(2)}) copy-start(bf16[1,1,1,1024,128]{4,3,2,1,0:T(8,128)(2,1)S(1)} %get-tuple-element.30) | copy-start | bytes 786436
  41.1 21.7 %all-to-all-start = ((bf16[2,2,64,1024]{3,0,1,2:T(2,128)(2,1)}), bf16[2,2,64,1024]{3,0,1,2:T(2,128)(2,1)}, u32[]{:S(2)}, u32[]{:S(2)}) async-start(bf16[2,2,64,1024]{3,0,1,2:T(2,128)(2,1)} %copy.131), calls=%async_computation | async-start | bytes 1048576 | tf_op jit(solution)/shard_map/all_to_all | solution.py:74
  57.0 10.7 %copy-start.22 = (bf16[1,2,128,1024]{3,2,1,0:T(8,128)(2,1)S(1)}, bf16[1,2,128,1024]{3,2,1,0:T(8,128)(2,1)}, u32[]{:S(2)}) copy-start(bf16[1,2,128,1024]{3,2,1,0:T(8,128)(2,1)} %param.7) | copy-start | bytes 1572868
  62.8 21.2 %all-to-all-start.2 = ((bf16[2,64,2,1024]{3,2,0,1:T(2,128)(2,1)}), bf16[2,64,2,1024]{3,2,0,1:T(2,128)(2,1)}, u32[]{:S(2)}, u32[]{:S(2)}) async-start(bf16[2,64,2,1024]{3,2,0,1:T(2,128)(2,1)} %copy.143), calls=%async_computation.2 | async-start | bytes 1048576 | tf_op jit(solution)/shard_map/all_to_all | solution.py:78
  84.1 2.3 copy-start.33
  91.3 21.1 %all-to-all-start.3 = ((bf16[2,2,64,1024]{3,0,1,2:T(2,128)(2,1)}), bf16[2,2,64,1024]{3,0,1,2:T(2,128)(2,1)}, u32[]{:S(2)}, u32[]{:S(2)}) async-start(bf16[2,2,64,1024]{3,0,1,2:T(2,128)(2,1)} %copy.148), calls=%async_computation.3 | async-start | bytes 1048576 | tf_op jit(solution)/shard_map/all_to_all | solution.py:74
  96.0 1.6 copy-start.19
  115.9 1.3 copy-start.20
  115.9 1.6 copy-start.21
  116.2 1.7 copy-start.12
  129.5 20.8 %all-to-all-start.4 = ((bf16[2,64,2,1024]{3,2,0,1:T(2,128)(2,1)}), bf16[2,64,2,1024]{3,2,0,1:T(2,128)(2,1)}, u32[]{:S(2)}, u32[]{:S(2)}) async-start(bf16[2,64,2,1024]{3,2,0,1:T(2,128)(2,1)} %copy.155), calls=%async_computation.4 | async-start | bytes 1048576 | tf_op jit(solution)/shard_map/all_to_all | solution.py:78
  135.4 1.4 copy-start.13
  158.5 20.3 %all-to-all-start.5 = ((bf16[2,2,64,1024]{3,0,1,2:T(2,128)(2,1)}), bf16[2,2,64,1024]{3,0,1,2:T(2,128)(2,1)}, u32[]{:S(2)}, u32[]{:S(2)}) async-start(bf16[2,2,64,1024]{3,0,1,2:T(2,128)(2,1)} %copy.158), calls=%async_computation.5 | async-start | bytes 1048576 | tf_op jit(solution)/shard_map/all_to_all | solution.py:74
  163.1 258.6 %reduce-scatter.10.cloned.1.call-start = ((), (), s32[]{:S(2)}) async-start(), calls=%async_computation.12 | async-start | bytes 270336
  163.2 1.3 copy-start.24
  184.0 1.6 copy-start.3
  187.2 1.2 copy-start.9
  190.9 2.0 copy-start.25
  195.9 3.7 copy-start.29
  195.9 3.7 copy-start.30
  199.5 446.5 %reduce-scatter.6.cloned.1.call-start = ((), (), s32[]{:S(2)}) async-start(), calls=%async_computation.10 | async-start | bytes 1081344 | tf_op jit(solution)/shard_map/reduce_scatter | solution.py:176
  202.5 667.8 %reduce-scatter.8.cloned.1.call-start = ((), (), s32[]{:S(2)}) async-start(), calls=%async_computation.11 | async-start | bytes 1081344 | tf_op jit(solution)/shard_map/reduce_scatter | solution.py:179
  210.7 212.5 %all-to-all-start.6 = ((bf16[2,64,2,1024]{3,2,0,1:T(2,128)(2,1)}), bf16[2,64,2,1024]{3,2,0,1:T(2,128)(2,1)S(1)}, u32[]{:S(2)}, u32[]{:S(2)}) async-start(bf16[2,64,2,1024]{3,2,0,1:T(2,128)(2,1)} %copy.162), calls=%async_computation.6 | async-start | bytes 1048576 | tf_op jit(solution)/shard_map/all_to_all | solution.py:78
  (15 other events, 13.9 us)
Sparse Core Ops, SparseCore 0:
  199.6 222.0 reduce-scatter.9
  426.8 219.1 reduce-scatter.5
  651.0 219.2 reduce-scatter.7
where the time goes:
time: 881 us; the launch traced here: 878 us
  waiting for transfers between devices  709 us (80%)
  local copies, waits for them, and re-layouts  60.9 us (7%)
  starting transfers between devices  44.5 us (5%)
  matrix products  36.6 us (4%)
  between operations  14.7 us (2%)
  other arithmetic  13.1 us (1%)
    reduce_scatter x1, waiting for transfers between devices, on_device(): lax.psum_scatter(jnp.stack(twos).astype(jnp.bfloat16), 'lat', scatter_dim...  223 us
    reduce_scatter x1, waiting for transfers between devices, on_device(): lax.psum_scatter(jnp.stack(ones).astype(jnp.bfloat16), 'lat', scatter_dim...  220 us
    unnamed x4, waiting for transfers between devices  207 us
    all_to_all x4, waiting for transfers between devices, to_modes(): lax.all_to_all(grid_part, 'lat', split_axis=2, concat_axis=1, tiled=True)  33.7 us
    all_to_all x4, starting transfers between devices, to_modes(): lax.all_to_all(grid_part, 'lat', split_axis=2, concat_axis=1, tiled=True)  27.6 us
    all_to_all x3, waiting for transfers between devices, to_grid(): lax.all_to_all(mode_part, 'lat', split_axis=1, concat_axis=2, tiled=True)  22.5 us
    unnamed x86, local copies, waits for them, and re-layouts  19.4 us
  transfers between devices with their start and end apart: 11, of which 10 were waited for; matrix products, arithmetic and copies ran while one was open for 5% of the time, Pallas kernels for 0%

commit v1 on v0

v1 whole, which is shorter than its diff:
```python
import math

import jax
import jax.numpy as jnp
import numpy as np
from jax import lax
from jax.experimental import pallas as pl
from jax.experimental.pallas import tpu as pltpu
from jax.sharding import PartitionSpec as P

LAYERS = 2
MAXK = 32
F32 = jnp.float32
BF16 = jnp.bfloat16


def lon_table(lon, rows, quarters, weighted):
    per = MAXK // quarters
    freqs = np.arange(MAXK)
    phase = 2.0 * math.pi * ((freqs[:, None] * np.arange(lon)[None, :]) % lon) / lon
    table = np.stack([np.cos(phase), -np.sin(phase)]) / math.sqrt(lon)
    table[1, 0] = 0.0
    table = table.astype(jnp.bfloat16).astype(np.float32)
    if weighted:
        table = table * np.where(freqs == 0, 1.0, 2.0)[None, :, None]
    split = table.reshape(2, quarters, per, lon).transpose(1, 0, 2, 3)
    full = np.zeros((quarters, 2, rows, per, rows, lon), np.float32)
    for row in range(rows):
        full[:, :, row, :, row, :] = split
    return full.reshape(quarters * 2 * rows * per, rows * lon).astype(jnp.bfloat16)


def lat_table(lat, rows):
    phase = 2.0 * math.pi * ((np.arange(lat)[:, None] * np.arange(lat)[None, :]) % lat) / lat
    cosine = np.cos(phase) / math.sqrt(lat)
    sine = np.sin(phase) / math.sqrt(lat)
    mixer = np.block([[cosine, sine], [-sine, cosine]])
    mixer = mixer.reshape(2 * lat, 2, lat // rows, rows).transpose(0, 2, 1, 3)
    return mixer.reshape(2 * lat, 2 * lat).astype(jnp.bfloat16)


def dot(left, right):
    return jnp.dot(left, right, preferred_element_type=F32)


def dot_rows(left, right):
    return lax.dot_general(left, right, (((1,), (1,)), ((), ())), preferred_element_type=F32)


def dot_cols(left, right):
    return lax.dot_general(left, right, (((0,), (0,)), ((), ())), preferred_element_type=F32)


def params(**kw):
    return pltpu.CompilerParams(vmem_limit_bytes=48 * 1024 * 1024, **kw)


def to_spectral(x, table, quarters, width):
    cells, channels = x.shape
    rows = table.shape[0] // quarters
    blocks = channels // width
    step = 2

    def body(t_ref, x_ref, o_ref):
        y = dot(t_ref[...], x_ref[...]).astype(BF16)
        for b in range(step):
            for q in range(quarters):
                o_ref[b * quarters + q] = y[q * rows : (q + 1) * rows, b * width : (b + 1) * width]

    return pl.pallas_call(
        body,
        grid=(blocks // step,),
        in_specs=[
            pl.BlockSpec(table.shape, lambda i: (0, 0)),
            pl.BlockSpec((cells, step * width), lambda i: (0, i)),
        ],
        out_specs=pl.BlockSpec((step * quarters, rows, width), lambda i: (i, 0, 0)),
        out_shape=jax.ShapeDtypeStruct((blocks * quarters, rows, width), BF16),
        compiler_params=params(),
        name="to_spectral",
    )(table, x)


def to_cells(parts, table_t, grid_add, quarters, width):
    cells, channels = grid_add.shape
    rows = parts.shape[1]
    blocks = channels // width
    step = 2

    def body(t_ref, p_ref, g_ref, o_ref):
        for b in range(step):
            part = p_ref[b * quarters : (b + 1) * quarters].reshape(quarters * rows, width)
            lanes = slice(b * width, (b + 1) * width)
            o_ref[:, lanes] = (g_ref[:, lanes].astype(F32) + dot(t_ref[...], part)).astype(BF16)

    return pl.pallas_call(
        body,
        grid=(blocks // step,),
        in_specs=[
            pl.BlockSpec(table_t.shape, lambda i: (0, 0)),
            pl.BlockSpec((step * quarters, rows, width), lambda i: (i, 0, 0)),
            pl.BlockSpec((cells, step * width), lambda i: (0, i)),
        ],
        out_specs=pl.BlockSpec((cells, step * width), lambda i: (0, i)),
        out_shape=jax.ShapeDtypeStruct((cells, channels), BF16),
        compiler_params=params(),
        name="to_cells",
    )(table_t, parts, grid_add)


def complex_square(w_ref, layer):
    real, imag = (w_ref[0, layer, 0], w_ref[0, layer, 1])
    return jnp.concatenate(
        [jnp.concatenate([real, imag], axis=1), jnp.concatenate([-imag, real], axis=1)], axis=0
    )


def spectral_chain(scalars, spec, du, mixer, w_first, w_second, bias, lat, width):
    per = spec.shape[0] * spec.shape[1] // (2 * lat)
    chunk = spec.shape
    tall = per * lat

    def body(s_ref, spec_ref, du_ref, l_ref, lt_ref, w1_ref, w2_ref, b_ref, da_ref, keep_ref, tmp):
        block, quarter = (s_ref[0], s_ref[1])
        mix, mix_t = (l_ref[...], lt_ref[...])

        def mixed(ref):
            tmp[...] = ref[...].reshape(2 * lat * per, width).astype(F32)
            parts = []
            for k in range(per):
                column = tmp[pl.ds(k, 2 * lat, stride=per), :].astype(BF16)
                z = dot(mix, column)
                parts.append(jnp.concatenate([z[:lat], z[lat:]], axis=1))
            return jnp.concatenate(parts, axis=0)

        rows = lax.broadcasted_iota(jnp.int32, (lat, lat), 0)
        cols = lax.broadcasted_iota(jnp.int32, (lat, lat), 1)
        eye = (rows == cols).astype(F32)
        back = ((rows + cols) % lat == 0).astype(F32)
        has_zero = (quarter == 0).astype(F32)
        even = (eye + 0.5 * has_zero * (back - eye)).astype(BF16)
        odd = (eye - 0.5 * has_zero * (back + eye)).astype(BF16)

        def through_grid(v):
            first = v[:lat]
            first = jnp.concatenate(
                [dot(even, first[:, :width]), dot(odd, first[:, width:])], axis=1
            )
            return jnp.concatenate([first, v[lat:].astype(F32)], axis=0)

        def mask_of(layer):
            mode = quarter * per + lax.broadcasted_iota(jnp.int32, (tall, 1), 0) // lat
            return (mode < s_ref[2 + layer * 8 + block]).astype(F32)

        def bias_of(layer, which):
            part = b_ref[0, layer, which]
            return jnp.concatenate([part[0:1], part[1:2]], axis=1)

        w_one = [complex_square(w1_ref, layer) for layer in range(LAYERS)]
        w_two = [complex_square(w2_ref, layer) for layer in range(LAYERS)]

        z = mixed(spec_ref)
        slopes = []
        for layer in range(LAYERS):
            z_low = z.astype(BF16)
            keep_ref[layer] = z_low
            pre = dot(z_low, w_one[layer]) + bias_of(layer, 0)
            sig = jax.nn.sigmoid(pre)
            hidden = (pre * sig).astype(BF16)
            keep_ref[2 + layer] = hidden
            slopes.append(sig * (1.0 + pre * (1.0 - sig)))
            if layer + 1 < LAYERS:
                out = ((dot(hidden, w_two[layer]) + bias_of(layer, 1)) * mask_of(layer)).astype(BF16)
                z = z + through_grid(out)
        grad = mixed(du_ref)
        total = None
        for layer in reversed(range(LAYERS)):
            dout = (grad * mask_of(layer)).astype(BF16)
            keep_ref[6 + layer] = dout
            dpre = (dot_rows(dout, w_two[layer]) * slopes[layer]).astype(BF16)
            keep_ref[4 + layer] = dpre
            dz = dot_rows(dpre, w_one[layer])
            if layer:
                grad = grad + through_grid(dz.astype(BF16))
            total = dz if total is None else total + dz
        total = total.astype(BF16)
        for k in range(per):
            part = total[k * lat : (k + 1) * lat]
            part = jnp.concatenate([part[:, :width], part[:, width:]], axis=0)
            tmp[pl.ds(k, 2 * lat, stride=per), :] = dot(mix_t, part)
        da_ref[...] = tmp[...].astype(BF16).reshape(chunk)

    whole = lambda shape: pl.BlockSpec(shape, lambda i, s: (0,) * len(shape))
    weight = pl.BlockSpec((1, LAYERS, 2, width, width), lambda i, s: (0, 0, 0, s[0], 0))
    return pl.pallas_call(
        body,
        grid_spec=pltpu.PrefetchScalarGridSpec(
            num_scalar_prefetch=1,
            grid=(1,),
            in_specs=[
                whole(chunk),
                whole(chunk),
                whole(mixer.shape),
                whole(mixer.shape),
                weight,
                weight,
                pl.BlockSpec((1, LAYERS, 2, 2, width), lambda i, s: (0, 0, 0, 0, s[0])),
            ],
            out_specs=[whole(chunk), whole((8, tall, 2 * width))],
            scratch_shapes=[pltpu.VMEM((2 * lat * per, width), F32)],
        ),
        out_shape=[
            jax.ShapeDtypeStruct(chunk, BF16),
            jax.ShapeDtypeStruct((8, tall, 2 * width), BF16),
        ],
        compiler_params=params(),
        name="spectral_chain",
    )(scalars, spec, du, mixer, mixer.T.copy(), w_first, w_second, bias)


def gradient_parts(scalars, kept_values, quarters, width):
    own = width // quarters
    count = 4 * LAYERS * own + 16

    def body(s_ref, v_ref, mine_ref, *rest):
        others, all_ref = (rest[:-1], rest[-1])
        index = lax.broadcasted_iota(jnp.int32, (16, width), 0)
        sums = jnp.zeros((16, width), F32)
        for which in range(2):
            for layer in range(LAYERS):
                right = v_ref[4 + 2 * which + layer]
                outer = dot_cols(v_ref[2 * which + layer], right)
                total = jnp.sum(right.astype(F32), axis=0, keepdims=True)
                squares = (
                    outer[:width, :width] + outer[width:, width:],
                    outer[:width, width:] - outer[width:, :width],
                )
                for r in range(2):
                    all_ref[(which * LAYERS + layer) * 2 + r] = squares[r]
                    slot = (layer * 2 + which) * 2 + r
                    sums = sums + jnp.where(index == slot, total[:, r * width : (r + 1) * width], 0.0)
        for step, o_ref in enumerate((mine_ref,) + others):
            start = pl.multiple_of((s_ref[1] + step) % quarters * own, own)
            for square in range(4 * LAYERS):
                part = all_ref[square, pl.ds(start, own), :]
                o_ref[square * own : (square + 1) * own] = part.astype(o_ref.dtype)
            o_ref[4 * LAYERS * own :] = sums.astype(o_ref.dtype)

    whole = lambda shape: pl.BlockSpec(shape, lambda i, s: (0,) * len(shape))
    return pl.pallas_call(
        body,
        grid_spec=pltpu.PrefetchScalarGridSpec(
            num_scalar_prefetch=1,
            grid=(1,),
            in_specs=[whole(kept_values.shape)],
            out_specs=[whole((count, width))] * quarters,
            scratch_shapes=[pltpu.VMEM((4 * LAYERS, width, width), F32)],
        ),
        out_shape=[jax.ShapeDtypeStruct((count, width), F32)]
        + [jax.ShapeDtypeStruct((count, width), BF16)] * (quarters - 1),
        compiler_params=params(),
        name="gradient_parts",
    )(scalars, kept_values)


def gradient_sum(scalars, parts, width):
    quarters = len(parts)
    own = width // quarters
    half = 2 * LAYERS * own

    def body(s_ref, *refs):
        first_ref, second_ref, bias_ref = refs[quarters:]
        total = refs[0][...]
        for ref in refs[1:quarters]:
            total = total + ref[...].astype(F32)
        first_ref[...] = total[:half]
        second_ref[...] = total[half : 2 * half]
        sums = total[2 * half : 2 * half + 8]
        mine = sums[:, :own]
        for q in range(1, quarters):
            mine = jnp.where(s_ref[1] == q, sums[:, q * own : (q + 1) * own], mine)
        bias_ref[...] = mine

    whole = lambda shape: pl.BlockSpec(shape, lambda i, s: (0,) * len(shape))
    return pl.pallas_call(
        body,
        grid_spec=pltpu.PrefetchScalarGridSpec(
            num_scalar_prefetch=1,
            grid=(1,),
            in_specs=[whole(part.shape) for part in parts],
            out_specs=[whole((half, width)), whole((half, width)), whole((8, own))],
        ),
        out_shape=[
            jax.ShapeDtypeStruct((half, width), F32),
            jax.ShapeDtypeStruct((half, width), F32),
            jax.ShapeDtypeStruct((8, own), F32),
        ],
        compiler_params=params(),
        name="gradient_sum",
    )(scalars, *parts)


def on_device(section_input, handoff, loss_grad, w_first, w_second, bias, kept):
    lat_count = lax.axis_size("lat")
    sections = lax.axis_size("section")
    _, rows, lon, channels = section_input.shape
    width = w_first.shape[-1]
    blocks = channels // width
    quarters = lat_count // blocks
    lat = rows * lat_count
    forward = lon_table(lon, rows, quarters, False)
    inverse = lon_table(lon, rows, quarters, True)
    mixer = lat_table(lat, rows)
    place = lax.axis_index("lat")
    scalars = jnp.concatenate(
        [jnp.stack([place // quarters, place % quarters]).astype(jnp.int32), kept.reshape(-1)]
    )

    received = lax.ppermute(handoff, "section", [(s, s - 1) for s in range(1, sections)])
    spec = to_spectral(section_input.reshape(rows * lon, channels), forward, quarters, width)
    spec = lax.all_to_all(spec, "lat", split_axis=0, concat_axis=0, tiled=True)
    cot = jnp.where(lax.axis_index("section") == sections - 1, loss_grad, received[0])
    cot = cot.reshape(rows * lon, channels)
    du = to_spectral(cot, inverse, quarters, width)
    du = lax.all_to_all(du, "lat", split_axis=0, concat_axis=0, tiled=True)
    da, values = spectral_chain(scalars, spec, du, mixer, w_first, w_second, bias, lat, width)
    da = lax.all_to_all(da, "lat", split_axis=0, concat_axis=0, tiled=True)
    parts = list(gradient_parts(scalars, values, quarters, width))
    for step in range(1, quarters):
        pairs = [
            (b * quarters + q, b * quarters + (q + step) % quarters)
            for b in range(blocks)
            for q in range(quarters)
        ]
        parts[step] = lax.ppermute(parts[step], "lat", pairs)
    handed = to_cells(da, forward.T.copy(), cot, quarters, width)
    first, second, biases = gradient_sum(scalars, parts, width)
    own = width // quarters
    return (
        handed.reshape(1, rows, lon, channels),
        first.reshape(1, LAYERS, 2, own, width),
        second.reshape(1, LAYERS, 2, own, width),
        biases.reshape(1, LAYERS, 2, 2, own),
    )


def solution(mesh):
    return jax.shard_map(
        on_device,
        mesh=mesh,
        in_specs=(
            P("section", "lat", None, None),
            P("section", "lat", None, None),
            P("lat", None, None),
            P("section", None, None, None, None),
            P("section", None, None, None, None),
            P("section", None, None, None, None),
            P("section", None, None),
        ),
        out_specs=(
            P("section", "lat", None, None),
            P("section", None, None, "lat", None),
            P("section", None, None, "lat", None),
            P("section", None, None, None, "lat"),
        ),
        check_vma=False,
    )
```

time: 881 us -> 78.9 us (0.09)
  waiting for transfers between devices: 709 us -> 25.7 us
  local copies, waits for them, and re-layouts: 60.9 us -> 4.42 us
  matrix products: 36.6 us -> 0 us
  between operations: 14.7 us -> 0.81 us
  other arithmetic: 13.1 us -> 0.14 us
  Pallas kernels: 0 us -> 11.1 us
  starting transfers between devices: 44.5 us -> 35.5 us
    reduce_scatter x2 -> x0, waiting for transfers between devices: 443 us -> none  [the longest x1 223 us: on_device(): lax.psum_scatter(jnp.stack(twos).astype(jnp.bfloat16), 'lat', scatter_dim...]
    unnamed x4 -> x0, waiting for transfers between devices: 207 us -> none
    dot_general x57 -> x0, matrix products: 36.6 us -> none  [the longest x16 12.8 us: prod(): jnp.einsum('rnb,rnh->nbh', first, second, preferred_element_type=jnp.floa...]
    all_to_all x7 -> x3, waiting for transfers between devices: 56.2 us -> 22.8 us  [the longest x1 12.2 us: on_device(): du = lax.all_to_all(du, 'lat', split_axis=0, concat_axis=0, tiled=True)]
    all_to_all x7 -> x3, starting transfers between devices: 41.7 us -> 21.3 us  [the longest x1 13.2 us: on_device(): spec = lax.all_to_all(spec, 'lat', split_axis=0, concat_axis=0, tiled=True)]
    unnamed x86 -> x20, local copies, waits for them, and re-layouts: 19.4 us -> 4.34 us
    reshape x8 -> x1, local copies, waits for them, and re-layouts: 14.1 us -> 0.08 us  [on_device(): kept.reshape(-1)]
    all_to_all x9 -> x0, local copies, waits for them, and re-layouts: 11.9 us -> none  [the longest x5 7.1 us: to_grid(): lax.all_to_all(mode_part, 'lat', split_axis=1, concat_axis=2, tiled=True)]
  transfers between devices with their start and end apart: 11 -> 7, of which waited for: 10 -> 3; matrix products, arithmetic and copies ran while one was open for 5% -> 0% of each run, Pallas kernels for 0% -> 8%
where the time goes in v1:
time: 78.9 us; the launch traced here: 77.6 us
  starting transfers between devices  35.5 us (45%)
  waiting for transfers between devices  25.7 us (33%)
  Pallas kernels  11.1 us (14%)
  local copies, waits for them, and re-layouts  4.42 us (6%)
  between operations  0.81 us (1%)
    all_to_all x1, starting transfers between devices, on_device(): spec = lax.all_to_all(spec, 'lat', split_axis=0, concat_axis=0, tiled=True)  13.2 us
    all_to_all x1, waiting for transfers between devices, on_device(): du = lax.all_to_all(du, 'lat', split_axis=0, concat_axis=0, tiled=True)  12.2 us
    ppermute x3, starting transfers between devices, on_device(): parts[step] = lax.ppermute(parts[step], 'lat', pairs)  11.5 us
    all_to_all x1, waiting for transfers between devices, on_device(): spec = lax.all_to_all(spec, 'lat', split_axis=0, concat_axis=0, tiled=True)  10.7 us
    unnamed x20, local copies, waits for them, and re-layouts  4.34 us
    all_to_all x1, starting transfers between devices, on_device(): du = lax.all_to_all(du, 'lat', split_axis=0, concat_axis=0, tiled=True)  4.09 us
    all_to_all x1, starting transfers between devices, on_device(): da = lax.all_to_all(da, 'lat', split_axis=0, concat_axis=0, tiled=True)  4 us
    pallas_call x2, Pallas kernels, to_spectral(): pl.pallas_call(body, grid=(blocks // step,), in_specs=[pl.BlockSpec(table...  3.7 us
  transfers between devices with their start and end apart: 7, of which 3 were waited for; matrix products, arithmetic and copies ran while one was open for 0% of the time, Pallas kernels for 8%

profile of v1, /device:TPU:56, one launch (start us, length us, event | category | flops | bytes accessed | tf_op | source)
XLA Modules:
  0.0 77.6 jit_solution(12639937894028157079)
XLA Ops:
  0.6 2.7 %collective-permute-start = (bf16[1,2,128,1024]{3,2,1,0:T(8,128)(2,1)}, bf16[1,2,128,1024]{3,2,1,0:T(8,128)(2,1)S(1)}, u32[]{:S(2)}, u32[]{:S(2)}) collective-permute-start(bf16[1,2,128,1024]{3,2,1,0:T(8,128)(2,1)} %param.13), channel_id=1, source_target_pairs={{32,0},{64,32},{96,64},{128,96},{160,128},{192,160},{224,192},{256... | collective-permute-start | bytes 1572872 | tf_op jit(solution)/shard_map/ppermute | solution.py:319
  3.3 0.0 copy-start.2
  3.3 1.0 %copy-done.2 = bf16[1,2,128,1024]{3,2,1,0:T(8,128)(2,1)S(1)} copy-done((bf16[1,2,128,1024]{3,2,1,0:T(8,128)(2,1)S(1)}, bf16[1,2,128,1024]{3,2,1,0:T(8,128)(2,1)}, u32[]{:S(2)}) %copy-start.2) | copy-done | bytes 524312
  4.4 0.8 %copy-done.4 = bf16[128,256]{1,0:T(8,128)(2,1)S(1)} copy-done((bf16[128,256]{1,0:T(8,128)(2,1)S(1)}, bf16[128,256]{1,0:T(8,128)(2,1)}, u32[]{:S(2)}) %copy-start.4) | copy-done | bytes 65560
  5.2 0.0 copy-start.8
  5.2 1.9 %to_spectral.2 = bf16[32,32,128]{2,1,0:T(8,128)(2,1)} custom-call(bf16[128,256]{1,0:T(8,128)(2,1)S(1)} %copy-done.4, bf16[256,1024]{1,0:T(8,128)(2,1)S(1)} %bitcast.12), custom_call_target="tpu_custom_call" | custom-call | tf_op jit(solution)/shard_map/to_spectral/pallas_call | solution.py:70
  7.1 13.2 %all-to-all-start = ((bf16[32,32,128]{2,1,0:T(8,128)(2,1)}), bf16[32,32,128]{2,1,0:T(8,128)(2,1)S(1)}, u32[]{:S(2)}, u32[]{:S(2)}) async-start(bf16[32,32,128]{2,1,0:T(8,128)(2,1)} %to_spectral.2), calls=%async_computation | async-start | bytes 524288 | tf_op jit(solution)/shard_map/all_to_all | solution.py:321
  20.3 0.0 collective-permute-done
  20.3 0.1 bitcast_select_fusion
  20.4 0.0 copy-done.3
  20.4 1.8 %to_spectral.3 = bf16[32,32,128]{2,1,0:T(8,128)(2,1)} custom-call(bf16[128,256]{1,0:T(8,128)(2,1)S(1)} %copy-done.3, bf16[256,1024]{1,0:T(8,128)(2,1)S(1)} %bitcast.10), custom_call_target="tpu_custom_call" | custom-call | tf_op jit(solution)/shard_map/to_spectral/pallas_call | solution.py:70
  22.2 10.7 %all-to-all-done.spec_ref = bf16[32,32,128]{2,1,0:T(8,128)(2,1)S(1)} async-done(((bf16[32,32,128]{2,1,0:T(8,128)(2,1)}), bf16[32,32,128]{2,1,0:T(8,128)(2,1)S(1)}, u32[]{:S(2)}, u32[]{:S(2)}) %all-to-all-start) | async-done | bytes 262176 | tf_op jit(solution)/shard_map/all_to_all | solution.py:321
  32.9 4.1 %all-to-all-start.1 = ((bf16[32,32,128]{2,1,0:T(8,128)(2,1)}), bf16[32,32,128]{2,1,0:T(8,128)(2,1)S(1)}, u32[]{:S(2)}, u32[]{:S(2)}) async-start(bf16[32,32,128]{2,1,0:T(8,128)(2,1)} %to_spectral.3), calls=%async_computation.1 | async-start | bytes 524288 | tf_op jit(solution)/shard_map/all_to_all | solution.py:325
  37.0 0.0 copy-done.9
  37.0 0.1 reshape.29
  37.1 0.1 pad_add_fusion.s_ref
  37.2 12.2 %all-to-all-done.1.du_ref = bf16[32,32,128]{2,1,0:T(8,128)(2,1)S(1)} async-done(((bf16[32,32,128]{2,1,0:T(8,128)(2,1)}), bf16[32,32,128]{2,1,0:T(8,128)(2,1)S(1)}, u32[]{:S(2)}, u32[]{:S(2)}) %all-to-all-start.1) | async-done | bytes 262176 | tf_op jit(solution)/shard_map/all_to_all | solution.py:325
  49.4 0.0 copy-start
  49.4 1.2 %copy-done = bf16[1,2,2,1024,128]{4,3,2,1,0:T(8,128)(2,1)S(1)} copy-done((bf16[1,2,2,1024,128]{4,3,2,1,0:T(8,128)(2,1)S(1)}, bf16[1,2,2,1024,128]{4,3,2,1,0:T(8,128)(2,1)}, u32[]{:S(2)}) %copy-start) | copy-done | bytes 1048600
  50.6 1.2 %copy-done.1 = bf16[1,2,2,1024,128]{4,3,2,1,0:T(8,128)(2,1)S(1)} copy-done((bf16[1,2,2,1024,128]{4,3,2,1,0:T(8,128)(2,1)S(1)}, bf16[1,2,2,1024,128]{4,3,2,1,0:T(8,128)(2,1)}, u32[]{:S(2)}) %copy-start.1) | copy-done | bytes 1048600
  51.8 3.0 %spectral_chain.1 = (bf16[32,32,128]{2,1,0:T(8,128)(2,1)}, bf16[8,512,256]{2,1,0:T(8,128)(2,1)S(1)}) custom-call(s32[18]{0:T(128)S(1)} %pad_add_fusion.s_ref, bf16[32,32,128]{2,1,0:T(8,128)(2,1)S(1)} %all-to-all-done.spec_ref, bf16[32,32,128]{2,1,0:T(8,128)(2,1)S(1)} %all-to-all-done.1.du_ref, bf16[128,128]{1,0:T(8,128)(2,1)S(1)} %copy-done.8, ...), custom_call_target="tpu_custom_call" | custom-call | tf_op jit(solution)/shard_map/spectral_chain/pallas_call | solution.py:195
  54.8 4.0 %all-to-all-start.2 = ((bf16[32,32,128]{2,1,0:T(8,128)(2,1)}), bf16[32,32,128]{2,1,0:T(8,128)(2,1)S(1)}, u32[]{:S(2)}, u32[]{:S(2)}) async-start(bf16[32,32,128]{2,1,0:T(8,128)(2,1)} %get-tuple-element.13), calls=%async_computation.2 | async-start | bytes 524288 | tf_op jit(solution)/shard_map/all_to_all | solution.py:327
  58.8 1.1 %gradient_parts.1 = (f32[272,128]{1,0:T(8,128)S(1)}, bf16[272,128]{1,0:T(8,128)(2,1)S(1)}, bf16[272,128]{1,0:T(8,128)(2,1)S(1)}, bf16[272,128]{1,0:T(8,128)(2,1)S(1)}) custom-call(s32[18]{0:T(128)S(1)} %pad_add_fusion.s_ref, bf16[8,512,256]{2,1,0:T(8,128)(2,1)S(1)} %get-tuple-element.14.v_ref), custom_call_target="tpu_custom_call" | custom-call | tf_op jit(solution)/shard_map/gradient_parts/pallas_call | solution.py:250
  59.9 3.6 %collective-permute-start.1 = (bf16[272,128]{1,0:T(8,128)(2,1)S(1)}, bf16[272,128]{1,0:T(8,128)(2,1)S(1)}, u32[]{:S(2)}, u32[]{:S(2)}) collective-permute-start(bf16[272,128]{1,0:T(8,128)(2,1)S(1)} %get-tuple-element.16), channel_id=1, source_target_pairs={{0,1},{1,2},{2,3},{3,0},{4,5},{5,6},{6,7},{7,4},{8,9},{9,10},{10,1... | collective-permute-start | bytes 208904 | tf_op jit(solution)/shard_map/ppermute | solution.py:335
  63.5 4.6 %collective-permute-start.2 = (bf16[272,128]{1,0:T(8,128)(2,1)S(1)}, bf16[272,128]{1,0:T(8,128)(2,1)S(1)}, u32[]{:S(2)}, u32[]{:S(2)}) collective-permute-start(bf16[272,128]{1,0:T(8,128)(2,1)S(1)} %get-tuple-element.17), channel_id=1, source_target_pairs={{0,2},{1,3},{2,0},{3,1},{4,6},{5,7},{6,4},{7,5},{8,10},{9,11},{10,... | collective-permute-start | bytes 208904 | tf_op jit(solution)/shard_map/ppermute | solution.py:335
  68.1 3.4 %collective-permute-start.3 = (bf16[272,128]{1,0:T(8,128)(2,1)S(1)}, bf16[272,128]{1,0:T(8,128)(2,1)S(1)}, u32[]{:S(2)}, u32[]{:S(2)}) collective-permute-start(bf16[272,128]{1,0:T(8,128)(2,1)S(1)} %get-tuple-element.18), channel_id=1, source_target_pairs={{0,3},{1,0},{2,1},{3,2},{4,7},{5,4},{6,5},{7,6},{8,11},{9,8},{10,9... | collective-permute-start | bytes 208904 | tf_op jit(solution)/shard_map/ppermute | solution.py:335
  71.4 0.0 collective-permute-done.1.refs_1_
  71.4 0.0 collective-permute-done.2.refs_2_
  71.4 2.8 %collective-permute-done.3.refs_3_ = bf16[272,128]{1,0:T(8,128)(2,1)S(1)} collective-permute-done((bf16[272,128]{1,0:T(8,128)(2,1)S(1)}, bf16[272,128]{1,0:T(8,128)(2,1)S(1)}, u32[]{:S(2)}, u32[]{:S(2)}) %collective-permute-start.3) | collective-permute-done | bytes 69664 | tf_op jit(solution)/shard_map/ppermute | solution.py:335
  74.3 1.4 %gradient_sum.1 = (f32[128,128]{1,0:T(8,128)}, f32[128,128]{1,0:T(8,128)}, f32[8,32]{1,0:T(8,128)}) custom-call(s32[18]{0:T(128)S(1)} %pad_add_fusion.s_ref, f32[272,128]{1,0:T(8,128)S(1)} %get-tuple-element.15.refs_0_, bf16[272,128]{1,0:T(8,128)(2,1)S(1)} %collective-permute-done.1.refs_1_, bf16[272,128]{1,0:T(8,128)(2,1)S(1)} %collective-permute-done.2.refs_2_, ...), custom_call_target="tpu_custom_call" | custom-call | tf_op jit(solution)/shard_map/gradient_sum/pallas_call | solution.py:285
  75.7 0.0 all-to-all-done.2.p_ref
  75.7 1.9 %to_cells.1 = bf16[256,1024]{1,0:T(8,128)(2,1)} custom-call(bf16[256,128]{1,0:T(8,128)(2,1)S(1)} %copy-done.5, bf16[32,32,128]{2,1,0:T(8,128)(2,1)S(1)} %all-to-all-done.2.p_ref, bf16[256,1024]{1,0:T(8,128)(2,1)S(1)} %bitcast.11), custom_call_target="tpu_custom_call" | custom-call | tf_op jit(solution)/shard_map/to_cells/pallas_call | solution.py:96
  (11 shorter events, 0.0 us)
Async XLA Ops:
  0.6 19.7 %collective-permute-start = (bf16[1,2,128,1024]{3,2,1,0:T(8,128)(2,1)}, bf16[1,2,128,1024]{3,2,1,0:T(8,128)(2,1)S(1)}, u32[]{:S(2)}, u32[]{:S(2)}) collective-permute-start(bf16[1,2,128,1024]{3,2,1,0:T(8,128)(2,1)} %param.13), channel_id=1, source_target_pairs={{32,0},{64,32},{96,64},{128,96},{160,128},{192,160},{224,192},{256... | collective-permute-start | bytes 1572872 | tf_op jit(solution)/shard_map/ppermute | solution.py:319
  3.3 1.0 %copy-start.2 = (bf16[1,2,128,1024]{3,2,1,0:T(8,128)(2,1)S(1)}, bf16[1,2,128,1024]{3,2,1,0:T(8,128)(2,1)}, u32[]{:S(2)}) copy-start(bf16[1,2,128,1024]{3,2,1,0:T(8,128)(2,1)} %param.12) | copy-start | bytes 1572868
  4.4 0.8 %copy-start.4 = (bf16[128,256]{1,0:T(8,128)(2,1)S(1)}, bf16[128,256]{1,0:T(8,128)(2,1)}, u32[]{:S(2)}) copy-start(bf16[128,256]{1,0:T(8,128)(2,1)} %constant.47.clone.t_ref) | copy-start | bytes 196612
  5.2 15.1 %copy-start.3 = (bf16[128,256]{1,0:T(8,128)(2,1)S(1)}, bf16[128,256]{1,0:T(8,128)(2,1)}, u32[]{:S(2)}) copy-start(bf16[128,256]{1,0:T(8,128)(2,1)} %constant.48.clone.t_ref) | copy-start | bytes 196612
  5.2 31.8 %copy-start.9 = (s32[1,2,8]{2,1,0:T(2,128)S(1)}, s32[1,2,8]{2,1,0:T(2,128)}, u32[]{:S(2)}) copy-start(s32[1,2,8]{2,1,0:T(2,128)} %param.18) | copy-start | bytes 196
  5.2 44.1 %copy-start.6 = (f32[1,2,2,2,1024]{4,3,2,1,0:T(2,128)S(1)}, f32[1,2,2,2,1024]{4,3,2,1,0:T(2,128)}, u32[]{:S(2)}) copy-start(f32[1,2,2,2,1024]{4,3,2,1,0:T(2,128)} %b_ref.1) | copy-start | bytes 98308
  5.2 44.1 %copy-start.7 = (bf16[128,128]{1,0:T(8,128)(2,1)S(1)}, bf16[128,128]{1,0:T(8,128)(2,1)}, u32[]{:S(2)}) copy-start(bf16[128,128]{1,0:T(8,128)(2,1)} %constant.50.clone.lt_ref) | copy-start | bytes 98308
  5.2 44.1 %copy-start.8 = (bf16[128,128]{1,0:T(8,128)(2,1)S(1)}, bf16[128,128]{1,0:T(8,128)(2,1)}, u32[]{:S(2)}) copy-start(bf16[128,128]{1,0:T(8,128)(2,1)} %constant.49.clone.l_ref) | copy-start | bytes 98308
  7.1 25.8 %all-to-all-start = ((bf16[32,32,128]{2,1,0:T(8,128)(2,1)}), bf16[32,32,128]{2,1,0:T(8,128)(2,1)S(1)}, u32[]{:S(2)}, u32[]{:S(2)}) async-start(bf16[32,32,128]{2,1,0:T(8,128)(2,1)} %to_spectral.2), calls=%async_computation | async-start | bytes 524288 | tf_op jit(solution)/shard_map/all_to_all | solution.py:321
  32.9 16.5 %all-to-all-start.1 = ((bf16[32,32,128]{2,1,0:T(8,128)(2,1)}), bf16[32,32,128]{2,1,0:T(8,128)(2,1)S(1)}, u32[]{:S(2)}, u32[]{:S(2)}) async-start(bf16[32,32,128]{2,1,0:T(8,128)(2,1)} %to_spectral.3), calls=%async_computation.1 | async-start | bytes 524288 | tf_op jit(solution)/shard_map/all_to_all | solution.py:325
  49.4 1.2 %copy-start = (bf16[1,2,2,1024,128]{4,3,2,1,0:T(8,128)(2,1)S(1)}, bf16[1,2,2,1024,128]{4,3,2,1,0:T(8,128)(2,1)}, u32[]{:S(2)}) copy-start(bf16[1,2,2,1024,128]{4,3,2,1,0:T(8,128)(2,1)} %w1_ref.1) | copy-start | bytes 3145732
  50.6 1.2 %copy-start.1 = (bf16[1,2,2,1024,128]{4,3,2,1,0:T(8,128)(2,1)S(1)}, bf16[1,2,2,1024,128]{4,3,2,1,0:T(8,128)(2,1)}, u32[]{:S(2)}) copy-start(bf16[1,2,2,1024,128]{4,3,2,1,0:T(8,128)(2,1)} %w2_ref.1) | copy-start | bytes 3145732
  54.8 20.9 %copy-start.5 = (bf16[256,128]{1,0:T(8,128)(2,1)S(1)}, bf16[256,128]{1,0:T(8,128)(2,1)}, u32[]{:S(2)}) copy-start(bf16[256,128]{1,0:T(8,128)(2,1)} %constant.51.clone.t_ref) | copy-start | bytes 196612
  54.8 20.9 %all-to-all-start.2 = ((bf16[32,32,128]{2,1,0:T(8,128)(2,1)}), bf16[32,32,128]{2,1,0:T(8,128)(2,1)S(1)}, u32[]{:S(2)}, u32[]{:S(2)}) async-start(bf16[32,32,128]{2,1,0:T(8,128)(2,1)} %get-tuple-element.13), calls=%async_computation.2 | async-start | bytes 524288 | tf_op jit(solution)/shard_map/all_to_all | solution.py:327
  59.9 11.6 %collective-permute-start.1 = (bf16[272,128]{1,0:T(8,128)(2,1)S(1)}, bf16[272,128]{1,0:T(8,128)(2,1)S(1)}, u32[]{:S(2)}, u32[]{:S(2)}) collective-permute-start(bf16[272,128]{1,0:T(8,128)(2,1)S(1)} %get-tuple-element.16), channel_id=1, source_target_pairs={{0,1},{1,2},{2,3},{3,0},{4,5},{5,6},{6,7},{7,4},{8,9},{9,10},{10,1... | collective-permute-start | bytes 208904 | tf_op jit(solution)/shard_map/ppermute | solution.py:335
  63.5 8.0 %collective-permute-start.2 = (bf16[272,128]{1,0:T(8,128)(2,1)S(1)}, bf16[272,128]{1,0:T(8,128)(2,1)S(1)}, u32[]{:S(2)}, u32[]{:S(2)}) collective-permute-start(bf16[272,128]{1,0:T(8,128)(2,1)S(1)} %get-tuple-element.17), channel_id=1, source_target_pairs={{0,2},{1,3},{2,0},{3,1},{4,6},{5,7},{6,4},{7,5},{8,10},{9,11},{10,... | collective-permute-start | bytes 208904 | tf_op jit(solution)/shard_map/ppermute | solution.py:335
  68.1 6.2 %collective-permute-start.3 = (bf16[272,128]{1,0:T(8,128)(2,1)S(1)}, bf16[272,128]{1,0:T(8,128)(2,1)S(1)}, u32[]{:S(2)}, u32[]{:S(2)}) collective-permute-start(bf16[272,128]{1,0:T(8,128)(2,1)S(1)} %get-tuple-element.18), channel_id=1, source_target_pairs={{0,3},{1,0},{2,1},{3,2},{4,7},{5,4},{6,5},{7,6},{8,11},{9,8},{10,9... | collective-permute-start | bytes 208904 | tf_op jit(solution)/shard_map/ppermute | solution.py:335

commit v2 on v1

v2 whole, which is shorter than its diff:
```python
import math

import jax
import jax.numpy as jnp
import numpy as np
from jax import lax
from jax.experimental import pallas as pl
from jax.experimental.pallas import tpu as pltpu
from jax.sharding import PartitionSpec as P

LAYERS = 2
MAXK = 32
F32 = jnp.float32
BF16 = jnp.bfloat16


def lon_table(lon, rows, quarters, weighted):
    per = MAXK // quarters
    freqs = np.arange(MAXK)
    phase = 2.0 * math.pi * ((freqs[:, None] * np.arange(lon)[None, :]) % lon) / lon
    table = np.stack([np.cos(phase), -np.sin(phase)]) / math.sqrt(lon)
    table[1, 0] = 0.0
    table = table.astype(jnp.bfloat16).astype(np.float32)
    if weighted:
        table = table * np.where(freqs == 0, 1.0, 2.0)[None, :, None]
    split = table.reshape(2, quarters, per, lon).transpose(1, 0, 2, 3)
    full = np.zeros((quarters, 2, rows, per, rows, lon), np.float32)
    for row in range(rows):
        full[:, :, row, :, row, :] = split
    return full.reshape(quarters * 2 * rows * per, rows * lon).astype(jnp.bfloat16)


def lat_table(lat, rows):
    phase = 2.0 * math.pi * ((np.arange(lat)[:, None] * np.arange(lat)[None, :]) % lat) / lat
    cosine = np.cos(phase) / math.sqrt(lat)
    sine = np.sin(phase) / math.sqrt(lat)
    mixer = np.block([[cosine, sine], [-sine, cosine]])
    mixer = mixer.reshape(2 * lat, 2, lat // rows, rows).transpose(0, 2, 1, 3)
    return mixer.reshape(2 * lat, 2 * lat).astype(jnp.bfloat16)


def dot(left, right):
    return jnp.dot(left, right, preferred_element_type=F32)


def dot_rows(left, right):
    return lax.dot_general(left, right, (((1,), (1,)), ((), ())), preferred_element_type=F32)


def dot_cols(left, right):
    return lax.dot_general(left, right, (((0,), (0,)), ((), ())), preferred_element_type=F32)


def params(**kw):
    return pltpu.CompilerParams(vmem_limit_bytes=12 * 1024 * 1024, **kw)


VMEM = pl.BlockSpec(memory_space=pltpu.VMEM)
SMEM = pl.BlockSpec(memory_space=pltpu.SMEM)
HBM = pl.BlockSpec(memory_space=pltpu.HBM)


def in_hbm(value):
    return pltpu.with_memory_space_constraint(value, pltpu.HBM)


def to_spectral(scalars, sources, table, quarters, width):
    cells, channels = sources[0].shape
    rows = table.shape[0] // quarters
    blocks = channels // width
    cuts = 4
    span = channels // cuts

    def body(s_ref, t_hbm, *refs):
        given = refs[: len(sources)]
        o_ref, t_buf, x_buf, t_sem, x_sem = refs[len(sources) :]

        def piece(source, cut):
            return pltpu.make_async_copy(
                source.at[:, pl.ds(cut * span, span)], x_buf.at[cut], x_sem.at[cut]
            )

        def begin(source):
            for cut in range(cuts):
                piece(source, cut).start()

        if len(given) == 1:
            begin(given[0])
        else:
            pl.when(s_ref[0] != 0)(lambda: begin(given[0]))
            pl.when(s_ref[0] == 0)(lambda: begin(given[1]))
        table_copy = pltpu.make_async_copy(t_hbm, t_buf, t_sem)
        table_copy.start()
        table_copy.wait()
        t = t_buf[...]
        for cut in range(cuts):
            piece(given[0], cut).wait()
            y = dot(t, x_buf[cut]).astype(BF16)
            for b in range(span // width):
                for q in range(quarters):
                    owner = (cut * (span // width) + b) * quarters + q
                    o_ref[owner] = y[q * rows : (q + 1) * rows, b * width : (b + 1) * width]

    return pl.pallas_call(
        body,
        in_specs=[SMEM, HBM] + [HBM] * len(sources),
        out_specs=VMEM,
        scratch_shapes=[
            pltpu.VMEM(table.shape, BF16),
            pltpu.VMEM((cuts, cells, span), BF16),
            pltpu.SemaphoreType.DMA(()),
            pltpu.SemaphoreType.DMA((cuts,)),
        ],
        out_shape=jax.ShapeDtypeStruct((blocks * quarters, rows, width), BF16),
        compiler_params=params(),
        name="to_spectral",
    )(scalars, in_hbm(jnp.asarray(table)), *[in_hbm(source) for source in sources])


def to_cells(parts, table_t, grid_add, quarters, width):
    cells, channels = grid_add.shape
    rows = parts.shape[1]
    cuts = 4
    span = channels // cuts
    step = span // width

    def body(t_ref, p_ref, g_ref, o_hbm, buf, sem):
        copies = []
        for cut in range(cuts):
            for b in range(step):
                block = cut * step + b
                part = p_ref[block * quarters : (block + 1) * quarters]
                part = part.reshape(quarters * rows, width)
                lanes = slice(block * width, (block + 1) * width)
                mixed = g_ref[:, lanes].astype(F32) + dot(t_ref[...], part)
                buf[cut, :, b * width : (b + 1) * width] = mixed.astype(BF16)
            copies.append(
                pltpu.make_async_copy(
                    buf.at[cut], o_hbm.at[:, pl.ds(cut * span, span)], sem.at[cut]
                )
            )
            copies[-1].start()
        for copy in copies:
            copy.wait()

    return pl.pallas_call(
        body,
        in_specs=[VMEM, VMEM, VMEM],
        out_specs=HBM,
        scratch_shapes=[
            pltpu.VMEM((cuts, cells, span), BF16),
            pltpu.SemaphoreType.DMA((cuts,)),
        ],
        out_shape=jax.ShapeDtypeStruct((cells, channels), BF16),
        compiler_params=params(),
        name="to_cells",
    )(table_t, parts, grid_add)


def block_params(scalars, w_first, w_second, bias, width):
    def body(s_ref, w1_hbm, w2_hbm, b_ref, w_ref, rows_ref, buf, sem):
        start = pl.multiple_of(s_ref[1] * width, width)
        copies = [
            pltpu.make_async_copy(w.at[0, :, :, pl.ds(start, width), :], buf.at[which], sem.at[which])
            for which, w in enumerate((w1_hbm, w2_hbm))
        ]
        for copy in copies:
            copy.start()
        for layer in range(LAYERS):
            for which in range(2):
                for r in range(2):
                    rows_ref[2 * layer + which, :, r * width : (r + 1) * width] = b_ref[
                        0, layer, which, pl.ds(r, 1), pl.ds(start, width)
                    ]
        for which in range(2):
            copies[which].wait()
            for layer in range(LAYERS):
                real, imag = (buf[which, layer, 0], buf[which, layer, 1])
                w_ref[2 * layer + which, :width, :width] = real
                w_ref[2 * layer + which, :width, width:] = imag
                w_ref[2 * layer + which, width:, :width] = -imag
                w_ref[2 * layer + which, width:, width:] = real

    return pl.pallas_call(
        body,
        in_specs=[SMEM, HBM, HBM, VMEM],
        out_specs=[VMEM, VMEM],
        scratch_shapes=[
            pltpu.VMEM((2, LAYERS, 2, width, width), BF16),
            pltpu.SemaphoreType.DMA((2,)),
        ],
        out_shape=[
            jax.ShapeDtypeStruct((2 * LAYERS, 2 * width, 2 * width), BF16),
            jax.ShapeDtypeStruct((2 * LAYERS, 1, 2 * width), F32),
        ],
        compiler_params=params(),
        name="block_params",
    )(scalars, in_hbm(w_first), in_hbm(w_second), bias)


def spectral_chain(scalars, parts, mixer, mixer_t, weights, biases, lat, width):
    sources, both, _ = parts.shape
    chunk = (sources, both // 2, width)
    per = sources * (both // 2) // (2 * lat)
    tall = per * lat

    def body(s_ref, parts_ref, l_ref, lt_ref, w_ref, b_ref, da_ref, keep_ref, tmp):
        quarter = s_ref[2]
        mix, mix_t = (l_ref[...], lt_ref[...])

        def mixed(slot):
            part = parts_ref[:, slot * (both // 2) : (slot + 1) * (both // 2), :]
            tmp[slot] = part.reshape(2 * lat * per, width).astype(F32)
            cells = []
            for k in range(per):
                column = tmp[slot, pl.ds(k, 2 * lat, stride=per), :].astype(BF16)
                z = dot(mix, column)
                cells.append(jnp.concatenate([z[:lat], z[lat:]], axis=1))
            return jnp.concatenate(cells, axis=0)

        rows = lax.broadcasted_iota(jnp.int32, (lat, lat), 0)
        cols = lax.broadcasted_iota(jnp.int32, (lat, lat), 1)
        eye = (rows == cols).astype(F32)
        back = ((rows + cols) % lat == 0).astype(F32)
        has_zero = (quarter == 0).astype(F32)
        even = (eye + 0.5 * has_zero * (back - eye)).astype(BF16)
        odd = (eye - 0.5 * has_zero * (back + eye)).astype(BF16)

        def through_grid(v):
            first = v[:lat]
            first = jnp.concatenate(
                [dot(even, first[:, :width]), dot(odd, first[:, width:])], axis=1
            )
            return jnp.concatenate([first, v[lat:].astype(F32)], axis=0)

        def mask_of(layer):
            mode = quarter * per + lax.broadcasted_iota(jnp.int32, (tall, 1), 0) // lat
            return (mode < s_ref[3 + layer]).astype(F32)

        z = mixed(0)
        slopes = []
        for layer in range(LAYERS):
            z_low = z.astype(BF16)
            keep_ref[layer] = z_low
            pre = dot(z_low, w_ref[2 * layer]) + b_ref[2 * layer]
            sig = jax.nn.sigmoid(pre)
            hidden = (pre * sig).astype(BF16)
            keep_ref[2 + layer] = hidden
            slopes.append(sig * (1.0 + pre * (1.0 - sig)))
            if layer + 1 < LAYERS:
                out = dot(hidden, w_ref[2 * layer + 1]) + b_ref[2 * layer + 1]
                z = z + through_grid((out * mask_of(layer)).astype(BF16))
        grad = mixed(1)
        total = None
        for layer in reversed(range(LAYERS)):
            dout = (grad * mask_of(layer)).astype(BF16)
            keep_ref[6 + layer] = dout
            dpre = (dot_rows(dout, w_ref[2 * layer + 1]) * slopes[layer]).astype(BF16)
            keep_ref[4 + layer] = dpre
            dz = dot_rows(dpre, w_ref[2 * layer])
            if layer:
                grad = grad + through_grid(dz.astype(BF16))
            total = dz if total is None else total + dz
        total = total.astype(BF16)
        for k in range(per):
            part = total[k * lat : (k + 1) * lat]
            part = jnp.concatenate([part[:, :width], part[:, width:]], axis=0)
            tmp[0, pl.ds(k, 2 * lat, stride=per), :] = dot(mix_t, part)
        da_ref[...] = tmp[0].astype(BF16).reshape(chunk)

    return pl.pallas_call(
        body,
        in_specs=[SMEM] + [VMEM] * 5,
        out_specs=[VMEM, VMEM],
        scratch_shapes=[pltpu.VMEM((2, 2 * lat * per, width), F32)],
        out_shape=[
            jax.ShapeDtypeStruct(chunk, BF16),
            jax.ShapeDtypeStruct((8, tall, 2 * width), BF16),
        ],
        compiler_params=params(),
        name="spectral_chain",
    )(scalars, parts, mixer, mixer_t, weights, biases)


def gradient_parts(scalars, kept_values, quarters, width):
    own = width // quarters
    count = 4 * LAYERS * own + 16

    def body(s_ref, v_ref, mine_ref, *rest):
        others, all_ref = (rest[:-1], rest[-1])
        index = lax.broadcasted_iota(jnp.int32, (16, width), 0)
        sums = jnp.zeros((16, width), F32)
        for which in range(2):
            for layer in range(LAYERS):
                right = v_ref[4 + 2 * which + layer]
                outer = dot_cols(v_ref[2 * which + layer], right)
                total = jnp.sum(right.astype(F32), axis=0, keepdims=True)
                squares = (
                    outer[:width, :width] + outer[width:, width:],
                    outer[:width, width:] - outer[width:, :width],
                )
                for r in range(2):
                    all_ref[(which * LAYERS + layer) * 2 + r] = squares[r]
                    slot = (layer * 2 + which) * 2 + r
                    sums = sums + jnp.where(index == slot, total[:, r * width : (r + 1) * width], 0.0)
        for step, o_ref in enumerate((mine_ref,) + others):
            start = pl.multiple_of((s_ref[2] + step) % quarters * own, own)
            for square in range(4 * LAYERS):
                part = all_ref[square, pl.ds(start, own), :]
                o_ref[square * own : (square + 1) * own] = part.astype(o_ref.dtype)
            o_ref[4 * LAYERS * own :] = sums.astype(o_ref.dtype)

    return pl.pallas_call(
        body,
        in_specs=[SMEM, VMEM],
        out_specs=[VMEM] * quarters,
        scratch_shapes=[pltpu.VMEM((4 * LAYERS, width, width), F32)],
        out_shape=[jax.ShapeDtypeStruct((count, width), F32)]
        + [jax.ShapeDtypeStruct((count, width), BF16)] * (quarters - 1),
        compiler_params=params(),
        name="gradient_parts",
    )(scalars, kept_values)


def gradient_sum(scalars, parts, width):
    quarters = len(parts)
    own = width // quarters
    half = 2 * LAYERS * own

    def body(s_ref, *refs):
        first_ref, second_ref, bias_ref = refs[quarters:]
        total = refs[0][...]
        for ref in refs[1:quarters]:
            total = total + ref[...].astype(F32)
        first_ref[...] = total[:half]
        second_ref[...] = total[half : 2 * half]
        sums = total[2 * half : 2 * half + 8]
        mine = sums[:, :own]
        for q in range(1, quarters):
            mine = jnp.where(s_ref[2] == q, sums[:, q * own : (q + 1) * own], mine)
        bias_ref[...] = mine

    return pl.pallas_call(
        body,
        in_specs=[SMEM] + [VMEM] * quarters,
        out_specs=[VMEM, VMEM, VMEM],
        out_shape=[
            jax.ShapeDtypeStruct((half, width), F32),
            jax.ShapeDtypeStruct((half, width), F32),
            jax.ShapeDtypeStruct((8, own), F32),
        ],
        compiler_params=params(),
        name="gradient_sum",
    )(scalars, *parts)


def on_device(section_input, handoff, loss_grad, w_first, w_second, bias, kept):
    lat_count = lax.axis_size("lat")
    sections = lax.axis_size("section")
    _, rows, lon, channels = section_input.shape
    width = w_first.shape[-1]
    blocks = channels // width
    quarters = lat_count // blocks
    lat = rows * lat_count
    forward = lon_table(lon, rows, quarters, False)
    inverse = lon_table(lon, rows, quarters, True)
    mixer = lat_table(lat, rows)
    place = lax.axis_index("lat")
    section = lax.axis_index("section")
    block = place // quarters
    limits = lax.dynamic_slice(kept, (0, 0, block), (1, LAYERS, 1)).reshape(-1)
    scalars = jnp.concatenate([jnp.stack([section, block, place % quarters]), limits])
    ring = [(s, (s - 1) % sections) for s in range(sections)]
    cells = (rows * lon, channels)

    handed_du = (handoff.reshape(cells), loss_grad.reshape(cells))
    du = to_spectral(section.reshape(1), handed_du, inverse, quarters, width)
    du = lax.ppermute(du, "section", ring)
    spec = to_spectral(section.reshape(1), (section_input.reshape(cells),), forward, quarters, width)
    both = jnp.concatenate([spec, du], axis=1)
    later, both = lax.optimization_barrier((handoff, both))
    both = lax.all_to_all(both, "lat", split_axis=0, concat_axis=0, tiled=True)
    received = lax.ppermute(later, "section", ring)
    cot = jnp.where(section == sections - 1, loss_grad, received[0]).reshape(cells)
    weights, biases = block_params(scalars, w_first, w_second, bias, width)
    da, values = spectral_chain(
        scalars, both, mixer, mixer.T.copy(), weights, biases, lat, width
    )
    da = lax.all_to_all(da, "lat", split_axis=0, concat_axis=0, tiled=True)
    parts = list(gradient_parts(scalars, values, quarters, width))
    for step in range(1, quarters):
        pairs = [
            (b * quarters + q, b * quarters + (q + step) % quarters)
            for b in range(blocks)
            for q in range(quarters)
        ]
        parts[step] = lax.ppermute(parts[step], "lat", pairs)
    handed = to_cells(da, forward.T.copy(), cot, quarters, width)
    handed, parts[0] = lax.optimization_barrier((handed, parts[0]))
    first, second, biases = gradient_sum(scalars, parts, width)
    own = width // quarters
    return (
        handed.reshape(1, rows, lon, channels),
        first.reshape(1, LAYERS, 2, own, width),
        second.reshape(1, LAYERS, 2, own, width),
        biases.reshape(1, LAYERS, 2, 2, own),
    )


def solution(mesh):
    return jax.shard_map(
        on_device,
        mesh=mesh,
        in_specs=(
            P("section", "lat", None, None),
            P("section", "lat", None, None),
            P("lat", None, None),
            P("section", None, None, None, None),
            P("section", None, None, None, None),
            P("section", None, None, None, None),
            P("section", None, None),
        ),
        out_specs=(
            P("section", "lat", None, None),
            P("section", None, None, "lat", None),
            P("section", None, None, "lat", None),
            P("section", None, None, None, "lat"),
        ),
        check_vma=False,
    )
```

time: 78.9 us -> 65.4 us (0.83)
  waiting for transfers between devices: 25.7 us -> 17 us
  local copies, waits for them, and re-layouts: 4.42 us -> 0.21 us
  starting transfers between devices: 35.5 us -> 32.4 us
  other arithmetic: 0.14 us -> 2.05 us
    all_to_all x2 -> x1, waiting for transfers between devices: 22.8 us -> 14.4 us  [on_device(): both = lax.all_to_all(both, 'lat', split_axis=0, concat_axis=0, tiled=True)]
    unnamed x20 -> x10, local copies, waits for them, and re-layouts: 4.34 us -> 0.03 us
    all_to_all x2 -> x1, starting transfers between devices: 17.3 us -> 13.2 us  [on_device(): both = lax.all_to_all(both, 'lat', split_axis=0, concat_axis=0, tiled=True)]
    ppermute x3, waiting for transfers between devices: 2.82 us -> 0.62 us  [on_device(): parts[step] = lax.ppermute(parts[step], 'lat', pairs)]
    ppermute x1 -> x2, waiting for transfers between devices: 0.01 us -> 1.98 us  [the longest x1 1.98 us: on_device(): du = lax.ppermute(du, 'section', ring)]
    all_to_all x1, starting transfers between devices: 4 us -> 5.18 us  [on_device(): da = lax.all_to_all(da, 'lat', split_axis=0, concat_axis=0, tiled=True)]
    select_n x1, other arithmetic: 0.07 us -> 1.11 us  [on_device(): jnp.where(section == sections - 1, loss_grad, received[0]).reshape(cells)]
    concatenate x1 -> x2, other arithmetic: 0.08 us -> 0.94 us  [the longest x1 0.86 us: on_device(): both = jnp.concatenate([spec, du], axis=1)]
  transfers between devices with their start and end apart: 7 -> 7, of which waited for: 3 -> 4; matrix products, arithmetic and copies ran while one was open for 0% -> 2% of each run, Pallas kernels for 8% -> 13%
where the time goes in v2:
time: 65.4 us; the launch traced here: 64.3 us
  starting transfers between devices  32.4 us (50%)
  waiting for transfers between devices  17 us (26%)
  Pallas kernels  11.8 us (18%)
  other arithmetic  2.05 us (3%)
  between operations  0.79 us (1%)
    all_to_all x1, waiting for transfers between devices, on_device(): both = lax.all_to_all(both, 'lat', split_axis=0, concat_axis=0, tiled=True)  14.4 us
    all_to_all x1, starting transfers between devices, on_device(): both = lax.all_to_all(both, 'lat', split_axis=0, concat_axis=0, tiled=True)  13.2 us
    ppermute x3, starting transfers between devices, on_device(): parts[step] = lax.ppermute(parts[step], 'lat', pairs)  11.7 us
    all_to_all x1, starting transfers between devices, on_device(): da = lax.all_to_all(da, 'lat', split_axis=0, concat_axis=0, tiled=True)  5.18 us
    pallas_call x2, Pallas kernels, to_spectral(): pl.pallas_call(body, in_specs=[SMEM, HBM] + [HBM] * len(sources), out_spe...  3.76 us
    pallas_call x1, Pallas kernels, spectral_chain(): pl.pallas_call(body, in_specs=[SMEM] + [VMEM] * 5, out_specs=[VMEM, VMEM]...  2.97 us
    ppermute x1, waiting for transfers between devices, on_device(): du = lax.ppermute(du, 'section', ring)  1.98 us
    ppermute x1, starting transfers between devices, on_device(): received = lax.ppermute(later, 'section', ring)  1.64 us
  transfers between devices with their start and end apart: 7, of which 4 were waited for; matrix products, arithmetic and copies ran while one was open for 2% of the time, Pallas kernels for 13%

profile of v2, /device:TPU:56, one launch (start us, length us, event | category | flops | bytes accessed | tf_op | source)
XLA Modules:
  0.0 64.3 jit_solution(5162102881012718604)
XLA Ops:
  0.6 0.0 copy-start
  0.7 0.0 copy-start.2
  0.7 1.9 %to_spectral.3 = bf16[32,32,128]{2,1,0:T(8,128)(2,1)S(1)} custom-call(s32[1]{0:T(128)} %bitcast.s_ref, bf16[128,256]{1,0:T(8,128)(2,1)} %constant.50.clone.t_hbm, bf16[256,1024]{1,0:T(8,128)(2,1)} %bitcast.4.refs_0_, bf16[256,1024]{1,0:T(8,128)(2,1)} %bitcast.14), custom_call_target="tpu_custom_call" | custom-call | tf_op jit(solution)/shard_map/to_spectral/pallas_call | solution.py:104
  2.6 0.8 %collective-permute-start = (bf16[32,32,128]{2,1,0:T(8,128)(2,1)S(1)}, bf16[32,32,128]{2,1,0:T(8,128)(2,1)S(1)}, u32[]{:S(2)}, u32[]{:S(2)}) collective-permute-start(bf16[32,32,128]{2,1,0:T(8,128)(2,1)S(1)} %to_spectral.3), channel_id=1, source_target_pairs={{0,480},{32,0},{64,32},{96,64},{128,96},{160,128},{192,160},{224,1... | collective-permute-start | bytes 786440 | tf_op jit(solution)/shard_map/ppermute | solution.py:378
  3.4 1.9 %to_spectral.2 = bf16[32,32,128]{2,1,0:T(8,128)(2,1)S(1)} custom-call(s32[1]{0:T(128)} %bitcast.s_ref, bf16[128,256]{1,0:T(8,128)(2,1)} %constant.51.clone.t_hbm, bf16[256,1024]{1,0:T(8,128)(2,1)} %bitcast.15), custom_call_target="tpu_custom_call" | custom-call | tf_op jit(solution)/shard_map/to_spectral/pallas_call | solution.py:104
  5.2 0.0 copy-start.3
  5.3 0.0 copy-start.4
  5.3 2.0 %collective-permute-done = bf16[32,32,128]{2,1,0:T(8,128)(2,1)S(1)} collective-permute-done((bf16[32,32,128]{2,1,0:T(8,128)(2,1)S(1)}, bf16[32,32,128]{2,1,0:T(8,128)(2,1)S(1)}, u32[]{:S(2)}, u32[]{:S(2)}) %collective-permute-start) | collective-permute-done | bytes 262176 | tf_op jit(solution)/shard_map/ppermute | solution.py:378
  7.2 0.9 %pad_maximum_fusion = bf16[32,64,128]{2,1,0:T(8,128)(2,1)} fusion(bf16[32,32,128]{2,1,0:T(8,128)(2,1)S(1)} %collective-permute-done, bf16[32,32,128]{2,1,0:T(8,128)(2,1)S(1)} %to_spectral.2), kind=kLoop, calls=%fused_computation | loop fusion | flops 1048576 | bytes 1048576 | tf_op jit(solution)/shard_map/concatenate | solution.py:380
  8.1 13.2 %all-to-all-start = ((bf16[32,64,128]{2,1,0:T(8,128)(2,1)}), bf16[32,64,128]{2,1,0:T(8,128)(2,1)S(1)}, u32[]{:S(2)}, u32[]{:S(2)}) async-start(bf16[32,64,128]{2,1,0:T(8,128)(2,1)} %pad_maximum_fusion), calls=%async_computation | async-start | bytes 1048576 | tf_op jit(solution)/shard_map/all_to_all | solution.py:382
  21.3 1.6 %collective-permute-start.1 = (bf16[1,2,128,1024]{3,2,1,0:T(8,128)(2,1)}, bf16[1,2,128,1024]{3,2,1,0:T(8,128)(2,1)}, u32[]{:S(2)}, u32[]{:S(2)}) collective-permute-start(bf16[1,2,128,1024]{3,2,1,0:T(8,128)(2,1)} %param.13), channel_id=1, source_target_pairs={{0,480},{32,0},{64,32},{96,64},{128,96},{160,128},{192,160},{224,1... | collective-permute-start | bytes 1572872 | tf_op jit(solution)/shard_map/ppermute | solution.py:383
  22.9 0.0 copy-done
  22.9 0.2 dynamic-slice_reduce_fusion
  23.1 0.1 pad_add_fusion.s_ref
  23.2 0.0 copy-done.2
  23.2 1.6 %block_params.1 = (bf16[4,256,256]{2,1,0:T(8,128)(2,1)S(1)}, f32[4,1,256]{2,1,0:T(1,128)S(1)}) custom-call(s32[5]{0:T(128)S(1)} %pad_add_fusion.s_ref, bf16[1,2,2,1024,128]{4,3,2,1,0:T(8,128)(2,1)} %w1_hbm.1, bf16[1,2,2,1024,128]{4,3,2,1,0:T(8,128)(2,1)} %w2_hbm.1, f32[1,2,2,2,1024]{4,3,2,1,0:T(2,128)S(1)} %copy-done.2), custom_call_target="tpu_custom_call" | custom-call | tf_op jit(solution)/shard_map/block_params/pallas_call | solution.py:184
  24.8 14.4 %all-to-all-done.parts_ref = bf16[32,64,128]{2,1,0:T(8,128)(2,1)S(1)} async-done(((bf16[32,64,128]{2,1,0:T(8,128)(2,1)}), bf16[32,64,128]{2,1,0:T(8,128)(2,1)S(1)}, u32[]{:S(2)}, u32[]{:S(2)}) %all-to-all-start) | async-done | bytes 524320 | tf_op jit(solution)/shard_map/all_to_all | solution.py:382
  39.1 0.0 copy-done.3
  39.1 3.0 %spectral_chain.1 = (bf16[32,32,128]{2,1,0:T(8,128)(2,1)}, bf16[8,512,256]{2,1,0:T(8,128)(2,1)S(1)}) custom-call(s32[5]{0:T(128)S(1)} %pad_add_fusion.s_ref, bf16[32,64,128]{2,1,0:T(8,128)(2,1)S(1)} %all-to-all-done.parts_ref, bf16[128,128]{1,0:T(8,128)(2,1)S(1)} %copy-done.3, bf16[128,128]{1,0:T(8,128)(2,1)S(1)} %copy-done.4, ...), custom_call_target="tpu_custom_call" | custom-call | tf_op jit(solution)/shard_map/spectral_chain/pallas_call | solution.py:271
  42.1 5.2 %all-to-all-start.1 = ((bf16[32,32,128]{2,1,0:T(8,128)(2,1)}), bf16[32,32,128]{2,1,0:T(8,128)(2,1)S(1)}, u32[]{:S(2)}, u32[]{:S(2)}) async-start(bf16[32,32,128]{2,1,0:T(8,128)(2,1)} %get-tuple-element.22), calls=%async_computation.1 | async-start | bytes 524288 | tf_op jit(solution)/shard_map/all_to_all | solution.py:389
  47.3 1.1 %gradient_parts.1 = (f32[272,128]{1,0:T(8,128)S(1)}, bf16[272,128]{1,0:T(8,128)(2,1)S(1)}, bf16[272,128]{1,0:T(8,128)(2,1)S(1)}, bf16[272,128]{1,0:T(8,128)(2,1)S(1)}) custom-call(s32[5]{0:T(128)S(1)} %pad_add_fusion.s_ref, bf16[8,512,256]{2,1,0:T(8,128)(2,1)S(1)} %get-tuple-element.24.v_ref), custom_call_target="tpu_custom_call" | custom-call | tf_op jit(solution)/shard_map/gradient_parts/pallas_call | solution.py:313
  48.4 3.7 %collective-permute-start.2 = (bf16[272,128]{1,0:T(8,128)(2,1)S(1)}, bf16[272,128]{1,0:T(8,128)(2,1)S(1)}, u32[]{:S(2)}, u32[]{:S(2)}) collective-permute-start(bf16[272,128]{1,0:T(8,128)(2,1)S(1)} %get-tuple-element.28), channel_id=1, source_target_pairs={{0,1},{1,2},{2,3},{3,0},{4,5},{5,6},{6,7},{7,4},{8,9},{9,10},{10,1... | collective-permute-start | bytes 208904 | tf_op jit(solution)/shard_map/ppermute | solution.py:397
  52.1 4.6 %collective-permute-start.3 = (bf16[272,128]{1,0:T(8,128)(2,1)S(1)}, bf16[272,128]{1,0:T(8,128)(2,1)S(1)}, u32[]{:S(2)}, u32[]{:S(2)}) collective-permute-start(bf16[272,128]{1,0:T(8,128)(2,1)S(1)} %get-tuple-element.29), channel_id=1, source_target_pairs={{0,2},{1,3},{2,0},{3,1},{4,6},{5,7},{6,4},{7,5},{8,10},{9,11},{10,... | collective-permute-start | bytes 208904 | tf_op jit(solution)/shard_map/ppermute | solution.py:397
  56.7 3.4 %collective-permute-start.4 = (bf16[272,128]{1,0:T(8,128)(2,1)S(1)}, bf16[272,128]{1,0:T(8,128)(2,1)S(1)}, u32[]{:S(2)}, u32[]{:S(2)}) collective-permute-start(bf16[272,128]{1,0:T(8,128)(2,1)S(1)} %get-tuple-element.30), channel_id=1, source_target_pairs={{0,3},{1,0},{2,1},{3,2},{4,7},{5,4},{6,5},{7,6},{8,11},{9,8},{10,9... | collective-permute-start | bytes 208904 | tf_op jit(solution)/shard_map/ppermute | solution.py:397
  60.0 0.0 collective-permute-done.1
  60.1 1.1 %bitcast_select_fusion = bf16[2,128,1024]{2,1,0:T(8,128)(2,1)S(1)} fusion(bf16[2,128,1024]{2,1,0:T(8,128)(2,1)} %param.14, bf16[1,2,128,1024]{3,2,1,0:T(8,128)(2,1)} %collective-permute-done.1, pred[]{:T(512)S(6)} %eq.5), kind=kLoop, calls=%fused_computation.1 | loop fusion | flops 262144 | bytes 1572865 | tf_op jit(solution)/shard_map/jit(_where)/select_n | solution.py:384
  61.2 0.1 all-to-all-done.1.p_ref
  61.2 1.0 %to_cells.1 = bf16[256,1024]{1,0:T(8,128)(2,1)} custom-call(bf16[256,128]{1,0:T(8,128)(2,1)S(1)} %copy-done.1, bf16[32,32,128]{2,1,0:T(8,128)(2,1)S(1)} %all-to-all-done.1.p_ref, bf16[256,1024]{1,0:T(8,128)(2,1)S(1)} %bitcast.13), custom_call_target="tpu_custom_call" | custom-call | tf_op jit(solution)/shard_map/to_cells/pallas_call | solution.py:146
  62.2 0.0 collective-permute-done.2.refs_1_
  62.2 0.0 collective-permute-done.3.refs_2_
  62.3 0.6 collective-permute-done.4.refs_3_
  62.9 1.4 %gradient_sum.1 = (f32[128,128]{1,0:T(8,128)}, f32[128,128]{1,0:T(8,128)}, f32[8,32]{1,0:T(8,128)}) custom-call(s32[5]{0:T(128)S(1)} %pad_add_fusion.s_ref, f32[272,128]{1,0:T(8,128)S(1)} %get-tuple-element.27.refs_0_, bf16[272,128]{1,0:T(8,128)(2,1)S(1)} %collective-permute-done.2.refs_1_, bf16[272,128]{1,0:T(8,128)(2,1)S(1)} %collective-permute-done.3.refs_2_, ...), custom_call_target="tpu_custom_call" | custom-call | tf_op jit(solution)/shard_map/gradient_sum/pallas_call | solution.py:343
  (3 shorter events, 0.0 us)
Async XLA Ops:
  0.6 22.3 %copy-start = (s32[1,2,8]{2,1,0:T(2,128)S(1)}, s32[1,2,8]{2,1,0:T(2,128)}, u32[]{:S(2)}) copy-start(s32[1,2,8]{2,1,0:T(2,128)} %param.18) | copy-start | bytes 196
  0.7 22.5 %copy-start.2 = (f32[1,2,2,2,1024]{4,3,2,1,0:T(2,128)S(1)}, f32[1,2,2,2,1024]{4,3,2,1,0:T(2,128)}, u32[]{:S(2)}) copy-start(f32[1,2,2,2,1024]{4,3,2,1,0:T(2,128)} %b_ref.1) | copy-start | bytes 98308
  2.6 4.7 %collective-permute-start = (bf16[32,32,128]{2,1,0:T(8,128)(2,1)S(1)}, bf16[32,32,128]{2,1,0:T(8,128)(2,1)S(1)}, u32[]{:S(2)}, u32[]{:S(2)}) collective-permute-start(bf16[32,32,128]{2,1,0:T(8,128)(2,1)S(1)} %to_spectral.3), channel_id=1, source_target_pairs={{0,480},{32,0},{64,32},{96,64},{128,96},{160,128},{192,160},{224,1... | collective-permute-start | bytes 786440 | tf_op jit(solution)/shard_map/ppermute | solution.py:378
  5.2 33.9 %copy-start.3 = (bf16[128,128]{1,0:T(8,128)(2,1)S(1)}, bf16[128,128]{1,0:T(8,128)(2,1)}, u32[]{:S(2)}) copy-start(bf16[128,128]{1,0:T(8,128)(2,1)} %constant.52.clone.l_ref) | copy-start | bytes 98308
  5.3 33.9 %copy-start.4 = (bf16[128,128]{1,0:T(8,128)(2,1)S(1)}, bf16[128,128]{1,0:T(8,128)(2,1)}, u32[]{:S(2)}) copy-start(bf16[128,128]{1,0:T(8,128)(2,1)} %constant.53.clone.lt_ref) | copy-start | bytes 98308
  8.1 31.0 %all-to-all-start = ((bf16[32,64,128]{2,1,0:T(8,128)(2,1)}), bf16[32,64,128]{2,1,0:T(8,128)(2,1)S(1)}, u32[]{:S(2)}, u32[]{:S(2)}) async-start(bf16[32,64,128]{2,1,0:T(8,128)(2,1)} %pad_maximum_fusion), calls=%async_computation | async-start | bytes 1048576 | tf_op jit(solution)/shard_map/all_to_all | solution.py:382
  21.3 38.8 %collective-permute-start.1 = (bf16[1,2,128,1024]{3,2,1,0:T(8,128)(2,1)}, bf16[1,2,128,1024]{3,2,1,0:T(8,128)(2,1)}, u32[]{:S(2)}, u32[]{:S(2)}) collective-permute-start(bf16[1,2,128,1024]{3,2,1,0:T(8,128)(2,1)} %param.13), channel_id=1, source_target_pairs={{0,480},{32,0},{64,32},{96,64},{128,96},{160,128},{192,160},{224,1... | collective-permute-start | bytes 1572872 | tf_op jit(solution)/shard_map/ppermute | solution.py:383
  42.1 19.1 %copy-start.1 = (bf16[256,128]{1,0:T(8,128)(2,1)S(1)}, bf16[256,128]{1,0:T(8,128)(2,1)}, u32[]{:S(2)}) copy-start(bf16[256,128]{1,0:T(8,128)(2,1)} %constant.54.clone.t_ref) | copy-start | bytes 196612
  42.1 19.1 %all-to-all-start.1 = ((bf16[32,32,128]{2,1,0:T(8,128)(2,1)}), bf16[32,32,128]{2,1,0:T(8,128)(2,1)S(1)}, u32[]{:S(2)}, u32[]{:S(2)}) async-start(bf16[32,32,128]{2,1,0:T(8,128)(2,1)} %get-tuple-element.22), calls=%async_computation.1 | async-start | bytes 524288 | tf_op jit(solution)/shard_map/all_to_all | solution.py:389
  48.4 13.9 %collective-permute-start.2 = (bf16[272,128]{1,0:T(8,128)(2,1)S(1)}, bf16[272,128]{1,0:T(8,128)(2,1)S(1)}, u32[]{:S(2)}, u32[]{:S(2)}) collective-permute-start(bf16[272,128]{1,0:T(8,128)(2,1)S(1)} %get-tuple-element.28), channel_id=1, source_target_pairs={{0,1},{1,2},{2,3},{3,0},{4,5},{5,6},{6,7},{7,4},{8,9},{9,10},{10,1... | collective-permute-start | bytes 208904 | tf_op jit(solution)/shard_map/ppermute | solution.py:397
  52.1 10.2 %collective-permute-start.3 = (bf16[272,128]{1,0:T(8,128)(2,1)S(1)}, bf16[272,128]{1,0:T(8,128)(2,1)S(1)}, u32[]{:S(2)}, u32[]{:S(2)}) collective-permute-start(bf16[272,128]{1,0:T(8,128)(2,1)S(1)} %get-tuple-element.29), channel_id=1, source_target_pairs={{0,2},{1,3},{2,0},{3,1},{4,6},{5,7},{6,4},{7,5},{8,10},{9,11},{10,... | collective-permute-start | bytes 208904 | tf_op jit(solution)/shard_map/ppermute | solution.py:397
  56.7 6.2 %collective-permute-start.4 = (bf16[272,128]{1,0:T(8,128)(2,1)S(1)}, bf16[272,128]{1,0:T(8,128)(2,1)S(1)}, u32[]{:S(2)}, u32[]{:S(2)}) collective-permute-start(bf16[272,128]{1,0:T(8,128)(2,1)S(1)} %get-tuple-element.30), channel_id=1, source_target_pairs={{0,3},{1,0},{2,1},{3,2},{4,7},{5,4},{6,5},{7,6},{8,11},{9,8},{10,9... | collective-permute-start | bytes 208904 | tf_op jit(solution)/shard_map/ppermute | solution.py:397

commit v3 on v2

--- a/solution.py
+++ b/solution.py
@@ -68,37 +68,38 @@
     cells, channels = sources[0].shape
     rows = table.shape[0] // quarters
     blocks = channels // width
-    cuts = 4
-    span = channels // cuts
+    cuts = 2
+    span = cells // cuts
 
     def body(s_ref, t_hbm, *refs):
         given = refs[: len(sources)]
         o_ref, t_buf, x_buf, t_sem, x_sem = refs[len(sources) :]
 
         def piece(source, cut):
-            return pltpu.make_async_copy(
-                source.at[:, pl.ds(cut * span, span)], x_buf.at[cut], x_sem.at[cut]
-            )
+            part = pl.ds(cut * span, span)
+            return pltpu.make_async_copy(source.at[part, :], x_buf.at[part, :], x_sem.at[cut])
 
         def begin(source):
             for cut in range(cuts):
                 piece(source, cut).start()
 
+        table_copy = pltpu.make_async_copy(t_hbm, t_buf, t_sem)
+        table_copy.start()
         if len(given) == 1:
             begin(given[0])
         else:
             pl.when(s_ref[0] != 0)(lambda: begin(given[0]))
             pl.when(s_ref[0] == 0)(lambda: begin(given[1]))
-        table_copy = pltpu.make_async_copy(t_hbm, t_buf, t_sem)
-        table_copy.start()
         table_copy.wait()
         t = t_buf[...]
         for cut in range(cuts):
             piece(given[0], cut).wait()
-            y = dot(t, x_buf[cut]).astype(BF16)
-            for b in range(span // width):
+        step = 2 * width
+        for cut in range(channels // step):
+            y = dot(t, x_buf[:, cut * step : (cut + 1) * step]).astype(BF16)
+            for b in range(2):
                 for q in range(quarters):
-                    owner = (cut * (span // width) + b) * quarters + q
+                    owner = (cut * 2 + b) * quarters + q
                     o_ref[owner] = y[q * rows : (q + 1) * rows, b * width : (b + 1) * width]
 
     return pl.pallas_call(
@@ -107,7 +108,7 @@
         out_specs=VMEM,
         scratch_shapes=[
             pltpu.VMEM(table.shape, BF16),
-            pltpu.VMEM((cuts, cells, span), BF16),
+            pltpu.VMEM((cells, channels), BF16),
             pltpu.SemaphoreType.DMA(()),
             pltpu.SemaphoreType.DMA((cuts,)),
         ],
@@ -120,25 +121,22 @@
 def to_cells(parts, table_t, grid_add, quarters, width):
     cells, channels = grid_add.shape
     rows = parts.shape[1]
-    cuts = 4
-    span = channels // cuts
-    step = span // width
+    blocks = channels // width
+    cuts = 2
+    span = cells // cuts
 
     def body(t_ref, p_ref, g_ref, o_hbm, buf, sem):
         copies = []
         for cut in range(cuts):
-            for b in range(step):
-                block = cut * step + b
+            own = slice(cut * span, (cut + 1) * span)
+            table = t_ref[own]
+            for block in range(blocks):
                 part = p_ref[block * quarters : (block + 1) * quarters]
                 part = part.reshape(quarters * rows, width)
                 lanes = slice(block * width, (block + 1) * width)
-                mixed = g_ref[:, lanes].astype(F32) + dot(t_ref[...], part)
-                buf[cut, :, b * width : (b + 1) * width] = mixed.astype(BF16)
-            copies.append(
-                pltpu.make_async_copy(
-                    buf.at[cut], o_hbm.at[:, pl.ds(cut * span, span)], sem.at[cut]
-                )
-            )
+                mixed = g_ref[own, lanes].astype(F32) + dot(table, part)
+                buf[own, lanes] = mixed.astype(BF16)
+            copies.append(pltpu.make_async_copy(buf.at[own], o_hbm.at[own], sem.at[cut]))
             copies[-1].start()
         for copy in copies:
             copy.wait()
@@ -148,7 +146,7 @@
         in_specs=[VMEM, VMEM, VMEM],
         out_specs=HBM,
         scratch_shapes=[
-            pltpu.VMEM((cuts, cells, span), BF16),
+            pltpu.VMEM((cells, channels), BF16),
             pltpu.SemaphoreType.DMA((cuts,)),
         ],
         out_shape=jax.ShapeDtypeStruct((cells, channels), BF16),
@@ -198,13 +196,16 @@
     )(scalars, in_hbm(w_first), in_hbm(w_second), bias)
 
 
-def spectral_chain(scalars, parts, mixer, mixer_t, weights, biases, lat, width):
+def spectral_chain(scalars, parts, mixer, mixer_t, weights, biases, lat, width, quarters):
     sources, both, _ = parts.shape
     chunk = (sources, both // 2, width)
     per = sources * (both // 2) // (2 * lat)
     tall = per * lat
 
-    def body(s_ref, parts_ref, l_ref, lt_ref, w_ref, b_ref, da_ref, keep_ref, tmp):
+    own = width // quarters
+    count = 4 * LAYERS * own + 16
+
+    def body(s_ref, parts_ref, l_ref, lt_ref, w_ref, b_ref, da_ref, mine_ref, send_ref, tmp, all_ref):
         quarter = s_ref[2]
         mix, mix_t = (l_ref[...], lt_ref[...])
 
@@ -239,13 +240,30 @@
 
         z = mixed(0)
         slopes = []
+        lefts = {}
+        index = lax.broadcasted_iota(jnp.int32, (16, width), 0)
+        sums = jnp.zeros((16, width), F32)
+
+        def products(which, layer, right, sums):
+            outer = dot_cols(lefts[which, layer], right)
+            total = jnp.sum(right.astype(F32), axis=0, keepdims=True)
+            squares = (
+                outer[:width, :width] + outer[width:, width:],
+                outer[:width, width:] - outer[width:, :width],
+            )
+            for r in range(2):
+                all_ref[(which * LAYERS + layer) * 2 + r] = squares[r]
+                slot = (layer * 2 + which) * 2 + r
+                sums = sums + jnp.where(index == slot, total[:, r * width : (r + 1) * width], 0.0)
+            return sums
+
         for layer in range(LAYERS):
             z_low = z.astype(BF16)
-            keep_ref[layer] = z_low
+            lefts[0, layer] = z_low
             pre = dot(z_low, w_ref[2 * layer]) + b_ref[2 * layer]
             sig = jax.nn.sigmoid(pre)
             hidden = (pre * sig).astype(BF16)
-            keep_ref[2 + layer] = hidden
+            lefts[1, layer] = hidden
             slopes.append(sig * (1.0 + pre * (1.0 - sig)))
             if layer + 1 < LAYERS:
                 out = dot(hidden, w_ref[2 * layer + 1]) + b_ref[2 * layer + 1]
@@ -254,9 +272,9 @@
         total = None
         for layer in reversed(range(LAYERS)):
             dout = (grad * mask_of(layer)).astype(BF16)
-            keep_ref[6 + layer] = dout
+            sums = products(1, layer, dout, sums)
             dpre = (dot_rows(dout, w_ref[2 * layer + 1]) * slopes[layer]).astype(BF16)
-            keep_ref[4 + layer] = dpre
+            sums = products(0, layer, dpre, sums)
             dz = dot_rows(dpre, w_ref[2 * layer])
             if layer:
                 grad = grad + through_grid(dz.astype(BF16))
@@ -267,44 +285,10 @@
             part = jnp.concatenate([part[:, :width], part[:, width:]], axis=0)
             tmp[0, pl.ds(k, 2 * lat, stride=per), :] = dot(mix_t, part)
         da_ref[...] = tmp[0].astype(BF16).reshape(chunk)
-
-    return pl.pallas_call(
-        body,
-        in_specs=[SMEM] + [VMEM] * 5,
-        out_specs=[VMEM, VMEM],
-        scratch_shapes=[pltpu.VMEM((2, 2 * lat * per, width), F32)],
-        out_shape=[
-            jax.ShapeDtypeStruct(chunk, BF16),
-            jax.ShapeDtypeStruct((8, tall, 2 * width), BF16),
-        ],
-        compiler_params=params(),
-        name="spectral_chain",
-    )(scalars, parts, mixer, mixer_t, weights, biases)
-
-
-def gradient_parts(scalars, kept_values, quarters, width):
-    own = width // quarters
-    count = 4 * LAYERS * own + 16
-
-    def body(s_ref, v_ref, mine_ref, *rest):
-        others, all_ref = (rest[:-1], rest[-1])
-        index = lax.broadcasted_iota(jnp.int32, (16, width), 0)
-        sums = jnp.zeros((16, width), F32)
-        for which in range(2):
-            for layer in range(LAYERS):
-                right = v_ref[4 + 2 * which + layer]
-                outer = dot_cols(v_ref[2 * which + layer], right)
-                total = jnp.sum(right.astype(F32), axis=0, keepdims=True)
-                squares = (
-                    outer[:width, :width] + outer[width:, width:],
-                    outer[:width, width:] - outer[width:, :width],
-                )
-                for r in range(2):
-                    all_ref[(which * LAYERS + layer) * 2 + r] = squares[r]
-                    slot = (layer * 2 + which) * 2 + r
-                    sums = sums + jnp.where(index == slot, total[:, r * width : (r + 1) * width], 0.0)
-        for step, o_ref in enumerate((mine_ref,) + others):
-            start = pl.multiple_of((s_ref[2] + step) % quarters * own, own)
+        targets = (quarter, quarter ^ 2, quarter ^ 1, quarter ^ 3)
+        for slot, target in enumerate(targets):
+            o_ref = (mine_ref, send_ref)[slot // 2].at[slot % 2]
+            start = pl.multiple_of(target * own, own)
             for square in range(4 * LAYERS):
                 part = all_ref[square, pl.ds(start, own), :]
                 o_ref[square * own : (square + 1) * own] = part.astype(o_ref.dtype)
@@ -312,37 +296,39 @@
 
     return pl.pallas_call(
         body,
-        in_specs=[SMEM, VMEM],
-        out_specs=[VMEM] * quarters,
-        scratch_shapes=[pltpu.VMEM((4 * LAYERS, width, width), F32)],
-        out_shape=[jax.ShapeDtypeStruct((count, width), F32)]
-        + [jax.ShapeDtypeStruct((count, width), BF16)] * (quarters - 1),
+        in_specs=[SMEM] + [VMEM] * 5,
+        out_specs=[VMEM] * 3,
+        scratch_shapes=[
+            pltpu.VMEM((2, 2 * lat * per, width), F32),
+            pltpu.VMEM((4 * LAYERS, width, width), F32),
+        ],
+        out_shape=[
+            jax.ShapeDtypeStruct(chunk, BF16),
+            jax.ShapeDtypeStruct((2, count, width), F32),
+            jax.ShapeDtypeStruct((2, count, width), BF16),
+        ],
         compiler_params=params(),
-        name="gradient_parts",
-    )(scalars, kept_values)
-
-
-def gradient_sum(scalars, parts, width):
-    quarters = len(parts)
+        name="spectral_chain",
+    )(scalars, parts, mixer, mixer_t, weights, biases)
+
+
+def gradient_sum(scalars, mine, near, far, width, quarters):
     own = width // quarters
     half = 2 * LAYERS * own
 
-    def body(s_ref, *refs):
-        first_ref, second_ref, bias_ref = refs[quarters:]
-        total = refs[0][...]
-        for ref in refs[1:quarters]:
-            total = total + ref[...].astype(F32)
+    def body(s_ref, mine_ref, near_ref, far_ref, first_ref, second_ref, bias_ref):
+        total = mine_ref[0] + near_ref[0].astype(F32) + far_ref[...].astype(F32)
         first_ref[...] = total[:half]
         second_ref[...] = total[half : 2 * half]
         sums = total[2 * half : 2 * half + 8]
-        mine = sums[:, :own]
+        part = sums[:, :own]
         for q in range(1, quarters):
-            mine = jnp.where(s_ref[2] == q, sums[:, q * own : (q + 1) * own], mine)
-        bias_ref[...] = mine
+            part = jnp.where(s_ref[2] == q, sums[:, q * own : (q + 1) * own], part)
+        bias_ref[...] = part
 
     return pl.pallas_call(
         body,
-        in_specs=[SMEM] + [VMEM] * quarters,
+        in_specs=[SMEM, VMEM, VMEM, VMEM],
         out_specs=[VMEM, VMEM, VMEM],
         out_shape=[
             jax.ShapeDtypeStruct((half, width), F32),
@@ -351,7 +337,7 @@
         ],
         compiler_params=params(),
         name="gradient_sum",
-    )(scalars, *parts)
+    )(scalars, mine, near, far)
 
 
 def on_device(section_input, handoff, loss_grad, w_first, w_second, bias, kept):
@@ -383,21 +369,19 @@
     received = lax.ppermute(later, "section", ring)
     cot = jnp.where(section == sections - 1, loss_grad, received[0]).reshape(cells)
     weights, biases = block_params(scalars, w_first, w_second, bias, width)
-    da, values = spectral_chain(
-        scalars, both, mixer, mixer.T.copy(), weights, biases, lat, width
+    cot, both = lax.optimization_barrier((cot, both))
+    da, mine, send = spectral_chain(
+        scalars, both, mixer, mixer.T.copy(), weights, biases, lat, width, quarters
     )
+
+    def swapped(value, bit):
+        return lax.ppermute(value, "lat", [(d, d ^ bit) for d in range(lat_count)])
+
+    near = swapped(send, 1)
     da = lax.all_to_all(da, "lat", split_axis=0, concat_axis=0, tiled=True)
-    parts = list(gradient_parts(scalars, values, quarters, width))
-    for step in range(1, quarters):
-        pairs = [
-            (b * quarters + q, b * quarters + (q + step) % quarters)
-            for b in range(blocks)
-            for q in range(quarters)
-        ]
-        parts[step] = lax.ppermute(parts[step], "lat", pairs)
+    far = swapped((mine[1] + near[1].astype(F32)).astype(BF16), 2)
+    first, second, biases = gradient_sum(scalars, mine, near, far, width, quarters)
     handed = to_cells(da, forward.T.copy(), cot, quarters, width)
-    handed, parts[0] = lax.optimization_barrier((handed, parts[0]))
-    first, second, biases = gradient_sum(scalars, parts, width)
     own = width // quarters
     return (
         handed.reshape(1, rows, lon, channels),

time: 65.4 us -> 67.8 us (1.037)
  waiting for transfers between devices: 17 us -> 25.4 us
  starting transfers between devices: 32.4 us -> 29.8 us
  Pallas kernels: 11.8 us -> 9.86 us
  other arithmetic: 2.05 us -> 1.03 us
    ppermute x3 -> x2, waiting for transfers between devices: 0.62 us -> 8.48 us  [swapped(): return lax.ppermute(value, 'lat', [(d, d ^ bit) for d in range(lat_count)])]
    all_to_all x1, waiting for transfers between devices: 14.4 us -> 9.43 us  [on_device(): both = lax.all_to_all(both, 'lat', split_axis=0, concat_axis=0, tiled=True)]
    ppermute x1, waiting for transfers between devices: 0.01 us -> 4.82 us  [on_device(): received = lax.ppermute(later, 'section', ring)]
    ppermute x3 -> x2, starting transfers between devices: 11.7 us -> 9.05 us  [swapped(): return lax.ppermute(value, 'lat', [(d, d ^ bit) for d in range(lat_count)])]
    pallas_call x2, Pallas kernels: 3.76 us -> 2.62 us  [to_spectral(): pl.pallas_call(body, in_specs=[SMEM, HBM] + [HBM] * len(sources), out_spe...]
    select_n x1, other arithmetic: 1.11 us -> 0.07 us  [on_device(): jnp.where(section == sections - 1, loss_grad, received[0]).reshape(cells)]
    pallas_call x3 -> x2, Pallas kernels: 5.43 us -> 4.65 us  [the longest x1 3.24 us: spectral_chain(): pl.pallas_call(body, in_specs=[SMEM] + [VMEM] * 5, out_specs=[VMEM] * 3,...]
  transfers between devices with their start and end apart: 7 -> 6, of which waited for: 4 -> 5; matrix products, arithmetic and copies ran while one was open for 2% -> 1% of each run, Pallas kernels for 13% -> 6%
where the time goes in v3:
time: 67.8 us; the launch traced here: 67 us
  starting transfers between devices  29.8 us (44%)
  waiting for transfers between devices  25.4 us (37%)
  Pallas kernels  9.86 us (15%)
  other arithmetic  1.03 us (2%)
  between operations  0.76 us (1%)
    all_to_all x1, starting transfers between devices, on_device(): both = lax.all_to_all(both, 'lat', split_axis=0, concat_axis=0, tiled=True)  13.2 us
    all_to_all x1, waiting for transfers between devices, on_device(): both = lax.all_to_all(both, 'lat', split_axis=0, concat_axis=0, tiled=True)  9.43 us
    ppermute x2, starting transfers between devices, swapped(): return lax.ppermute(value, 'lat', [(d, d ^ bit) for d in range(lat_count)])  9.05 us
    ppermute x2, waiting for transfers between devices, swapped(): return lax.ppermute(value, 'lat', [(d, d ^ bit) for d in range(lat_count)])  8.48 us
    all_to_all x1, starting transfers between devices, on_device(): da = lax.all_to_all(da, 'lat', split_axis=0, concat_axis=0, tiled=True)  5.05 us
    ppermute x1, waiting for transfers between devices, on_device(): received = lax.ppermute(later, 'section', ring)  4.82 us
    pallas_call x1, Pallas kernels, spectral_chain(): pl.pallas_call(body, in_specs=[SMEM] + [VMEM] * 5, out_specs=[VMEM] * 3,...  3.24 us
    ppermute x1, waiting for transfers between devices, on_device(): du = lax.ppermute(du, 'section', ring)  2.65 us
  transfers between devices with their start and end apart: 6, of which 5 were waited for; matrix products, arithmetic and copies ran while one was open for 1% of the time, Pallas kernels for 6%

profile of v3, /device:TPU:56, one launch (start us, length us, event | category | flops | bytes accessed | tf_op | source)
XLA Modules:
  0.0 67.0 jit_solution(11245995063662111683)
XLA Ops:
  0.6 0.0 copy-start
  0.7 1.3 %to_spectral.3 = bf16[32,32,128]{2,1,0:T(8,128)(2,1)S(1)} custom-call(s32[1]{0:T(128)} %bitcast.s_ref, bf16[128,256]{1,0:T(8,128)(2,1)} %constant.50.clone.t_hbm, bf16[256,1024]{1,0:T(8,128)(2,1)} %bitcast.17, bf16[256,1024]{1,0:T(8,128)(2,1)} %bitcast.16), custom_call_target="tpu_custom_call" | custom-call | tf_op jit(solution)/shard_map/to_spectral/pallas_call | solution.py:105
  2.0 0.8 %collective-permute-start = (bf16[32,32,128]{2,1,0:T(8,128)(2,1)S(1)}, bf16[32,32,128]{2,1,0:T(8,128)(2,1)S(1)}, u32[]{:S(2)}, u32[]{:S(2)}) collective-permute-start(bf16[32,32,128]{2,1,0:T(8,128)(2,1)S(1)} %to_spectral.3), channel_id=1, source_target_pairs={{0,480},{32,0},{64,32},{96,64},{128,96},{160,128},{192,160},{224,1... | collective-permute-start | bytes 786440 | tf_op jit(solution)/shard_map/ppermute | solution.py:364
  2.8 1.3 %to_spectral.2 = bf16[32,32,128]{2,1,0:T(8,128)(2,1)S(1)} custom-call(s32[1]{0:T(128)} %bitcast.s_ref, bf16[128,256]{1,0:T(8,128)(2,1)} %constant.51.clone.t_hbm, bf16[256,1024]{1,0:T(8,128)(2,1)} %bitcast.18), custom_call_target="tpu_custom_call" | custom-call | tf_op jit(solution)/shard_map/to_spectral/pallas_call | solution.py:105
  4.1 2.7 %collective-permute-done = bf16[32,32,128]{2,1,0:T(8,128)(2,1)S(1)} collective-permute-done((bf16[32,32,128]{2,1,0:T(8,128)(2,1)S(1)}, bf16[32,32,128]{2,1,0:T(8,128)(2,1)S(1)}, u32[]{:S(2)}, u32[]{:S(2)}) %collective-permute-start) | collective-permute-done | bytes 262176 | tf_op jit(solution)/shard_map/ppermute | solution.py:364
  6.7 0.9 %pad_maximum_fusion = bf16[32,64,128]{2,1,0:T(8,128)(2,1)} fusion(bf16[32,32,128]{2,1,0:T(8,128)(2,1)S(1)} %collective-permute-done, bf16[32,32,128]{2,1,0:T(8,128)(2,1)S(1)} %to_spectral.2), kind=kLoop, calls=%fused_computation | loop fusion | flops 1048576 | bytes 1048576 | tf_op jit(solution)/shard_map/concatenate | solution.py:366
  7.6 13.2 %all-to-all-start = ((bf16[32,64,128]{2,1,0:T(8,128)(2,1)}), bf16[32,64,128]{2,1,0:T(8,128)(2,1)S(1)}, u32[]{:S(2)}, u32[]{:S(2)}) async-start(bf16[32,64,128]{2,1,0:T(8,128)(2,1)} %pad_maximum_fusion), calls=%async_computation | async-start | bytes 1048576 | tf_op jit(solution)/shard_map/all_to_all | solution.py:368
  20.8 0.0 copy-done.6
  20.8 0.0 copy-start.2
  20.8 1.6 %collective-permute-start.1 = (bf16[1,2,128,1024]{3,2,1,0:T(8,128)(2,1)S(1)}, bf16[1,2,128,1024]{3,2,1,0:T(8,128)(2,1)S(1)}, u32[]{:S(2)}, u32[]{:S(2)}) collective-permute-start(bf16[1,2,128,1024]{3,2,1,0:T(8,128)(2,1)S(1)} %copy-done.6), channel_id=1, source_target_pairs={{0,480},{32,0},{64,32},{96,64},{128,96},{160,128},{192,160},{224,1... | collective-permute-start | bytes 1572872 | tf_op jit(solution)/shard_map/ppermute | solution.py:369
  22.5 0.0 copy-done
  22.5 0.2 dynamic-slice_reduce_fusion
  22.7 0.1 pad_add_fusion.s_ref
  22.8 0.0 copy-done.2
  22.8 1.6 %block_params.1 = (bf16[4,256,256]{2,1,0:T(8,128)(2,1)S(1)}, f32[4,1,256]{2,1,0:T(1,128)S(1)}) custom-call(s32[5]{0:T(128)S(1)} %pad_add_fusion.s_ref, bf16[1,2,2,1024,128]{4,3,2,1,0:T(8,128)(2,1)} %w1_hbm.1, bf16[1,2,2,1024,128]{4,3,2,1,0:T(8,128)(2,1)} %w2_hbm.1, f32[1,2,2,2,1024]{4,3,2,1,0:T(2,128)S(1)} %copy-done.2), custom_call_target="tpu_custom_call" | custom-call | tf_op jit(solution)/shard_map/block_params/pallas_call | solution.py:182
  24.3 0.0 copy-start.3
  24.3 0.0 copy-start.4
  24.4 4.8 %collective-permute-done.1 = bf16[1,2,128,1024]{3,2,1,0:T(8,128)(2,1)S(1)} collective-permute-done((bf16[1,2,128,1024]{3,2,1,0:T(8,128)(2,1)S(1)}, bf16[1,2,128,1024]{3,2,1,0:T(8,128)(2,1)S(1)}, u32[]{:S(2)}, u32[]{:S(2)}) %collective-permute-start.1) | collective-permute-done | bytes 524320 | tf_op jit(solution)/shard_map/ppermute | solution.py:369
  29.2 0.0 copy-done.5
  29.2 0.1 bitcast_select_fusion
  29.3 9.4 %all-to-all-done.parts_ref = bf16[32,64,128]{2,1,0:T(8,128)(2,1)S(1)} async-done(((bf16[32,64,128]{2,1,0:T(8,128)(2,1)}), bf16[32,64,128]{2,1,0:T(8,128)(2,1)S(1)}, u32[]{:S(2)}, u32[]{:S(2)}) %all-to-all-start) | async-done | bytes 524320 | tf_op jit(solution)/shard_map/all_to_all | solution.py:368
  38.7 0.0 copy-done.4
  38.7 3.2 %spectral_chain.1 = (bf16[32,32,128]{2,1,0:T(8,128)(2,1)}, f32[2,272,128]{2,1,0:T(8,128)S(1)}, bf16[2,272,128]{2,1,0:T(8,128)(2,1)S(1)}) custom-call(s32[5]{0:T(128)S(1)} %pad_add_fusion.s_ref, bf16[32,64,128]{2,1,0:T(8,128)(2,1)S(1)} %all-to-all-done.parts_ref, bf16[128,128]{1,0:T(8,128)(2,1)S(1)} %copy-done.4, bf16[128,128]{1,0:T(8,128)(2,1)S(1)} %copy-done.3, ...), custom_call_target="tpu_custom_call" | custom-call | tf_op jit(solution)/shard_map/spectral_chain/pallas_call | solution.py:297
  41.9 5.1 %all-to-all-start.1 = ((bf16[32,32,128]{2,1,0:T(8,128)(2,1)}), bf16[32,32,128]{2,1,0:T(8,128)(2,1)S(1)}, u32[]{:S(2)}, u32[]{:S(2)}) async-start(bf16[32,32,128]{2,1,0:T(8,128)(2,1)} %get-tuple-element.21), calls=%async_computation.1 | async-start | bytes 524288 | tf_op jit(solution)/shard_map/all_to_all | solution.py:381
  47.0 3.7 %collective-permute-start.2 = (bf16[2,272,128]{2,1,0:T(8,128)(2,1)S(1)}, bf16[2,272,128]{2,1,0:T(8,128)(2,1)S(1)}, u32[]{:S(2)}, u32[]{:S(2)}) collective-permute-start(bf16[2,272,128]{2,1,0:T(8,128)(2,1)S(1)} %get-tuple-element.24), channel_id=1, source_target_pairs={{0,1},{1,0},{2,3},{3,2},{4,5},{5,4},{6,7},{7,6},{8,9},{9,8},{10,11... | collective-permute-start | bytes 417800 | tf_op jit(solution)/shard_map/ppermute | solution.py:378
  50.7 6.0 %collective-permute-done.2.near_ref = bf16[2,272,128]{2,1,0:T(8,128)(2,1)S(1)} collective-permute-done((bf16[2,272,128]{2,1,0:T(8,128)(2,1)S(1)}, bf16[2,272,128]{2,1,0:T(8,128)(2,1)S(1)}, u32[]{:S(2)}, u32[]{:S(2)}) %collective-permute-start.2) | collective-permute-done | bytes 139296 | tf_op jit(solution)/shard_map/ppermute | solution.py:378
  56.7 0.0 copy-start.1
  56.7 5.4 %collective-permute-start.3 = (bf16[272,128]{1,0:T(8,128)(2,1)S(1)}, bf16[272,128]{1,0:T(8,128)(2,1)S(1)}, u32[]{:S(2)}, u32[]{:S(2)}) collective-permute-start(bf16[272,128]{1,0:T(8,128)(2,1)S(1)} %fusion), channel_id=1, source_target_pairs={{0,2},{1,3},{2,0},{3,1},{4,6},{5,7},{6,4},{7,5},{8,10},{9,11},{10,... | collective-permute-start | bytes 208904 | tf_op jit(solution)/shard_map/ppermute | solution.py:378
  62.1 2.5 %collective-permute-done.3.far_ref = bf16[272,128]{1,0:T(8,128)(2,1)S(1)} collective-permute-done((bf16[272,128]{1,0:T(8,128)(2,1)S(1)}, bf16[272,128]{1,0:T(8,128)(2,1)S(1)}, u32[]{:S(2)}, u32[]{:S(2)}) %collective-permute-start.3) | collective-permute-done | bytes 69664 | tf_op jit(solution)/shard_map/ppermute | solution.py:378
  64.6 1.4 %gradient_sum.1 = (f32[128,128]{1,0:T(8,128)}, f32[128,128]{1,0:T(8,128)}, f32[8,32]{1,0:T(8,128)}) custom-call(s32[5]{0:T(128)S(1)} %pad_add_fusion.s_ref, f32[2,272,128]{2,1,0:T(8,128)S(1)} %get-tuple-element.23.mine_ref, bf16[2,272,128]{2,1,0:T(8,128)(2,1)S(1)} %collective-permute-done.2.near_ref, bf16[272,128]{1,0:T(8,128)(2,1)S(1)} %collective-permute-done.3.far_ref), custom_call_target="tpu_custom_call" | custom-call | tf_op jit(solution)/shard_map/gradient_sum/pallas_call | solution.py:329
  66.0 0.0 all-to-all-done.1.p_ref
  66.0 1.0 %to_cells.1 = bf16[256,1024]{1,0:T(8,128)(2,1)} custom-call(bf16[256,128]{1,0:T(8,128)(2,1)S(1)} %copy-done.1, bf16[32,32,128]{2,1,0:T(8,128)(2,1)S(1)} %all-to-all-done.1.p_ref, bf16[256,1024]{1,0:T(8,128)(2,1)S(1)} %bitcast.15), custom_call_target="tpu_custom_call" | custom-call | tf_op jit(solution)/shard_map/to_cells/pallas_call | solution.py:144
  (5 shorter events, 0.0 us)
Async XLA Ops:
  0.6 21.9 %copy-start = (s32[1,2,8]{2,1,0:T(2,128)S(1)}, s32[1,2,8]{2,1,0:T(2,128)}, u32[]{:S(2)}) copy-start(s32[1,2,8]{2,1,0:T(2,128)} %param.18) | copy-start | bytes 196
  2.0 4.8 %collective-permute-start = (bf16[32,32,128]{2,1,0:T(8,128)(2,1)S(1)}, bf16[32,32,128]{2,1,0:T(8,128)(2,1)S(1)}, u32[]{:S(2)}, u32[]{:S(2)}) collective-permute-start(bf16[32,32,128]{2,1,0:T(8,128)(2,1)S(1)} %to_spectral.3), channel_id=1, source_target_pairs={{0,480},{32,0},{64,32},{96,64},{128,96},{160,128},{192,160},{224,1... | collective-permute-start | bytes 786440 | tf_op jit(solution)/shard_map/ppermute | solution.py:364
  7.6 13.2 %copy-start.6 = (bf16[1,2,128,1024]{3,2,1,0:T(8,128)(2,1)S(1)}, bf16[1,2,128,1024]{3,2,1,0:T(8,128)(2,1)}, u32[]{:S(2)}) copy-start(bf16[1,2,128,1024]{3,2,1,0:T(8,128)(2,1)} %param.13) | copy-start | bytes 1572868
  7.6 31.1 %all-to-all-start = ((bf16[32,64,128]{2,1,0:T(8,128)(2,1)}), bf16[32,64,128]{2,1,0:T(8,128)(2,1)S(1)}, u32[]{:S(2)}, u32[]{:S(2)}) async-start(bf16[32,64,128]{2,1,0:T(8,128)(2,1)} %pad_maximum_fusion), calls=%async_computation | async-start | bytes 1048576 | tf_op jit(solution)/shard_map/all_to_all | solution.py:368
  20.8 1.9 %copy-start.2 = (f32[1,2,2,2,1024]{4,3,2,1,0:T(2,128)S(1)}, f32[1,2,2,2,1024]{4,3,2,1,0:T(2,128)}, u32[]{:S(2)}) copy-start(f32[1,2,2,2,1024]{4,3,2,1,0:T(2,128)} %b_ref.1) | copy-start | bytes 98308
  20.8 8.3 %collective-permute-start.1 = (bf16[1,2,128,1024]{3,2,1,0:T(8,128)(2,1)S(1)}, bf16[1,2,128,1024]{3,2,1,0:T(8,128)(2,1)S(1)}, u32[]{:S(2)}, u32[]{:S(2)}) collective-permute-start(bf16[1,2,128,1024]{3,2,1,0:T(8,128)(2,1)S(1)} %copy-done.6), channel_id=1, source_target_pairs={{0,480},{32,0},{64,32},{96,64},{128,96},{160,128},{192,160},{224,1... | collective-permute-start | bytes 1572872 | tf_op jit(solution)/shard_map/ppermute | solution.py:369
  22.8 6.4 %copy-start.5 = (bf16[2,128,1024]{2,1,0:T(8,128)(2,1)S(1)}, bf16[2,128,1024]{2,1,0:T(8,128)(2,1)}, u32[]{:S(2)}) copy-start(bf16[2,128,1024]{2,1,0:T(8,128)(2,1)} %param.14) | copy-start | bytes 1572868
  24.3 14.4 %copy-start.3 = (bf16[128,128]{1,0:T(8,128)(2,1)S(1)}, bf16[128,128]{1,0:T(8,128)(2,1)}, u32[]{:S(2)}) copy-start(bf16[128,128]{1,0:T(8,128)(2,1)} %constant.53.clone.lt_ref) | copy-start | bytes 98308
  24.3 14.3 %copy-start.4 = (bf16[128,128]{1,0:T(8,128)(2,1)S(1)}, bf16[128,128]{1,0:T(8,128)(2,1)}, u32[]{:S(2)}) copy-start(bf16[128,128]{1,0:T(8,128)(2,1)} %constant.52.clone.l_ref) | copy-start | bytes 98308
  41.9 24.1 %all-to-all-start.1 = ((bf16[32,32,128]{2,1,0:T(8,128)(2,1)}), bf16[32,32,128]{2,1,0:T(8,128)(2,1)S(1)}, u32[]{:S(2)}, u32[]{:S(2)}) async-start(bf16[32,32,128]{2,1,0:T(8,128)(2,1)} %get-tuple-element.21), calls=%async_computation.1 | async-start | bytes 524288 | tf_op jit(solution)/shard_map/all_to_all | solution.py:381
  47.0 9.7 %collective-permute-start.2 = (bf16[2,272,128]{2,1,0:T(8,128)(2,1)S(1)}, bf16[2,272,128]{2,1,0:T(8,128)(2,1)S(1)}, u32[]{:S(2)}, u32[]{:S(2)}) collective-permute-start(bf16[2,272,128]{2,1,0:T(8,128)(2,1)S(1)} %get-tuple-element.24), channel_id=1, source_target_pairs={{0,1},{1,0},{2,3},{3,2},{4,5},{5,4},{6,7},{7,6},{8,9},{9,8},{10,11... | collective-permute-start | bytes 417800 | tf_op jit(solution)/shard_map/ppermute | solution.py:378
  56.7 9.3 %copy-start.1 = (bf16[256,128]{1,0:T(8,128)(2,1)S(1)}, bf16[256,128]{1,0:T(8,128)(2,1)}, u32[]{:S(2)}) copy-start(bf16[256,128]{1,0:T(8,128)(2,1)} %constant.54.clone.t_ref) | copy-start | bytes 196612
  56.7 7.8 %collective-permute-start.3 = (bf16[272,128]{1,0:T(8,128)(2,1)S(1)}, bf16[272,128]{1,0:T(8,128)(2,1)S(1)}, u32[]{:S(2)}, u32[]{:S(2)}) collective-permute-start(bf16[272,128]{1,0:T(8,128)(2,1)S(1)} %fusion), channel_id=1, source_target_pairs={{0,2},{1,3},{2,0},{3,1},{4,6},{5,7},{6,4},{7,5},{8,10},{9,11},{10,... | collective-permute-start | bytes 208904 | tf_op jit(solution)/shard_map/ppermute | solution.py:378

commit v4 on v3

--- a/solution.py
+++ b/solution.py
@@ -205,7 +205,8 @@
     own = width // quarters
     count = 4 * LAYERS * own + 16
 
-    def body(s_ref, parts_ref, l_ref, lt_ref, w_ref, b_ref, da_ref, mine_ref, send_ref, tmp, all_ref):
+    def body(s_ref, parts_ref, l_ref, lt_ref, w_ref, b_ref, da_ref, *rest):
+        mine_and_sent, tmp, all_ref = (rest[:quarters], rest[quarters], rest[quarters + 1])
         quarter = s_ref[2]
         mix, mix_t = (l_ref[...], lt_ref[...])
 
@@ -285,10 +286,8 @@
             part = jnp.concatenate([part[:, :width], part[:, width:]], axis=0)
             tmp[0, pl.ds(k, 2 * lat, stride=per), :] = dot(mix_t, part)
         da_ref[...] = tmp[0].astype(BF16).reshape(chunk)
-        targets = (quarter, quarter ^ 2, quarter ^ 1, quarter ^ 3)
-        for slot, target in enumerate(targets):
-            o_ref = (mine_ref, send_ref)[slot // 2].at[slot % 2]
-            start = pl.multiple_of(target * own, own)
+        for step, o_ref in enumerate(mine_and_sent):
+            start = pl.multiple_of((quarter + step) % quarters * own, own)
             for square in range(4 * LAYERS):
                 part = all_ref[square, pl.ds(start, own), :]
                 o_ref[square * own : (square + 1) * own] = part.astype(o_ref.dtype)
@@ -297,39 +296,61 @@
     return pl.pallas_call(
         body,
         in_specs=[SMEM] + [VMEM] * 5,
-        out_specs=[VMEM] * 3,
+        out_specs=[VMEM] * (1 + quarters),
         scratch_shapes=[
             pltpu.VMEM((2, 2 * lat * per, width), F32),
             pltpu.VMEM((4 * LAYERS, width, width), F32),
         ],
         out_shape=[
             jax.ShapeDtypeStruct(chunk, BF16),
-            jax.ShapeDtypeStruct((2, count, width), F32),
-            jax.ShapeDtypeStruct((2, count, width), BF16),
-        ],
+            jax.ShapeDtypeStruct((count, width), F32),
+        ]
+        + [jax.ShapeDtypeStruct((count, width), BF16)] * (quarters - 1),
         compiler_params=params(),
         name="spectral_chain",
     )(scalars, parts, mixer, mixer_t, weights, biases)
 
 
-def gradient_sum(scalars, mine, near, far, width, quarters):
+def gradient_sum(scalars, parts, width):
+    quarters = len(parts)
     own = width // quarters
     half = 2 * LAYERS * own
 
-    def body(s_ref, mine_ref, near_ref, far_ref, first_ref, second_ref, bias_ref):
-        total = mine_ref[0] + near_ref[0].astype(F32) + far_ref[...].astype(F32)
-        first_ref[...] = total[:half]
-        second_ref[...] = total[half : 2 * half]
-        sums = total[2 * half : 2 * half + 8]
+    def body(s_ref, *refs):
+        first_hbm, second_hbm, bias_hbm, buf, bias_buf, sem = refs[quarters:]
+
+        def added(start, size):
+            total = refs[0][start : start + size]
+            for ref in refs[1:quarters]:
+                total = total + ref[start : start + size].astype(F32)
+            return total
+
+        copies = [
+            pltpu.make_async_copy(bias_buf, bias_hbm, sem.at[2]),
+            pltpu.make_async_copy(buf.at[0], first_hbm, sem.at[0]),
+            pltpu.make_async_copy(buf.at[1], second_hbm, sem.at[1]),
+        ]
+        sums = added(2 * half, 16)[:8]
         part = sums[:, :own]
         for q in range(1, quarters):
             part = jnp.where(s_ref[2] == q, sums[:, q * own : (q + 1) * own], part)
-        bias_ref[...] = part
+        bias_buf[...] = part
+        copies[0].start()
+        for which in range(2):
+            buf[which] = added(which * half, half)
+            copies[1 + which].start()
+        for copy in copies:
+            copy.wait()
 
     return pl.pallas_call(
         body,
-        in_specs=[SMEM, VMEM, VMEM, VMEM],
-        out_specs=[VMEM, VMEM, VMEM],
+        in_specs=[SMEM] + [VMEM] * quarters,
+        out_specs=[HBM] * 3,
+        scratch_shapes=[
+            pltpu.VMEM((2, half, width), F32),
+            pltpu.VMEM((8, own), F32),
+            pltpu.SemaphoreType.DMA((3,)),
+        ],
         out_shape=[
             jax.ShapeDtypeStruct((half, width), F32),
             jax.ShapeDtypeStruct((half, width), F32),
@@ -337,7 +358,7 @@
         ],
         compiler_params=params(),
         name="gradient_sum",
-    )(scalars, mine, near, far)
+    )(scalars, *parts)
 
 
 def on_device(section_input, handoff, loss_grad, w_first, w_second, bias, kept):
@@ -363,25 +384,27 @@
     du = to_spectral(section.reshape(1), handed_du, inverse, quarters, width)
     du = lax.ppermute(du, "section", ring)
     spec = to_spectral(section.reshape(1), (section_input.reshape(cells),), forward, quarters, width)
+    later, spec = lax.optimization_barrier((handoff, spec))
     both = jnp.concatenate([spec, du], axis=1)
-    later, both = lax.optimization_barrier((handoff, both))
     both = lax.all_to_all(both, "lat", split_axis=0, concat_axis=0, tiled=True)
     received = lax.ppermute(later, "section", ring)
     cot = jnp.where(section == sections - 1, loss_grad, received[0]).reshape(cells)
     weights, biases = block_params(scalars, w_first, w_second, bias, width)
     cot, both = lax.optimization_barrier((cot, both))
-    da, mine, send = spectral_chain(
+    da, *parts = spectral_chain(
         scalars, both, mixer, mixer.T.copy(), weights, biases, lat, width, quarters
     )
-
-    def swapped(value, bit):
-        return lax.ppermute(value, "lat", [(d, d ^ bit) for d in range(lat_count)])
-
-    near = swapped(send, 1)
     da = lax.all_to_all(da, "lat", split_axis=0, concat_axis=0, tiled=True)
-    far = swapped((mine[1] + near[1].astype(F32)).astype(BF16), 2)
-    first, second, biases = gradient_sum(scalars, mine, near, far, width, quarters)
+    for step in range(1, quarters):
+        pairs = [
+            (b * quarters + q, b * quarters + (q + step) % quarters)
+            for b in range(blocks)
+            for q in range(quarters)
+        ]
+        parts[step] = lax.ppermute(parts[step], "lat", pairs)
     handed = to_cells(da, forward.T.copy(), cot, quarters, width)
+    handed, parts[0] = lax.optimization_barrier((handed, parts[0]))
+    first, second, biases = gradient_sum(scalars, parts, width)
     own = width // quarters
     return (
         handed.reshape(1, rows, lon, channels),

time: 67.8 us -> 64.2 us (0.947)
  waiting for transfers between devices: 25.4 us -> 19.2 us
  starting transfers between devices: 29.8 us -> 32.5 us
    ppermute x2 -> x3, waiting for transfers between devices: 8.48 us -> 0.01 us  [on_device(): parts[step] = lax.ppermute(parts[step], 'lat', pairs)]
    ppermute x2 -> x3, starting transfers between devices: 9.05 us -> 11.7 us  [on_device(): parts[step] = lax.ppermute(parts[step], 'lat', pairs)]
    all_to_all x1, waiting for transfers between devices: 0.01 us -> 2.24 us  [on_device(): da = lax.all_to_all(da, 'lat', split_axis=0, concat_axis=0, tiled=True)]
  transfers between devices with their start and end apart: 6 -> 7, of which waited for: 5 -> 4; matrix products, arithmetic and copies ran while one was open for 1% -> 1% of each run, Pallas kernels for 6% -> 6%
where the time goes in v4:
time: 64.2 us; the launch traced here: 63.6 us
  starting transfers between devices  32.5 us (51%)
  waiting for transfers between devices  19.2 us (30%)
  Pallas kernels  9.96 us (16%)
  other arithmetic  1 us (2%)
  between operations  0.78 us (1%)
    all_to_all x1, starting transfers between devices, on_device(): both = lax.all_to_all(both, 'lat', split_axis=0, concat_axis=0, tiled=True)  13.2 us
    ppermute x3, starting transfers between devices, on_device(): parts[step] = lax.ppermute(parts[step], 'lat', pairs)  11.7 us
    all_to_all x1, waiting for transfers between devices, on_device(): both = lax.all_to_all(both, 'lat', split_axis=0, concat_axis=0, tiled=True)  9.44 us
    all_to_all x1, starting transfers between devices, on_device(): da = lax.all_to_all(da, 'lat', split_axis=0, concat_axis=0, tiled=True)  5.18 us
    ppermute x1, waiting for transfers between devices, on_device(): received = lax.ppermute(later, 'section', ring)  4.82 us
    pallas_call x1, Pallas kernels, spectral_chain(): pl.pallas_call(body, in_specs=[SMEM] + [VMEM] * 5, out_specs=[VMEM] * (1...  3.24 us
    ppermute x1, waiting for transfers between devices, on_device(): du = lax.ppermute(du, 'section', ring)  2.65 us
    pallas_call x2, Pallas kernels, to_spectral(): pl.pallas_call(body, in_specs=[SMEM, HBM] + [HBM] * len(sources), out_spe...  2.62 us
  transfers between devices with their start and end apart: 7, of which 4 were waited for; matrix products, arithmetic and copies ran while one was open for 1% of the time, Pallas kernels for 6%

profile of v4, /device:TPU:56, one launch (start us, length us, event | category | flops | bytes accessed | tf_op | source)
XLA Modules:
  0.0 63.6 jit_solution(4716561092875469056)
XLA Ops:
  0.6 0.0 copy-start
  0.7 1.3 %to_spectral.3 = bf16[32,32,128]{2,1,0:T(8,128)(2,1)S(1)} custom-call(s32[1]{0:T(128)} %bitcast.s_ref, bf16[128,256]{1,0:T(8,128)(2,1)} %constant.50.clone.t_hbm, bf16[256,1024]{1,0:T(8,128)(2,1)} %bitcast.15, bf16[256,1024]{1,0:T(8,128)(2,1)} %bitcast.14), custom_call_target="tpu_custom_call" | custom-call | tf_op jit(solution)/shard_map/to_spectral/pallas_call | solution.py:105
  2.0 0.8 %collective-permute-start.1 = (bf16[32,32,128]{2,1,0:T(8,128)(2,1)S(1)}, bf16[32,32,128]{2,1,0:T(8,128)(2,1)S(1)}, u32[]{:S(2)}, u32[]{:S(2)}) collective-permute-start(bf16[32,32,128]{2,1,0:T(8,128)(2,1)S(1)} %to_spectral.3), channel_id=1, source_target_pairs={{0,480},{32,0},{64,32},{96,64},{128,96},{160,128},{192,160},{224,1... | collective-permute-start | bytes 786440 | tf_op jit(solution)/shard_map/ppermute | solution.py:385
  2.8 1.3 %to_spectral.2 = bf16[32,32,128]{2,1,0:T(8,128)(2,1)S(1)} custom-call(s32[1]{0:T(128)} %bitcast.s_ref, bf16[128,256]{1,0:T(8,128)(2,1)} %constant.51.clone.t_hbm, bf16[256,1024]{1,0:T(8,128)(2,1)} %bitcast.16), custom_call_target="tpu_custom_call" | custom-call | tf_op jit(solution)/shard_map/to_spectral/pallas_call | solution.py:105
  4.1 2.7 %collective-permute-done.1 = bf16[32,32,128]{2,1,0:T(8,128)(2,1)S(1)} collective-permute-done((bf16[32,32,128]{2,1,0:T(8,128)(2,1)S(1)}, bf16[32,32,128]{2,1,0:T(8,128)(2,1)S(1)}, u32[]{:S(2)}, u32[]{:S(2)}) %collective-permute-start.1) | collective-permute-done | bytes 262176 | tf_op jit(solution)/shard_map/ppermute | solution.py:385
  6.7 0.9 %pad_maximum_fusion = bf16[32,64,128]{2,1,0:T(8,128)(2,1)} fusion(bf16[32,32,128]{2,1,0:T(8,128)(2,1)S(1)} %collective-permute-done.1, bf16[32,32,128]{2,1,0:T(8,128)(2,1)S(1)} %to_spectral.2), kind=kLoop, calls=%fused_computation | loop fusion | flops 1048576 | bytes 1048576 | tf_op jit(solution)/shard_map/concatenate | solution.py:388
  7.6 13.2 %all-to-all-start = ((bf16[32,64,128]{2,1,0:T(8,128)(2,1)}), bf16[32,64,128]{2,1,0:T(8,128)(2,1)S(1)}, u32[]{:S(2)}, u32[]{:S(2)}) async-start(bf16[32,64,128]{2,1,0:T(8,128)(2,1)} %pad_maximum_fusion), calls=%async_computation | async-start | bytes 1048576 | tf_op jit(solution)/shard_map/all_to_all | solution.py:389
  20.8 0.0 copy-done.6
  20.8 0.0 copy-start.2
  20.8 1.6 %collective-permute-start = (bf16[1,2,128,1024]{3,2,1,0:T(8,128)(2,1)S(1)}, bf16[1,2,128,1024]{3,2,1,0:T(8,128)(2,1)S(1)}, u32[]{:S(2)}, u32[]{:S(2)}) collective-permute-start(bf16[1,2,128,1024]{3,2,1,0:T(8,128)(2,1)S(1)} %copy-done.6), channel_id=1, source_target_pairs={{0,480},{32,0},{64,32},{96,64},{128,96},{160,128},{192,160},{224,1... | collective-permute-start | bytes 1572872 | tf_op jit(solution)/shard_map/ppermute | solution.py:390
  22.5 0.0 copy-done
  22.5 0.2 dynamic-slice_reduce_fusion
  22.7 0.1 pad_add_fusion.s_ref
  22.8 0.0 copy-done.2
  22.8 1.6 %block_params.1 = (bf16[4,256,256]{2,1,0:T(8,128)(2,1)S(1)}, f32[4,1,256]{2,1,0:T(1,128)S(1)}) custom-call(s32[5]{0:T(128)S(1)} %pad_add_fusion.s_ref, bf16[1,2,2,1024,128]{4,3,2,1,0:T(8,128)(2,1)} %w1_hbm.1, bf16[1,2,2,1024,128]{4,3,2,1,0:T(8,128)(2,1)} %w2_hbm.1, f32[1,2,2,2,1024]{4,3,2,1,0:T(2,128)S(1)} %copy-done.2), custom_call_target="tpu_custom_call" | custom-call | tf_op jit(solution)/shard_map/block_params/pallas_call | solution.py:182
  24.3 0.0 copy-start.3
  24.3 0.0 copy-start.4
  24.4 4.8 %collective-permute-done = bf16[1,2,128,1024]{3,2,1,0:T(8,128)(2,1)S(1)} collective-permute-done((bf16[1,2,128,1024]{3,2,1,0:T(8,128)(2,1)S(1)}, bf16[1,2,128,1024]{3,2,1,0:T(8,128)(2,1)S(1)}, u32[]{:S(2)}, u32[]{:S(2)}) %collective-permute-start) | collective-permute-done | bytes 524320 | tf_op jit(solution)/shard_map/ppermute | solution.py:390
  29.2 0.0 copy-done.5
  29.2 0.1 bitcast_select_fusion
  29.2 9.4 %all-to-all-done.parts_ref = bf16[32,64,128]{2,1,0:T(8,128)(2,1)S(1)} async-done(((bf16[32,64,128]{2,1,0:T(8,128)(2,1)}), bf16[32,64,128]{2,1,0:T(8,128)(2,1)S(1)}, u32[]{:S(2)}, u32[]{:S(2)}) %all-to-all-start) | async-done | bytes 524320 | tf_op jit(solution)/shard_map/all_to_all | solution.py:389
  38.7 3.2 %spectral_chain.1 = (bf16[32,32,128]{2,1,0:T(8,128)(2,1)}, f32[272,128]{1,0:T(8,128)S(1)}, bf16[272,128]{1,0:T(8,128)(2,1)S(1)}, bf16[272,128]{1,0:T(8,128)(2,1)S(1)}, bf16[272,128]{1,0:T(8,128)(2,1)S(1)}) custom-call(s32[5]{0:T(128)S(1)} %pad_add_fusion.s_ref, bf16[32,64,128]{2,1,0:T(8,128)(2,1)S(1)} %all-to-all-done.parts_ref, ...), custom_call_target="tpu_custom_call" | custom-call | tf_op jit(solution)/shard_map/spectral_chain/pallas_call | solution.py:296
  41.9 5.2 %all-to-all-start.1 = ((bf16[32,32,128]{2,1,0:T(8,128)(2,1)}), bf16[32,32,128]{2,1,0:T(8,128)(2,1)S(1)}, u32[]{:S(2)}, u32[]{:S(2)}) async-start(bf16[32,32,128]{2,1,0:T(8,128)(2,1)} %get-tuple-element.25), calls=%async_computation.1 | async-start | bytes 524288 | tf_op jit(solution)/shard_map/all_to_all | solution.py:397
  47.1 3.7 %collective-permute-start.2 = (bf16[272,128]{1,0:T(8,128)(2,1)S(1)}, bf16[272,128]{1,0:T(8,128)(2,1)S(1)}, u32[]{:S(2)}, u32[]{:S(2)}) collective-permute-start(bf16[272,128]{1,0:T(8,128)(2,1)S(1)} %get-tuple-element.30), channel_id=1, source_target_pairs={{0,1},{1,2},{2,3},{3,0},{4,5},{5,6},{6,7},{7,4},{8,9},{9,10},{10,1... | collective-permute-start | bytes 208904 | tf_op jit(solution)/shard_map/ppermute | solution.py:404
  50.8 4.6 %collective-permute-start.3 = (bf16[272,128]{1,0:T(8,128)(2,1)S(1)}, bf16[272,128]{1,0:T(8,128)(2,1)S(1)}, u32[]{:S(2)}, u32[]{:S(2)}) collective-permute-start(bf16[272,128]{1,0:T(8,128)(2,1)S(1)} %get-tuple-element.31), channel_id=1, source_target_pairs={{0,2},{1,3},{2,0},{3,1},{4,6},{5,7},{6,4},{7,5},{8,10},{9,11},{10,... | collective-permute-start | bytes 208904 | tf_op jit(solution)/shard_map/ppermute | solution.py:404
  55.4 3.4 %collective-permute-start.4 = (bf16[272,128]{1,0:T(8,128)(2,1)S(1)}, bf16[272,128]{1,0:T(8,128)(2,1)S(1)}, u32[]{:S(2)}, u32[]{:S(2)}) collective-permute-start(bf16[272,128]{1,0:T(8,128)(2,1)S(1)} %get-tuple-element.32), channel_id=1, source_target_pairs={{0,3},{1,0},{2,1},{3,2},{4,7},{5,4},{6,5},{7,6},{8,11},{9,8},{10,9... | collective-permute-start | bytes 208904 | tf_op jit(solution)/shard_map/ppermute | solution.py:404
  58.8 2.2 %all-to-all-done.1.p_ref = bf16[32,32,128]{2,1,0:T(8,128)(2,1)S(1)} async-done(((bf16[32,32,128]{2,1,0:T(8,128)(2,1)}), bf16[32,32,128]{2,1,0:T(8,128)(2,1)S(1)}, u32[]{:S(2)}, u32[]{:S(2)}) %all-to-all-start.1) | async-done | bytes 262176 | tf_op jit(solution)/shard_map/all_to_all | solution.py:397
  61.1 1.0 %to_cells.1 = bf16[256,1024]{1,0:T(8,128)(2,1)} custom-call(bf16[256,128]{1,0:T(8,128)(2,1)S(1)} %copy-done.1, bf16[32,32,128]{2,1,0:T(8,128)(2,1)S(1)} %all-to-all-done.1.p_ref, bf16[256,1024]{1,0:T(8,128)(2,1)S(1)} %bitcast.13), custom_call_target="tpu_custom_call" | custom-call | tf_op jit(solution)/shard_map/to_cells/pallas_call | solution.py:144
  62.1 0.0 collective-permute-done.2.refs_1_
  62.1 0.0 collective-permute-done.3.refs_2_
  62.1 0.0 collective-permute-done.4.refs_3_
  62.1 1.5 %gradient_sum.1 = (f32[128,128]{1,0:T(8,128)}, f32[128,128]{1,0:T(8,128)}, f32[8,32]{1,0:T(8,128)}) custom-call(s32[5]{0:T(128)S(1)} %pad_add_fusion.s_ref, f32[272,128]{1,0:T(8,128)S(1)} %get-tuple-element.29.refs_0_, bf16[272,128]{1,0:T(8,128)(2,1)S(1)} %collective-permute-done.2.refs_1_, bf16[272,128]{1,0:T(8,128)(2,1)S(1)} %collective-permute-done.3.refs_2_, ...), custom_call_target="tpu_custom_call" | custom-call | tf_op jit(solution)/shard_map/gradient_sum/pallas_call | solution.py:345
  (6 shorter events, 0.0 us)
Async XLA Ops:
  0.6 21.9 %copy-start = (s32[1,2,8]{2,1,0:T(2,128)S(1)}, s32[1,2,8]{2,1,0:T(2,128)}, u32[]{:S(2)}) copy-start(s32[1,2,8]{2,1,0:T(2,128)} %param.18) | copy-start | bytes 196
  2.0 4.8 %collective-permute-start.1 = (bf16[32,32,128]{2,1,0:T(8,128)(2,1)S(1)}, bf16[32,32,128]{2,1,0:T(8,128)(2,1)S(1)}, u32[]{:S(2)}, u32[]{:S(2)}) collective-permute-start(bf16[32,32,128]{2,1,0:T(8,128)(2,1)S(1)} %to_spectral.3), channel_id=1, source_target_pairs={{0,480},{32,0},{64,32},{96,64},{128,96},{160,128},{192,160},{224,1... | collective-permute-start | bytes 786440 | tf_op jit(solution)/shard_map/ppermute | solution.py:385
  7.6 13.2 %copy-start.6 = (bf16[1,2,128,1024]{3,2,1,0:T(8,128)(2,1)S(1)}, bf16[1,2,128,1024]{3,2,1,0:T(8,128)(2,1)}, u32[]{:S(2)}) copy-start(bf16[1,2,128,1024]{3,2,1,0:T(8,128)(2,1)} %param.13) | copy-start | bytes 1572868
  7.6 31.1 %all-to-all-start = ((bf16[32,64,128]{2,1,0:T(8,128)(2,1)}), bf16[32,64,128]{2,1,0:T(8,128)(2,1)S(1)}, u32[]{:S(2)}, u32[]{:S(2)}) async-start(bf16[32,64,128]{2,1,0:T(8,128)(2,1)} %pad_maximum_fusion), calls=%async_computation | async-start | bytes 1048576 | tf_op jit(solution)/shard_map/all_to_all | solution.py:389
  20.8 1.9 %copy-start.2 = (f32[1,2,2,2,1024]{4,3,2,1,0:T(2,128)S(1)}, f32[1,2,2,2,1024]{4,3,2,1,0:T(2,128)}, u32[]{:S(2)}) copy-start(f32[1,2,2,2,1024]{4,3,2,1,0:T(2,128)} %b_ref.1) | copy-start | bytes 98308
  20.8 8.3 %collective-permute-start = (bf16[1,2,128,1024]{3,2,1,0:T(8,128)(2,1)S(1)}, bf16[1,2,128,1024]{3,2,1,0:T(8,128)(2,1)S(1)}, u32[]{:S(2)}, u32[]{:S(2)}) collective-permute-start(bf16[1,2,128,1024]{3,2,1,0:T(8,128)(2,1)S(1)} %copy-done.6), channel_id=1, source_target_pairs={{0,480},{32,0},{64,32},{96,64},{128,96},{160,128},{192,160},{224,1... | collective-permute-start | bytes 1572872 | tf_op jit(solution)/shard_map/ppermute | solution.py:390
  22.8 6.4 %copy-start.5 = (bf16[2,128,1024]{2,1,0:T(8,128)(2,1)S(1)}, bf16[2,128,1024]{2,1,0:T(8,128)(2,1)}, u32[]{:S(2)}) copy-start(bf16[2,128,1024]{2,1,0:T(8,128)(2,1)} %param.14) | copy-start | bytes 1572868
  24.3 14.4 %copy-start.3 = (bf16[128,128]{1,0:T(8,128)(2,1)S(1)}, bf16[128,128]{1,0:T(8,128)(2,1)}, u32[]{:S(2)}) copy-start(bf16[128,128]{1,0:T(8,128)(2,1)} %constant.53.clone.lt_ref) | copy-start | bytes 98308
  24.3 14.3 %copy-start.4 = (bf16[128,128]{1,0:T(8,128)(2,1)S(1)}, bf16[128,128]{1,0:T(8,128)(2,1)}, u32[]{:S(2)}) copy-start(bf16[128,128]{1,0:T(8,128)(2,1)} %constant.52.clone.l_ref) | copy-start | bytes 98308
  41.9 19.1 %copy-start.1 = (bf16[256,128]{1,0:T(8,128)(2,1)S(1)}, bf16[256,128]{1,0:T(8,128)(2,1)}, u32[]{:S(2)}) copy-start(bf16[256,128]{1,0:T(8,128)(2,1)} %constant.54.clone.t_ref) | copy-start | bytes 196612
  41.9 19.1 %all-to-all-start.1 = ((bf16[32,32,128]{2,1,0:T(8,128)(2,1)}), bf16[32,32,128]{2,1,0:T(8,128)(2,1)S(1)}, u32[]{:S(2)}, u32[]{:S(2)}) async-start(bf16[32,32,128]{2,1,0:T(8,128)(2,1)} %get-tuple-element.25), calls=%async_computation.1 | async-start | bytes 524288 | tf_op jit(solution)/shard_map/all_to_all | solution.py:397
  47.1 15.0 %collective-permute-start.2 = (bf16[272,128]{1,0:T(8,128)(2,1)S(1)}, bf16[272,128]{1,0:T(8,128)(2,1)S(1)}, u32[]{:S(2)}, u32[]{:S(2)}) collective-permute-start(bf16[272,128]{1,0:T(8,128)(2,1)S(1)} %get-tuple-element.30), channel_id=1, source_target_pairs={{0,1},{1,2},{2,3},{3,0},{4,5},{5,6},{6,7},{7,4},{8,9},{9,10},{10,1... | collective-permute-start | bytes 208904 | tf_op jit(solution)/shard_map/ppermute | solution.py:404
  50.8 11.3 %collective-permute-start.3 = (bf16[272,128]{1,0:T(8,128)(2,1)S(1)}, bf16[272,128]{1,0:T(8,128)(2,1)S(1)}, u32[]{:S(2)}, u32[]{:S(2)}) collective-permute-start(bf16[272,128]{1,0:T(8,128)(2,1)S(1)} %get-tuple-element.31), channel_id=1, source_target_pairs={{0,2},{1,3},{2,0},{3,1},{4,6},{5,7},{6,4},{7,5},{8,10},{9,11},{10,... | collective-permute-start | bytes 208904 | tf_op jit(solution)/shard_map/ppermute | solution.py:404
  55.4 6.7 %collective-permute-start.4 = (bf16[272,128]{1,0:T(8,128)(2,1)S(1)}, bf16[272,128]{1,0:T(8,128)(2,1)S(1)}, u32[]{:S(2)}, u32[]{:S(2)}) collective-permute-start(bf16[272,128]{1,0:T(8,128)(2,1)S(1)} %get-tuple-element.32), channel_id=1, source_target_pairs={{0,3},{1,0},{2,1},{3,2},{4,7},{5,4},{6,5},{7,6},{8,11},{9,8},{10,9... | collective-permute-start | bytes 208904 | tf_op jit(solution)/shard_map/ppermute | solution.py:404

commit v5 on v4

--- a/solution.py
+++ b/solution.py
@@ -205,8 +205,7 @@
     own = width // quarters
     count = 4 * LAYERS * own + 16
 
-    def body(s_ref, parts_ref, l_ref, lt_ref, w_ref, b_ref, da_ref, *rest):
-        mine_and_sent, tmp, all_ref = (rest[:quarters], rest[quarters], rest[quarters + 1])
+    def body(s_ref, parts_ref, l_ref, lt_ref, w_ref, b_ref, da_ref, send_ref, tmp, all_ref):
         quarter = s_ref[2]
         mix, mix_t = (l_ref[...], lt_ref[...])
 
@@ -286,43 +285,40 @@
             part = jnp.concatenate([part[:, :width], part[:, width:]], axis=0)
             tmp[0, pl.ds(k, 2 * lat, stride=per), :] = dot(mix_t, part)
         da_ref[...] = tmp[0].astype(BF16).reshape(chunk)
-        for step, o_ref in enumerate(mine_and_sent):
-            start = pl.multiple_of((quarter + step) % quarters * own, own)
-            for square in range(4 * LAYERS):
-                part = all_ref[square, pl.ds(start, own), :]
-                o_ref[square * own : (square + 1) * own] = part.astype(o_ref.dtype)
-            o_ref[4 * LAYERS * own :] = sums.astype(o_ref.dtype)
+        for square in range(4 * LAYERS):
+            part = all_ref[square].astype(BF16)
+            for q in range(quarters):
+                send_ref[q, square * own : (square + 1) * own] = part[q * own : (q + 1) * own]
+        for q in range(quarters):
+            send_ref[q, 4 * LAYERS * own :] = sums.astype(BF16)
 
     return pl.pallas_call(
         body,
         in_specs=[SMEM] + [VMEM] * 5,
-        out_specs=[VMEM] * (1 + quarters),
+        out_specs=[VMEM] * 2,
         scratch_shapes=[
             pltpu.VMEM((2, 2 * lat * per, width), F32),
             pltpu.VMEM((4 * LAYERS, width, width), F32),
         ],
         out_shape=[
             jax.ShapeDtypeStruct(chunk, BF16),
-            jax.ShapeDtypeStruct((count, width), F32),
-        ]
-        + [jax.ShapeDtypeStruct((count, width), BF16)] * (quarters - 1),
+            jax.ShapeDtypeStruct((quarters, count, width), BF16),
+        ],
         compiler_params=params(),
         name="spectral_chain",
     )(scalars, parts, mixer, mixer_t, weights, biases)
 
 
 def gradient_sum(scalars, parts, width):
-    quarters = len(parts)
+    quarters = parts.shape[0]
     own = width // quarters
     half = 2 * LAYERS * own
 
-    def body(s_ref, *refs):
-        first_hbm, second_hbm, bias_hbm, buf, bias_buf, sem = refs[quarters:]
-
+    def body(s_ref, p_ref, first_hbm, second_hbm, bias_hbm, buf, bias_buf, sem):
         def added(start, size):
-            total = refs[0][start : start + size]
-            for ref in refs[1:quarters]:
-                total = total + ref[start : start + size].astype(F32)
+            total = p_ref[0, start : start + size].astype(F32)
+            for q in range(1, quarters):
+                total = total + p_ref[q, start : start + size].astype(F32)
             return total
 
         copies = [
@@ -344,7 +340,7 @@
 
     return pl.pallas_call(
         body,
-        in_specs=[SMEM] + [VMEM] * quarters,
+        in_specs=[SMEM, VMEM],
         out_specs=[HBM] * 3,
         scratch_shapes=[
             pltpu.VMEM((2, half, width), F32),
@@ -358,7 +354,7 @@
         ],
         compiler_params=params(),
         name="gradient_sum",
-    )(scalars, *parts)
+    )(scalars, parts)
 
 
 def on_device(section_input, handoff, loss_grad, w_first, w_second, bias, kept):
@@ -391,19 +387,19 @@
     cot = jnp.where(section == sections - 1, loss_grad, received[0]).reshape(cells)
     weights, biases = block_params(scalars, w_first, w_second, bias, width)
     cot, both = lax.optimization_barrier((cot, both))
-    da, *parts = spectral_chain(
+    da, parts = spectral_chain(
         scalars, both, mixer, mixer.T.copy(), weights, biases, lat, width, quarters
     )
     da = lax.all_to_all(da, "lat", split_axis=0, concat_axis=0, tiled=True)
-    for step in range(1, quarters):
-        pairs = [
-            (b * quarters + q, b * quarters + (q + step) % quarters)
-            for b in range(blocks)
-            for q in range(quarters)
-        ]
-        parts[step] = lax.ppermute(parts[step], "lat", pairs)
+    groups = [[b * quarters + q for q in range(quarters)] for b in range(blocks)]
+
+    def exchanged(value):
+        return lax.all_to_all(
+            value, "lat", split_axis=0, concat_axis=0, tiled=True, axis_index_groups=groups
+        )
+
+    parts = lax.cond(jnp.max(limits) > 0, exchanged, jnp.zeros_like, parts)
     handed = to_cells(da, forward.T.copy(), cot, quarters, width)
-    handed, parts[0] = lax.optimization_barrier((handed, parts[0]))
     first, second, biases = gradient_sum(scalars, parts, width)
     own = width // quarters
     return (

time: 64.2 us -> 72.2 us (1.12)
  starting transfers between devices: 32.5 us -> 19.5 us
  blocking collectives: 0 us -> 11.6 us
  waiting for transfers between devices: 19.2 us -> 26.9 us
    ppermute x3 -> x0, starting transfers between devices: 11.7 us -> none  [on_device(): parts[step] = lax.ppermute(parts[step], 'lat', pairs)]
    all_to_all x0 -> x1, blocking collectives: none -> 11.6 us  [exchanged(): lax.all_to_all(value, 'lat', split_axis=0, concat_axis=0, tiled=True, axi...]
    all_to_all x1, waiting for transfers between devices: 2.24 us -> 11.9 us  [on_device(): da = lax.all_to_all(da, 'lat', split_axis=0, concat_axis=0, tiled=True)]
    ppermute x1, waiting for transfers between devices: 4.82 us -> 2.96 us  [on_device(): received = lax.ppermute(later, 'section', ring)]
    all_to_all x1, starting transfers between devices: 5.18 us -> 3.87 us  [on_device(): da = lax.all_to_all(da, 'lat', split_axis=0, concat_axis=0, tiled=True)]
  transfers between devices with their start and end apart: 7 -> 4, of which waited for: 4 -> 4; matrix products, arithmetic and copies ran while one was open for 1% -> 1% of each run, Pallas kernels for 6% -> 6%
where the time goes in v5:
time: 72.2 us; the launch traced here: 71.8 us
  waiting for transfers between devices  26.9 us (37%)
  starting transfers between devices  19.5 us (27%)
  blocking collectives  11.6 us (16%)
  Pallas kernels  9.94 us (14%)
  other arithmetic  1.71 us (2%)
  between operations  1.39 us (2%)
    all_to_all x1, starting transfers between devices, on_device(): both = lax.all_to_all(both, 'lat', split_axis=0, concat_axis=0, tiled=True)  13.2 us
    all_to_all x1, waiting for transfers between devices, on_device(): da = lax.all_to_all(da, 'lat', split_axis=0, concat_axis=0, tiled=True)  11.9 us
    all_to_all x1, blocking collectives, exchanged(): lax.all_to_all(value, 'lat', split_axis=0, concat_axis=0, tiled=True, axi...  11.6 us
    all_to_all x1, waiting for transfers between devices, on_device(): both = lax.all_to_all(both, 'lat', split_axis=0, concat_axis=0, tiled=True)  9.44 us
    all_to_all x1, starting transfers between devices, on_device(): da = lax.all_to_all(da, 'lat', split_axis=0, concat_axis=0, tiled=True)  3.87 us
    pallas_call x1, Pallas kernels, spectral_chain(): pl.pallas_call(body, in_specs=[SMEM] + [VMEM] * 5, out_specs=[VMEM] * 2,...  3.22 us
    ppermute x1, waiting for transfers between devices, on_device(): received = lax.ppermute(later, 'section', ring)  2.96 us
    ppermute x1, waiting for transfers between devices, on_device(): du = lax.ppermute(du, 'section', ring)  2.65 us
  transfers between devices with their start and end apart: 4, of which 4 were waited for; matrix products, arithmetic and copies ran while one was open for 1% of the time, Pallas kernels for 6%

profile of v5, /device:TPU:56, one launch (start us, length us, event | category | flops | bytes accessed | tf_op | source)
XLA Modules:
  0.0 71.8 jit_solution(13542166406616070814)
XLA Ops:
  0.6 1.3 %to_spectral.3 = bf16[32,32,128]{2,1,0:T(8,128)(2,1)S(1)} custom-call(s32[1]{0:T(128)} %bitcast.s_ref, bf16[128,256]{1,0:T(8,128)(2,1)} %constant.54.clone.t_hbm, bf16[256,1024]{1,0:T(8,128)(2,1)} %bitcast.15, bf16[256,1024]{1,0:T(8,128)(2,1)} %bitcast.14), custom_call_target="tpu_custom_call" | custom-call | tf_op jit(solution)/shard_map/to_spectral/pallas_call | solution.py:105
  1.9 0.8 %collective-permute-start.1 = (bf16[32,32,128]{2,1,0:T(8,128)(2,1)S(1)}, bf16[32,32,128]{2,1,0:T(8,128)(2,1)S(1)}, u32[]{:S(2)}, u32[]{:S(2)}) collective-permute-start(bf16[32,32,128]{2,1,0:T(8,128)(2,1)S(1)} %to_spectral.3), channel_id=1, source_target_pairs={{0,480},{32,0},{64,32},{96,64},{128,96},{160,128},{192,160},{224,1... | collective-permute-start | bytes 786440 | tf_op jit(solution)/shard_map/ppermute | solution.py:381
  2.7 1.3 %to_spectral.2 = bf16[32,32,128]{2,1,0:T(8,128)(2,1)S(1)} custom-call(s32[1]{0:T(128)} %bitcast.s_ref, bf16[128,256]{1,0:T(8,128)(2,1)} %constant.55.clone.t_hbm, bf16[256,1024]{1,0:T(8,128)(2,1)} %bitcast.16), custom_call_target="tpu_custom_call" | custom-call | tf_op jit(solution)/shard_map/to_spectral/pallas_call | solution.py:105
  4.1 2.6 %collective-permute-done.1 = bf16[32,32,128]{2,1,0:T(8,128)(2,1)S(1)} collective-permute-done((bf16[32,32,128]{2,1,0:T(8,128)(2,1)S(1)}, bf16[32,32,128]{2,1,0:T(8,128)(2,1)S(1)}, u32[]{:S(2)}, u32[]{:S(2)}) %collective-permute-start.1) | collective-permute-done | bytes 262176 | tf_op jit(solution)/shard_map/ppermute | solution.py:381
  6.7 0.9 %pad_maximum_fusion = bf16[32,64,128]{2,1,0:T(8,128)(2,1)} fusion(bf16[32,32,128]{2,1,0:T(8,128)(2,1)S(1)} %collective-permute-done.1, bf16[32,32,128]{2,1,0:T(8,128)(2,1)S(1)} %to_spectral.2), kind=kLoop, calls=%fused_computation | loop fusion | flops 1048576 | bytes 1048576 | tf_op jit(solution)/shard_map/concatenate | solution.py:384
  7.6 0.0 copy-start.5
  7.6 13.2 %all-to-all-start.1 = ((bf16[32,64,128]{2,1,0:T(8,128)(2,1)}), bf16[32,64,128]{2,1,0:T(8,128)(2,1)S(1)}, u32[]{:S(2)}, u32[]{:S(2)}) async-start(bf16[32,64,128]{2,1,0:T(8,128)(2,1)} %pad_maximum_fusion), calls=%async_computation.1 | async-start | bytes 1048576 | tf_op jit(solution)/shard_map/all_to_all | solution.py:385
  20.8 0.0 copy-done.5
  20.8 1.6 %collective-permute-start = (bf16[1,2,128,1024]{3,2,1,0:T(8,128)(2,1)S(1)}, bf16[1,2,128,1024]{3,2,1,0:T(8,128)(2,1)S(1)}, u32[]{:S(2)}, u32[]{:S(2)}) collective-permute-start(bf16[1,2,128,1024]{3,2,1,0:T(8,128)(2,1)S(1)} %copy-done.5), channel_id=1, source_target_pairs={{0,480},{32,0},{64,32},{96,64},{128,96},{160,128},{192,160},{224,1... | collective-permute-start | bytes 1572872 | tf_op jit(solution)/shard_map/ppermute | solution.py:386
  22.5 0.0 copy-start.1
  22.5 0.7 copy-done.6
  23.1 0.7 dynamic-slice_reduce_fusion
  24.5 0.1 pad_add_fusion.s_ref
  24.6 0.0 copy-done.1
  24.6 1.6 %block_params.1 = (bf16[4,256,256]{2,1,0:T(8,128)(2,1)S(1)}, f32[4,1,256]{2,1,0:T(1,128)S(1)}) custom-call(s32[5]{0:T(128)S(1)} %pad_add_fusion.s_ref, bf16[1,2,2,1024,128]{4,3,2,1,0:T(8,128)(2,1)} %w1_hbm.1, bf16[1,2,2,1024,128]{4,3,2,1,0:T(8,128)(2,1)} %w2_hbm.1, f32[1,2,2,2,1024]{4,3,2,1,0:T(2,128)S(1)} %copy-done.1), custom_call_target="tpu_custom_call" | custom-call | tf_op jit(solution)/shard_map/block_params/pallas_call | solution.py:182
  26.2 0.0 copy-start.2
  26.2 0.0 copy-start.3
  26.2 3.0 %collective-permute-done = bf16[1,2,128,1024]{3,2,1,0:T(8,128)(2,1)S(1)} collective-permute-done((bf16[1,2,128,1024]{3,2,1,0:T(8,128)(2,1)S(1)}, bf16[1,2,128,1024]{3,2,1,0:T(8,128)(2,1)S(1)}, u32[]{:S(2)}, u32[]{:S(2)}) %collective-permute-start) | collective-permute-done | bytes 524320 | tf_op jit(solution)/shard_map/ppermute | solution.py:386
  29.2 0.0 copy-done.4
  29.2 0.1 bitcast_select_fusion
  29.2 9.4 %all-to-all-done.1.parts_ref = bf16[32,64,128]{2,1,0:T(8,128)(2,1)S(1)} async-done(((bf16[32,64,128]{2,1,0:T(8,128)(2,1)}), bf16[32,64,128]{2,1,0:T(8,128)(2,1)S(1)}, u32[]{:S(2)}, u32[]{:S(2)}) %all-to-all-start.1) | async-done | bytes 524320 | tf_op jit(solution)/shard_map/all_to_all | solution.py:385
  38.7 0.0 copy-done.2
  38.7 0.0 copy-done.3
  38.7 3.2 %spectral_chain.1 = (bf16[32,32,128]{2,1,0:T(8,128)(2,1)}, bf16[4,272,128]{2,1,0:T(8,128)(2,1)S(1)}) custom-call(s32[5]{0:T(128)S(1)} %pad_add_fusion.s_ref, bf16[32,64,128]{2,1,0:T(8,128)(2,1)S(1)} %all-to-all-done.1.parts_ref, bf16[128,128]{1,0:T(8,128)(2,1)S(1)} %copy-done.3, bf16[128,128]{1,0:T(8,128)(2,1)S(1)} %copy-done.2, ...), custom_call_target="tpu_custom_call" | custom-call | tf_op jit(solution)/shard_map/spectral_chain/pallas_call | solution.py:295
  41.9 11.6 %conditional.1 = (bf16[4,272,128]{2,1,0:T(8,128)(2,1)S(1)}) conditional(s32[]{:T(128)} %convert_element_type.3, () %tuple.18, bf16[4,272,128]{2,1,0:T(8,128)(2,1)S(1)} %get-tuple-element.26), branch_computations={%region_1.2_spmd, %region_2.3_spmd} | conditional | bytes 557064 | solution.py:401
  41.9 11.6 %all_to_all.14 = bf16[4,272,128]{2,1,0:T(8,128)(2,1)S(1)} all-to-all(bf16[4,272,128]{2,1,0:T(8,128)(2,1)S(1)} %param.1), channel_id=1, replica_groups={{0,1,2,3},{4,5,6,7},{8,9,10,11},{12,13,14,15},{16,17,18,19},{20,21,22,2..., dimensions={0} | all-to-all | bytes 557056 | tf_op jit(solution)/shard_map/cond/branch_1_fun/all_to_all | solution.py:397
  53.5 3.9 %all-to-all-start.2 = ((bf16[32,32,128]{2,1,0:T(8,128)(2,1)}), bf16[32,32,128]{2,1,0:T(8,128)(2,1)S(1)}, u32[]{:S(2)}, u32[]{:S(2)}) async-start(bf16[32,32,128]{2,1,0:T(8,128)(2,1)} %get-tuple-element.24), calls=%async_computation.2 | async-start | bytes 524288 | tf_op jit(solution)/shard_map/all_to_all | solution.py:393
  57.3 0.0 copy-start
  57.4 1.5 %gradient_sum.1 = (f32[128,128]{1,0:T(8,128)}, f32[128,128]{1,0:T(8,128)}, f32[8,32]{1,0:T(8,128)}) custom-call(s32[5]{0:T(128)S(1)} %pad_add_fusion.s_ref, bf16[4,272,128]{2,1,0:T(8,128)(2,1)S(1)} %get-tuple-element.32.p_ref), custom_call_target="tpu_custom_call" | custom-call | tf_op jit(solution)/shard_map/gradient_sum/pallas_call | solution.py:341
  58.9 11.9 %all-to-all-done.2.p_ref = bf16[32,32,128]{2,1,0:T(8,128)(2,1)S(1)} async-done(((bf16[32,32,128]{2,1,0:T(8,128)(2,1)}), bf16[32,32,128]{2,1,0:T(8,128)(2,1)S(1)}, u32[]{:S(2)}, u32[]{:S(2)}) %all-to-all-start.2) | async-done | bytes 262176 | tf_op jit(solution)/shard_map/all_to_all | solution.py:393
  70.7 0.0 copy-done
  70.7 1.0 %to_cells.1 = bf16[256,1024]{1,0:T(8,128)(2,1)} custom-call(bf16[256,128]{1,0:T(8,128)(2,1)S(1)} %copy-done, bf16[32,32,128]{2,1,0:T(8,128)(2,1)S(1)} %all-to-all-done.2.p_ref, bf16[256,1024]{1,0:T(8,128)(2,1)S(1)} %bitcast.13), custom_call_target="tpu_custom_call" | custom-call | tf_op jit(solution)/shard_map/to_cells/pallas_call | solution.py:144
  (2 shorter events, 0.0 us)
Async XLA Ops:
  1.9 4.8 %collective-permute-start.1 = (bf16[32,32,128]{2,1,0:T(8,128)(2,1)S(1)}, bf16[32,32,128]{2,1,0:T(8,128)(2,1)S(1)}, u32[]{:S(2)}, u32[]{:S(2)}) collective-permute-start(bf16[32,32,128]{2,1,0:T(8,128)(2,1)S(1)} %to_spectral.3), channel_id=1, source_target_pairs={{0,480},{32,0},{64,32},{96,64},{128,96},{160,128},{192,160},{224,1... | collective-permute-start | bytes 786440 | tf_op jit(solution)/shard_map/ppermute | solution.py:381
  7.6 13.2 %copy-start.5 = (bf16[1,2,128,1024]{3,2,1,0:T(8,128)(2,1)S(1)}, bf16[1,2,128,1024]{3,2,1,0:T(8,128)(2,1)}, u32[]{:S(2)}) copy-start(bf16[1,2,128,1024]{3,2,1,0:T(8,128)(2,1)} %param.15) | copy-start | bytes 1572868
  7.6 31.1 %all-to-all-start.1 = ((bf16[32,64,128]{2,1,0:T(8,128)(2,1)}), bf16[32,64,128]{2,1,0:T(8,128)(2,1)S(1)}, u32[]{:S(2)}, u32[]{:S(2)}) async-start(bf16[32,64,128]{2,1,0:T(8,128)(2,1)} %pad_maximum_fusion), calls=%async_computation.1 | async-start | bytes 1048576 | tf_op jit(solution)/shard_map/all_to_all | solution.py:385
  20.8 8.3 %collective-permute-start = (bf16[1,2,128,1024]{3,2,1,0:T(8,128)(2,1)S(1)}, bf16[1,2,128,1024]{3,2,1,0:T(8,128)(2,1)S(1)}, u32[]{:S(2)}, u32[]{:S(2)}) collective-permute-start(bf16[1,2,128,1024]{3,2,1,0:T(8,128)(2,1)S(1)} %copy-done.5), channel_id=1, source_target_pairs={{0,480},{32,0},{64,32},{96,64},{128,96},{160,128},{192,160},{224,1... | collective-permute-start | bytes 1572872 | tf_op jit(solution)/shard_map/ppermute | solution.py:386
  22.5 2.1 %copy-start.1 = (f32[1,2,2,2,1024]{4,3,2,1,0:T(2,128)S(1)}, f32[1,2,2,2,1024]{4,3,2,1,0:T(2,128)}, u32[]{:S(2)}) copy-start(f32[1,2,2,2,1024]{4,3,2,1,0:T(2,128)} %b_ref.1) | copy-start | bytes 98308
  22.5 0.7 copy-start.6
  24.6 4.6 %copy-start.4 = (bf16[2,128,1024]{2,1,0:T(8,128)(2,1)S(1)}, bf16[2,128,1024]{2,1,0:T(8,128)(2,1)}, u32[]{:S(2)}) copy-start(bf16[2,128,1024]{2,1,0:T(8,128)(2,1)} %param.16) | copy-start | bytes 1572868
  26.2 12.5 %copy-start.2 = (bf16[128,128]{1,0:T(8,128)(2,1)S(1)}, bf16[128,128]{1,0:T(8,128)(2,1)}, u32[]{:S(2)}) copy-start(bf16[128,128]{1,0:T(8,128)(2,1)} %constant.57.clone.lt_ref) | copy-start | bytes 98308
  26.2 12.5 %copy-start.3 = (bf16[128,128]{1,0:T(8,128)(2,1)S(1)}, bf16[128,128]{1,0:T(8,128)(2,1)}, u32[]{:S(2)}) copy-start(bf16[128,128]{1,0:T(8,128)(2,1)} %constant.56.clone.l_ref) | copy-start | bytes 98308
  53.5 17.3 %all-to-all-start.2 = ((bf16[32,32,128]{2,1,0:T(8,128)(2,1)}), bf16[32,32,128]{2,1,0:T(8,128)(2,1)S(1)}, u32[]{:S(2)}, u32[]{:S(2)}) async-start(bf16[32,32,128]{2,1,0:T(8,128)(2,1)} %get-tuple-element.24), calls=%async_computation.2 | async-start | bytes 524288 | tf_op jit(solution)/shard_map/all_to_all | solution.py:393
  57.3 13.4 %copy-start = (bf16[256,128]{1,0:T(8,128)(2,1)S(1)}, bf16[256,128]{1,0:T(8,128)(2,1)}, u32[]{:S(2)}) copy-start(bf16[256,128]{1,0:T(8,128)(2,1)} %constant.58.clone.t_ref) | copy-start | bytes 196612

commit v6 on v3

--- a/solution.py
+++ b/solution.py
@@ -196,18 +196,17 @@
     )(scalars, in_hbm(w_first), in_hbm(w_second), bias)
 
 
-def spectral_chain(scalars, parts, mixer, mixer_t, weights, biases, lat, width, quarters):
+def spectral_chain(scalars, parts, mixer, weights, biases, lat, width, quarters):
     sources, both, _ = parts.shape
-    chunk = (sources, both // 2, width)
     per = sources * (both // 2) // (2 * lat)
     tall = per * lat
 
     own = width // quarters
     count = 4 * LAYERS * own + 16
 
-    def body(s_ref, parts_ref, l_ref, lt_ref, w_ref, b_ref, da_ref, mine_ref, send_ref, tmp, all_ref):
+    def body(s_ref, parts_ref, l_ref, w_ref, b_ref, dz_ref, mine_ref, send_ref, tmp, all_ref):
         quarter = s_ref[2]
-        mix, mix_t = (l_ref[...], lt_ref[...])
+        mix = l_ref[...]
 
         def mixed(slot):
             part = parts_ref[:, slot * (both // 2) : (slot + 1) * (both // 2), :]
@@ -279,12 +278,7 @@
             if layer:
                 grad = grad + through_grid(dz.astype(BF16))
             total = dz if total is None else total + dz
-        total = total.astype(BF16)
-        for k in range(per):
-            part = total[k * lat : (k + 1) * lat]
-            part = jnp.concatenate([part[:, :width], part[:, width:]], axis=0)
-            tmp[0, pl.ds(k, 2 * lat, stride=per), :] = dot(mix_t, part)
-        da_ref[...] = tmp[0].astype(BF16).reshape(chunk)
+        dz_ref[...] = total.astype(BF16)
         targets = (quarter, quarter ^ 2, quarter ^ 1, quarter ^ 3)
         for slot, target in enumerate(targets):
             o_ref = (mine_ref, send_ref)[slot // 2].at[slot % 2]
@@ -296,46 +290,87 @@
 
     return pl.pallas_call(
         body,
-        in_specs=[SMEM] + [VMEM] * 5,
+        in_specs=[SMEM] + [VMEM] * 4,
         out_specs=[VMEM] * 3,
         scratch_shapes=[
             pltpu.VMEM((2, 2 * lat * per, width), F32),
             pltpu.VMEM((4 * LAYERS, width, width), F32),
         ],
         out_shape=[
-            jax.ShapeDtypeStruct(chunk, BF16),
+            jax.ShapeDtypeStruct((tall, 2 * width), BF16),
             jax.ShapeDtypeStruct((2, count, width), F32),
             jax.ShapeDtypeStruct((2, count, width), BF16),
         ],
         compiler_params=params(),
         name="spectral_chain",
-    )(scalars, parts, mixer, mixer_t, weights, biases)
+    )(scalars, parts, mixer, weights, biases)
+
+
+def to_bands(dz, mixer_t, lat, width, sources):
+    per = dz.shape[0] // lat
+    chunk = (sources, 2 * lat * per // sources, width)
+
+    def body(dz_ref, lt_ref, da_ref, tmp):
+        mix_t = lt_ref[...]
+        for k in range(per):
+            part = dz_ref[k * lat : (k + 1) * lat]
+            part = jnp.concatenate([part[:, :width], part[:, width:]], axis=0)
+            tmp[pl.ds(k, 2 * lat, stride=per), :] = dot(mix_t, part)
+        da_ref[...] = tmp[...].astype(BF16).reshape(chunk)
+
+    return pl.pallas_call(
+        body,
+        in_specs=[VMEM, VMEM],
+        out_specs=VMEM,
+        scratch_shapes=[pltpu.VMEM((2 * lat * per, width), F32)],
+        out_shape=jax.ShapeDtypeStruct(chunk, BF16),
+        compiler_params=params(),
+        name="to_bands",
+    )(dz, mixer_t)
 
 
 def gradient_sum(scalars, mine, near, far, width, quarters):
     own = width // quarters
     half = 2 * LAYERS * own
 
-    def body(s_ref, mine_ref, near_ref, far_ref, first_ref, second_ref, bias_ref):
-        total = mine_ref[0] + near_ref[0].astype(F32) + far_ref[...].astype(F32)
-        first_ref[...] = total[:half]
-        second_ref[...] = total[half : 2 * half]
-        sums = total[2 * half : 2 * half + 8]
+    def body(s_ref, m_ref, n_ref, f_ref, first_hbm, second_hbm, bias_hbm, buf, bias_buf, sem):
+        def added(start, size):
+            part = slice(start, start + size)
+            return m_ref[0, part] + n_ref[0, part].astype(F32) + f_ref[part].astype(F32)
+
+        copies = [
+            pltpu.make_async_copy(bias_buf, bias_hbm, sem.at[2]),
+            pltpu.make_async_copy(buf.at[0], first_hbm, sem.at[0]),
+            pltpu.make_async_copy(buf.at[1], second_hbm, sem.at[1]),
+        ]
+        sums = added(2 * half, 16)[:8]
         part = sums[:, :own]
         for q in range(1, quarters):
             part = jnp.where(s_ref[2] == q, sums[:, q * own : (q + 1) * own], part)
-        bias_ref[...] = part
-
-    return pl.pallas_call(
-        body,
-        in_specs=[SMEM, VMEM, VMEM, VMEM],
-        out_specs=[VMEM, VMEM, VMEM],
+        bias_buf[...] = part
+        copies[0].start()
+        for which in range(2):
+            buf[which] = added(which * half, half)
+            copies[1 + which].start()
+        for copy in copies:
+            copy.wait()
+
+    return pl.pallas_call(
+        body,
+        in_specs=[SMEM] + [VMEM] * 3,
+        out_specs=[HBM] * 3,
+        scratch_shapes=[
+            pltpu.VMEM((2, half, width), F32),
+            pltpu.VMEM((8, own), F32),
+            pltpu.SemaphoreType.DMA((3,)),
+        ],
         out_shape=[
             jax.ShapeDtypeStruct((half, width), F32),
             jax.ShapeDtypeStruct((half, width), F32),
             jax.ShapeDtypeStruct((8, own), F32),
         ],
         compiler_params=params(),
+        cost_estimate=pl.CostEstimate(flops=2 * 10**9, transcendentals=0, bytes_accessed=1 << 20),
         name="gradient_sum",
     )(scalars, mine, near, far)
 
@@ -370,14 +405,15 @@
     cot = jnp.where(section == sections - 1, loss_grad, received[0]).reshape(cells)
     weights, biases = block_params(scalars, w_first, w_second, bias, width)
     cot, both = lax.optimization_barrier((cot, both))
-    da, mine, send = spectral_chain(
-        scalars, both, mixer, mixer.T.copy(), weights, biases, lat, width, quarters
+    dz, mine, send = spectral_chain(
+        scalars, both, mixer, weights, biases, lat, width, quarters
     )
 
     def swapped(value, bit):
         return lax.ppermute(value, "lat", [(d, d ^ bit) for d in range(lat_count)])
 
     near = swapped(send, 1)
+    da = to_bands(dz, mixer.T.copy(), lat, width, lat_count)
     da = lax.all_to_all(da, "lat", split_axis=0, concat_axis=0, tiled=True)
     far = swapped((mine[1] + near[1].astype(F32)).astype(BF16), 2)
     first, second, biases = gradient_sum(scalars, mine, near, far, width, quarters)

time: 67.8 us -> 64.6 us (0.953)
  waiting for transfers between devices: 25.4 us -> 22.8 us
    ppermute x2, waiting for transfers between devices: 8.48 us -> 2.98 us  [swapped(): return lax.ppermute(value, 'lat', [(d, d ^ bit) for d in range(lat_count)])]
    all_to_all x1, waiting for transfers between devices: 0.01 us -> 2.87 us  [on_device(): da = lax.all_to_all(da, 'lat', split_axis=0, concat_axis=0, tiled=True)]
    ppermute x2, starting transfers between devices: 9.05 us -> 8.18 us  [swapped(): return lax.ppermute(value, 'lat', [(d, d ^ bit) for d in range(lat_count)])]
    pallas_call x2 -> x3, Pallas kernels: 4.65 us -> 4.86 us  [the longest x1 2.4 us: spectral_chain(): pl.pallas_call(body, in_specs=[SMEM] + [VMEM] * 4, out_specs=[VMEM] * 3,...]
  transfers between devices with their start and end apart: 6 -> 6, of which waited for: 5 -> 5; matrix products, arithmetic and copies ran while one was open for 1% -> 1% of each run, Pallas kernels for 6% -> 8%
where the time goes in v6:
time: 64.6 us; the launch traced here: 64.1 us
  starting transfers between devices  29.2 us (45%)
  waiting for transfers between devices  22.8 us (35%)
  Pallas kernels  10.1 us (16%)
  other arithmetic  1.03 us (2%)
  between operations  0.78 us (1%)
    all_to_all x1, starting transfers between devices, on_device(): both = lax.all_to_all(both, 'lat', split_axis=0, concat_axis=0, tiled=True)  13.2 us
    all_to_all x1, waiting for transfers between devices, on_device(): both = lax.all_to_all(both, 'lat', split_axis=0, concat_axis=0, tiled=True)  9.43 us
    ppermute x2, starting transfers between devices, swapped(): return lax.ppermute(value, 'lat', [(d, d ^ bit) for d in range(lat_count)])  8.18 us
    all_to_all x1, starting transfers between devices, on_device(): da = lax.all_to_all(da, 'lat', split_axis=0, concat_axis=0, tiled=True)  5.39 us
    ppermute x1, waiting for transfers between devices, on_device(): received = lax.ppermute(later, 'section', ring)  4.84 us
    ppermute x2, waiting for transfers between devices, swapped(): return lax.ppermute(value, 'lat', [(d, d ^ bit) for d in range(lat_count)])  2.98 us
    all_to_all x1, waiting for transfers between devices, on_device(): da = lax.all_to_all(da, 'lat', split_axis=0, concat_axis=0, tiled=True)  2.87 us
    ppermute x1, waiting for transfers between devices, on_device(): du = lax.ppermute(du, 'section', ring)  2.65 us
  transfers between devices with their start and end apart: 6, of which 5 were waited for; matrix products, arithmetic and copies ran while one was open for 1% of the time, Pallas kernels for 8%

profile of v6, /device:TPU:56, one launch (start us, length us, event | category | flops | bytes accessed | tf_op | source)
XLA Modules:
  0.0 64.1 jit_solution(1225535010417465040)
XLA Ops:
  0.6 0.0 copy-start
  0.7 1.3 %to_spectral.3 = bf16[32,32,128]{2,1,0:T(8,128)(2,1)S(1)} custom-call(s32[1]{0:T(128)} %bitcast.s_ref, bf16[128,256]{1,0:T(8,128)(2,1)} %constant.50.clone.t_hbm, bf16[256,1024]{1,0:T(8,128)(2,1)} %bitcast.17, bf16[256,1024]{1,0:T(8,128)(2,1)} %bitcast.16), custom_call_target="tpu_custom_call" | custom-call | tf_op jit(solution)/shard_map/to_spectral/pallas_call | solution.py:105
  2.0 0.8 %collective-permute-start = (bf16[32,32,128]{2,1,0:T(8,128)(2,1)S(1)}, bf16[32,32,128]{2,1,0:T(8,128)(2,1)S(1)}, u32[]{:S(2)}, u32[]{:S(2)}) collective-permute-start(bf16[32,32,128]{2,1,0:T(8,128)(2,1)S(1)} %to_spectral.3), channel_id=1, source_target_pairs={{0,480},{32,0},{64,32},{96,64},{128,96},{160,128},{192,160},{224,1... | collective-permute-start | bytes 786440 | tf_op jit(solution)/shard_map/ppermute | solution.py:399
  2.8 1.3 %to_spectral.2 = bf16[32,32,128]{2,1,0:T(8,128)(2,1)S(1)} custom-call(s32[1]{0:T(128)} %bitcast.s_ref, bf16[128,256]{1,0:T(8,128)(2,1)} %constant.51.clone.t_hbm, bf16[256,1024]{1,0:T(8,128)(2,1)} %bitcast.18), custom_call_target="tpu_custom_call" | custom-call | tf_op jit(solution)/shard_map/to_spectral/pallas_call | solution.py:105
  4.1 2.7 %collective-permute-done = bf16[32,32,128]{2,1,0:T(8,128)(2,1)S(1)} collective-permute-done((bf16[32,32,128]{2,1,0:T(8,128)(2,1)S(1)}, bf16[32,32,128]{2,1,0:T(8,128)(2,1)S(1)}, u32[]{:S(2)}, u32[]{:S(2)}) %collective-permute-start) | collective-permute-done | bytes 262176 | tf_op jit(solution)/shard_map/ppermute | solution.py:399
  6.7 0.9 %pad_maximum_fusion = bf16[32,64,128]{2,1,0:T(8,128)(2,1)} fusion(bf16[32,32,128]{2,1,0:T(8,128)(2,1)S(1)} %collective-permute-done, bf16[32,32,128]{2,1,0:T(8,128)(2,1)S(1)} %to_spectral.2), kind=kLoop, calls=%fused_computation | loop fusion | flops 1048576 | bytes 1048576 | tf_op jit(solution)/shard_map/concatenate | solution.py:401
  7.6 13.2 %all-to-all-start = ((bf16[32,64,128]{2,1,0:T(8,128)(2,1)}), bf16[32,64,128]{2,1,0:T(8,128)(2,1)S(1)}, u32[]{:S(2)}, u32[]{:S(2)}) async-start(bf16[32,64,128]{2,1,0:T(8,128)(2,1)} %pad_maximum_fusion), calls=%async_computation | async-start | bytes 1048576 | tf_op jit(solution)/shard_map/all_to_all | solution.py:403
  20.8 0.0 copy-done.6
  20.8 0.0 copy-start.2
  20.8 1.6 %collective-permute-start.1 = (bf16[1,2,128,1024]{3,2,1,0:T(8,128)(2,1)S(1)}, bf16[1,2,128,1024]{3,2,1,0:T(8,128)(2,1)S(1)}, u32[]{:S(2)}, u32[]{:S(2)}) collective-permute-start(bf16[1,2,128,1024]{3,2,1,0:T(8,128)(2,1)S(1)} %copy-done.6), channel_id=1, source_target_pairs={{0,480},{32,0},{64,32},{96,64},{128,96},{160,128},{192,160},{224,1... | collective-permute-start | bytes 1572872 | tf_op jit(solution)/shard_map/ppermute | solution.py:404
  22.5 0.0 copy-done
  22.5 0.2 dynamic-slice_reduce_fusion
  22.7 0.1 pad_add_fusion.s_ref
  22.8 0.0 copy-done.2
  22.8 1.6 %block_params.1 = (bf16[4,256,256]{2,1,0:T(8,128)(2,1)S(1)}, f32[4,1,256]{2,1,0:T(1,128)S(1)}) custom-call(s32[5]{0:T(128)S(1)} %pad_add_fusion.s_ref, bf16[1,2,2,1024,128]{4,3,2,1,0:T(8,128)(2,1)} %w1_hbm.1, bf16[1,2,2,1024,128]{4,3,2,1,0:T(8,128)(2,1)} %w2_hbm.1, f32[1,2,2,2,1024]{4,3,2,1,0:T(2,128)S(1)} %copy-done.2), custom_call_target="tpu_custom_call" | custom-call | tf_op jit(solution)/shard_map/block_params/pallas_call | solution.py:182
  24.3 0.0 copy-start.4
  24.3 4.8 %collective-permute-done.1 = bf16[1,2,128,1024]{3,2,1,0:T(8,128)(2,1)S(1)} collective-permute-done((bf16[1,2,128,1024]{3,2,1,0:T(8,128)(2,1)S(1)}, bf16[1,2,128,1024]{3,2,1,0:T(8,128)(2,1)S(1)}, u32[]{:S(2)}, u32[]{:S(2)}) %collective-permute-start.1) | collective-permute-done | bytes 524320 | tf_op jit(solution)/shard_map/ppermute | solution.py:404
  29.2 0.0 copy-done.5
  29.2 0.1 bitcast_select_fusion
  29.3 9.4 %all-to-all-done.parts_ref = bf16[32,64,128]{2,1,0:T(8,128)(2,1)S(1)} async-done(((bf16[32,64,128]{2,1,0:T(8,128)(2,1)}), bf16[32,64,128]{2,1,0:T(8,128)(2,1)S(1)}, u32[]{:S(2)}, u32[]{:S(2)}) %all-to-all-start) | async-done | bytes 524320 | tf_op jit(solution)/shard_map/all_to_all | solution.py:403
  38.7 2.4 %spectral_chain.1 = (bf16[512,256]{1,0:T(8,128)(2,1)S(1)}, f32[2,272,128]{2,1,0:T(8,128)S(1)}, bf16[2,272,128]{2,1,0:T(8,128)(2,1)S(1)}) custom-call(s32[5]{0:T(128)S(1)} %pad_add_fusion.s_ref, bf16[32,64,128]{2,1,0:T(8,128)(2,1)S(1)} %all-to-all-done.parts_ref, bf16[128,128]{1,0:T(8,128)(2,1)S(1)} %copy-done.4, ...), custom_call_target="tpu_custom_call" | custom-call | tf_op jit(solution)/shard_map/spectral_chain/pallas_call | solution.py:291
  41.1 2.8 %collective-permute-start.2 = (bf16[2,272,128]{2,1,0:T(8,128)(2,1)S(1)}, bf16[2,272,128]{2,1,0:T(8,128)(2,1)S(1)}, u32[]{:S(2)}, u32[]{:S(2)}) collective-permute-start(bf16[2,272,128]{2,1,0:T(8,128)(2,1)S(1)} %get-tuple-element.24), channel_id=1, source_target_pairs={{0,1},{1,0},{2,3},{3,2},{4,5},{5,4},{6,7},{7,6},{8,9},{9,8},{10,11... | collective-permute-start | bytes 417800 | tf_op jit(solution)/shard_map/ppermute | solution.py:413
  44.0 0.0 copy-done.3
  44.0 1.0 %to_bands.1 = bf16[32,32,128]{2,1,0:T(8,128)(2,1)} custom-call(bf16[512,256]{1,0:T(8,128)(2,1)S(1)} %get-tuple-element.21.dz_ref, bf16[128,128]{1,0:T(8,128)(2,1)S(1)} %copy-done.3), custom_call_target="tpu_custom_call" | custom-call | tf_op jit(solution)/shard_map/to_bands/pallas_call | solution.py:321
  44.9 5.4 %all-to-all-start.1 = ((bf16[32,32,128]{2,1,0:T(8,128)(2,1)}), bf16[32,32,128]{2,1,0:T(8,128)(2,1)S(1)}, u32[]{:S(2)}, u32[]{:S(2)}) async-start(bf16[32,32,128]{2,1,0:T(8,128)(2,1)} %to_bands.1), calls=%async_computation.1 | async-start | bytes 524288 | tf_op jit(solution)/shard_map/all_to_all | solution.py:417
  50.3 0.0 collective-permute-done.2.n_ref
  50.4 0.0 copy-start.1
  50.4 5.3 %collective-permute-start.3 = (bf16[272,128]{1,0:T(8,128)(2,1)S(1)}, bf16[272,128]{1,0:T(8,128)(2,1)S(1)}, u32[]{:S(2)}, u32[]{:S(2)}) collective-permute-start(bf16[272,128]{1,0:T(8,128)(2,1)S(1)} %fusion), channel_id=1, source_target_pairs={{0,2},{1,3},{2,0},{3,1},{4,6},{5,7},{6,4},{7,5},{8,10},{9,11},{10,... | collective-permute-start | bytes 208904 | tf_op jit(solution)/shard_map/ppermute | solution.py:413
  55.7 3.0 %collective-permute-done.3.f_ref = bf16[272,128]{1,0:T(8,128)(2,1)S(1)} collective-permute-done((bf16[272,128]{1,0:T(8,128)(2,1)S(1)}, bf16[272,128]{1,0:T(8,128)(2,1)S(1)}, u32[]{:S(2)}, u32[]{:S(2)}) %collective-permute-start.3) | collective-permute-done | bytes 69664 | tf_op jit(solution)/shard_map/ppermute | solution.py:413
  58.7 1.5 %gradient_sum.1 = (f32[128,128]{1,0:T(8,128)}, f32[128,128]{1,0:T(8,128)}, f32[8,32]{1,0:T(8,128)}) custom-call(s32[5]{0:T(128)S(1)} %pad_add_fusion.s_ref, f32[2,272,128]{2,1,0:T(8,128)S(1)} %get-tuple-element.23.m_ref, bf16[2,272,128]{2,1,0:T(8,128)(2,1)S(1)} %collective-permute-done.2.n_ref, bf16[272,128]{1,0:T(8,128)(2,1)S(1)} %collective-permute-done.3.f_ref), custom_call_target="tpu_custom_call" | custom-call | flops 2000000000 | bytes 1048576 | tf_op jit(solution)/shard_map/gradient_sum/pallas_call | solution.py:358
  60.2 2.9 %all-to-all-done.1.p_ref = bf16[32,32,128]{2,1,0:T(8,128)(2,1)S(1)} async-done(((bf16[32,32,128]{2,1,0:T(8,128)(2,1)}), bf16[32,32,128]{2,1,0:T(8,128)(2,1)S(1)}, u32[]{:S(2)}, u32[]{:S(2)}) %all-to-all-start.1) | async-done | bytes 262176 | tf_op jit(solution)/shard_map/all_to_all | solution.py:417
  63.1 1.0 %to_cells.1 = bf16[256,1024]{1,0:T(8,128)(2,1)} custom-call(bf16[256,128]{1,0:T(8,128)(2,1)S(1)} %copy-done.1, bf16[32,32,128]{2,1,0:T(8,128)(2,1)S(1)} %all-to-all-done.1.p_ref, bf16[256,1024]{1,0:T(8,128)(2,1)S(1)} %bitcast.15), custom_call_target="tpu_custom_call" | custom-call | tf_op jit(solution)/shard_map/to_cells/pallas_call | solution.py:144
  (6 shorter events, 0.0 us)
Async XLA Ops:
  0.6 21.9 %copy-start = (s32[1,2,8]{2,1,0:T(2,128)S(1)}, s32[1,2,8]{2,1,0:T(2,128)}, u32[]{:S(2)}) copy-start(s32[1,2,8]{2,1,0:T(2,128)} %param.18) | copy-start | bytes 196
  2.0 4.8 %collective-permute-start = (bf16[32,32,128]{2,1,0:T(8,128)(2,1)S(1)}, bf16[32,32,128]{2,1,0:T(8,128)(2,1)S(1)}, u32[]{:S(2)}, u32[]{:S(2)}) collective-permute-start(bf16[32,32,128]{2,1,0:T(8,128)(2,1)S(1)} %to_spectral.3), channel_id=1, source_target_pairs={{0,480},{32,0},{64,32},{96,64},{128,96},{160,128},{192,160},{224,1... | collective-permute-start | bytes 786440 | tf_op jit(solution)/shard_map/ppermute | solution.py:399
  7.6 13.2 %copy-start.6 = (bf16[1,2,128,1024]{3,2,1,0:T(8,128)(2,1)S(1)}, bf16[1,2,128,1024]{3,2,1,0:T(8,128)(2,1)}, u32[]{:S(2)}) copy-start(bf16[1,2,128,1024]{3,2,1,0:T(8,128)(2,1)} %param.13) | copy-start | bytes 1572868
  7.6 31.1 %all-to-all-start = ((bf16[32,64,128]{2,1,0:T(8,128)(2,1)}), bf16[32,64,128]{2,1,0:T(8,128)(2,1)S(1)}, u32[]{:S(2)}, u32[]{:S(2)}) async-start(bf16[32,64,128]{2,1,0:T(8,128)(2,1)} %pad_maximum_fusion), calls=%async_computation | async-start | bytes 1048576 | tf_op jit(solution)/shard_map/all_to_all | solution.py:403
  20.8 1.9 %copy-start.2 = (f32[1,2,2,2,1024]{4,3,2,1,0:T(2,128)S(1)}, f32[1,2,2,2,1024]{4,3,2,1,0:T(2,128)}, u32[]{:S(2)}) copy-start(f32[1,2,2,2,1024]{4,3,2,1,0:T(2,128)} %b_ref.1) | copy-start | bytes 98308
  20.8 8.3 %collective-permute-start.1 = (bf16[1,2,128,1024]{3,2,1,0:T(8,128)(2,1)S(1)}, bf16[1,2,128,1024]{3,2,1,0:T(8,128)(2,1)S(1)}, u32[]{:S(2)}, u32[]{:S(2)}) collective-permute-start(bf16[1,2,128,1024]{3,2,1,0:T(8,128)(2,1)S(1)} %copy-done.6), channel_id=1, source_target_pairs={{0,480},{32,0},{64,32},{96,64},{128,96},{160,128},{192,160},{224,1... | collective-permute-start | bytes 1572872 | tf_op jit(solution)/shard_map/ppermute | solution.py:404
  22.8 6.4 %copy-start.5 = (bf16[2,128,1024]{2,1,0:T(8,128)(2,1)S(1)}, bf16[2,128,1024]{2,1,0:T(8,128)(2,1)}, u32[]{:S(2)}) copy-start(bf16[2,128,1024]{2,1,0:T(8,128)(2,1)} %param.14) | copy-start | bytes 1572868
  24.3 14.4 %copy-start.4 = (bf16[128,128]{1,0:T(8,128)(2,1)S(1)}, bf16[128,128]{1,0:T(8,128)(2,1)}, u32[]{:S(2)}) copy-start(bf16[128,128]{1,0:T(8,128)(2,1)} %constant.52.clone.l_ref) | copy-start | bytes 98308
  38.7 5.3 %copy-start.3 = (bf16[128,128]{1,0:T(8,128)(2,1)S(1)}, bf16[128,128]{1,0:T(8,128)(2,1)}, u32[]{:S(2)}) copy-start(bf16[128,128]{1,0:T(8,128)(2,1)} %constant.53.clone.lt_ref) | copy-start | bytes 98308
  41.1 9.2 %collective-permute-start.2 = (bf16[2,272,128]{2,1,0:T(8,128)(2,1)S(1)}, bf16[2,272,128]{2,1,0:T(8,128)(2,1)S(1)}, u32[]{:S(2)}, u32[]{:S(2)}) collective-permute-start(bf16[2,272,128]{2,1,0:T(8,128)(2,1)S(1)} %get-tuple-element.24), channel_id=1, source_target_pairs={{0,1},{1,0},{2,3},{3,2},{4,5},{5,4},{6,7},{7,6},{8,9},{9,8},{10,11... | collective-permute-start | bytes 417800 | tf_op jit(solution)/shard_map/ppermute | solution.py:413
  44.9 18.1 %all-to-all-start.1 = ((bf16[32,32,128]{2,1,0:T(8,128)(2,1)}), bf16[32,32,128]{2,1,0:T(8,128)(2,1)S(1)}, u32[]{:S(2)}, u32[]{:S(2)}) async-start(bf16[32,32,128]{2,1,0:T(8,128)(2,1)} %to_bands.1), calls=%async_computation.1 | async-start | bytes 524288 | tf_op jit(solution)/shard_map/all_to_all | solution.py:417
  50.4 12.7 %copy-start.1 = (bf16[256,128]{1,0:T(8,128)(2,1)S(1)}, bf16[256,128]{1,0:T(8,128)(2,1)}, u32[]{:S(2)}) copy-start(bf16[256,128]{1,0:T(8,128)(2,1)} %constant.54.clone.t_ref) | copy-start | bytes 196612
  50.4 8.3 %collective-permute-start.3 = (bf16[272,128]{1,0:T(8,128)(2,1)S(1)}, bf16[272,128]{1,0:T(8,128)(2,1)S(1)}, u32[]{:S(2)}, u32[]{:S(2)}) collective-permute-start(bf16[272,128]{1,0:T(8,128)(2,1)S(1)} %fusion), channel_id=1, source_target_pairs={{0,2},{1,3},{2,0},{3,1},{4,6},{5,7},{6,4},{7,5},{8,10},{9,11},{10,... | collective-permute-start | bytes 208904 | tf_op jit(solution)/shard_map/ppermute | solution.py:413

commit v7 on v6

--- a/solution.py
+++ b/solution.py
@@ -64,47 +64,29 @@
     return pltpu.with_memory_space_constraint(value, pltpu.HBM)
 
 
-def to_spectral(scalars, sources, table, quarters, width):
-    cells, channels = sources[0].shape
+def to_spectral(x, table, quarters, width):
+    cells, channels = x.shape
     rows = table.shape[0] // quarters
     blocks = channels // width
     cuts = 2
     span = cells // cuts
 
-    def body(s_ref, t_hbm, *refs):
-        given = refs[: len(sources)]
-        o_ref, t_buf, x_buf, t_sem, x_sem = refs[len(sources) :]
-
-        def piece(source, cut):
+    def body(t_hbm, x_hbm, o_ref, t_buf, x_buf, t_sem, x_sem):
+        copies = [pltpu.make_async_copy(t_hbm, t_buf, t_sem)]
+        for cut in range(cuts):
             part = pl.ds(cut * span, span)
-            return pltpu.make_async_copy(source.at[part, :], x_buf.at[part, :], x_sem.at[cut])
-
-        def begin(source):
-            for cut in range(cuts):
-                piece(source, cut).start()
-
-        table_copy = pltpu.make_async_copy(t_hbm, t_buf, t_sem)
-        table_copy.start()
-        if len(given) == 1:
-            begin(given[0])
-        else:
-            pl.when(s_ref[0] != 0)(lambda: begin(given[0]))
-            pl.when(s_ref[0] == 0)(lambda: begin(given[1]))
-        table_copy.wait()
-        t = t_buf[...]
-        for cut in range(cuts):
-            piece(given[0], cut).wait()
-        step = 2 * width
-        for cut in range(channels // step):
-            y = dot(t, x_buf[:, cut * step : (cut + 1) * step]).astype(BF16)
-            for b in range(2):
-                for q in range(quarters):
-                    owner = (cut * 2 + b) * quarters + q
-                    o_ref[owner] = y[q * rows : (q + 1) * rows, b * width : (b + 1) * width]
-
-    return pl.pallas_call(
-        body,
-        in_specs=[SMEM, HBM] + [HBM] * len(sources),
+            copies.append(
+                pltpu.make_async_copy(x_hbm.at[part, :], x_buf.at[part, :], x_sem.at[cut])
+            )
+        for copy in copies:
+            copy.start()
+        for copy in copies:
+            copy.wait()
+        transform(t_buf[...], x_buf, o_ref, 0, quarters, width)
+
+    return pl.pallas_call(
+        body,
+        in_specs=[HBM, HBM],
         out_specs=VMEM,
         scratch_shapes=[
             pltpu.VMEM(table.shape, BF16),
@@ -115,7 +97,68 @@
         out_shape=jax.ShapeDtypeStruct((blocks * quarters, rows, width), BF16),
         compiler_params=params(),
         name="to_spectral",
-    )(scalars, in_hbm(jnp.asarray(table)), *[in_hbm(source) for source in sources])
+    )(in_hbm(jnp.asarray(table)), in_hbm(x))
+
+
+def transform(table, x_ref, o_ref, at, quarters, width):
+    rows = table.shape[0] // quarters
+    step = 2 * width
+    for cut in range(x_ref.shape[1] // step):
+        y = dot(table, x_ref[:, cut * step : (cut + 1) * step]).astype(BF16)
+        for b in range(2):
+            for q in range(quarters):
+                owner = (cut * 2 + b) * quarters + q
+                part = y[q * rows : (q + 1) * rows, b * width : (b + 1) * width]
+                o_ref[owner, at : at + rows] = part
+
+
+def to_spectral_joined(scalars, spec, received, loss_grad, table, quarters, width):
+    cells, channels = loss_grad.shape
+    owners, rows, _ = spec.shape
+    cuts = 2
+    span = cells // cuts
+
+    def body(s_ref, t_ref, spec_ref, received_ref, loss_hbm, o_hbm, cot_ref, buf, x_sem, o_sem):
+        def piece(source, cut):
+            part = pl.ds(cut * span, span)
+            return pltpu.make_async_copy(source.at[part, :], cot_ref.at[part, :], x_sem.at[cut])
+
+        def begin(source):
+            for cut in range(cuts):
+                piece(source, cut).start()
+
+        pl.when(s_ref[0] == 0)(lambda: begin(received_ref))
+        pl.when(s_ref[0] != 0)(lambda: begin(loss_hbm))
+        buf[:, :rows] = spec_ref[...]
+        for cut in range(cuts):
+            piece(received_ref, cut).wait()
+        copies = []
+        half = owners // 2
+        for cut in range(2):
+            lanes = pl.ds(cut * (channels // 2), channels // 2)
+            own = pl.ds(cut * half, half)
+            transform(t_ref[...], cot_ref.at[:, lanes], buf.at[own], rows, quarters, width)
+            copies.append(pltpu.make_async_copy(buf.at[own], o_hbm.at[own], o_sem.at[cut]))
+            copies[-1].start()
+        for copy in copies:
+            copy.wait()
+
+    return pl.pallas_call(
+        body,
+        in_specs=[SMEM, VMEM, VMEM, VMEM, HBM],
+        out_specs=[HBM, VMEM],
+        scratch_shapes=[
+            pltpu.VMEM((owners, 2 * rows, width), BF16),
+            pltpu.SemaphoreType.DMA((cuts,)),
+            pltpu.SemaphoreType.DMA((2,)),
+        ],
+        out_shape=[
+            jax.ShapeDtypeStruct((owners, 2 * rows, width), BF16),
+            jax.ShapeDtypeStruct((cells, channels), BF16),
+        ],
+        compiler_params=params(),
+        name="to_spectral_joined",
+    )(scalars, table, spec, received, in_hbm(loss_grad))
 
 
 def to_cells(parts, table_t, grid_add, quarters, width):
@@ -394,17 +437,14 @@
     ring = [(s, (s - 1) % sections) for s in range(sections)]
     cells = (rows * lon, channels)
 
-    handed_du = (handoff.reshape(cells), loss_grad.reshape(cells))
-    du = to_spectral(section.reshape(1), handed_du, inverse, quarters, width)
-    du = lax.ppermute(du, "section", ring)
-    spec = to_spectral(section.reshape(1), (section_input.reshape(cells),), forward, quarters, width)
-    both = jnp.concatenate([spec, du], axis=1)
-    later, both = lax.optimization_barrier((handoff, both))
+    received = lax.ppermute(handoff.reshape(cells), "section", ring)
+    spec = to_spectral(section_input.reshape(cells), forward, quarters, width)
+    last = (section == sections - 1).astype(jnp.int32).reshape(1)
+    both, cot = to_spectral_joined(
+        last, spec, received, loss_grad.reshape(cells), inverse, quarters, width
+    )
     both = lax.all_to_all(both, "lat", split_axis=0, concat_axis=0, tiled=True)
-    received = lax.ppermute(later, "section", ring)
-    cot = jnp.where(section == sections - 1, loss_grad, received[0]).reshape(cells)
     weights, biases = block_params(scalars, w_first, w_second, bias, width)
-    cot, both = lax.optimization_barrier((cot, both))
     dz, mine, send = spectral_chain(
         scalars, both, mixer, weights, biases, lat, width, quarters
     )

time: 64.6 us -> 66.8 us (1.034)
  waiting for transfers between devices: 22.8 us -> 26.6 us
  other arithmetic: 1.03 us -> 0.1 us
  starting transfers between devices: 29.2 us -> 28.4 us
    all_to_all x1, waiting for transfers between devices: 9.43 us -> 14.1 us  [on_device(): both = lax.all_to_all(both, 'lat', split_axis=0, concat_axis=0, tiled=True)]
    ppermute x2 -> x1, waiting for transfers between devices: 7.49 us -> 5.83 us  [on_device(): received = lax.ppermute(handoff.reshape(cells), 'section', ring)]
    ppermute x2 -> x1, starting transfers between devices: 2.44 us -> 0.8 us  [on_device(): received = lax.ppermute(handoff.reshape(cells), 'section', ring)]
    concatenate x1 -> x0, other arithmetic: 0.86 us -> none  [on_device(): both = jnp.concatenate([spec, du], axis=1)]
  transfers between devices with their start and end apart: 6 -> 5, of which waited for: 5 -> 4; matrix products, arithmetic and copies ran while one was open for 1% -> 0% of each run, Pallas kernels for 8% -> 8%
where the time goes in v7:
time: 66.8 us; the launch traced here: 66.4 us
  starting transfers between devices  28.4 us (43%)
  waiting for transfers between devices  26.6 us (40%)
  Pallas kernels  9.88 us (15%)
  between operations  0.79 us (1%)
  local copies, waits for them, and re-layouts  0.67 us (1%)
    all_to_all x1, waiting for transfers between devices, on_device(): both = lax.all_to_all(both, 'lat', split_axis=0, concat_axis=0, tiled=True)  14.1 us
    all_to_all x1, starting transfers between devices, on_device(): both = lax.all_to_all(both, 'lat', split_axis=0, concat_axis=0, tiled=True)  13 us
    ppermute x2, starting transfers between devices, swapped(): return lax.ppermute(value, 'lat', [(d, d ^ bit) for d in range(lat_count)])  8.8 us
    ppermute x1, waiting for transfers between devices, on_device(): received = lax.ppermute(handoff.reshape(cells), 'section', ring)  5.83 us
    all_to_all x1, starting transfers between devices, on_device(): da = lax.all_to_all(da, 'lat', split_axis=0, concat_axis=0, tiled=True)  5.79 us
    ppermute x2, waiting for transfers between devices, swapped(): return lax.ppermute(value, 'lat', [(d, d ^ bit) for d in range(lat_count)])  3.33 us
    all_to_all x1, waiting for transfers between devices, on_device(): da = lax.all_to_all(da, 'lat', split_axis=0, concat_axis=0, tiled=True)  3.31 us
    pallas_call x1, Pallas kernels, spectral_chain(): pl.pallas_call(body, in_specs=[SMEM] + [VMEM] * 4, out_specs=[VMEM] * 3,...  2.4 us
  transfers between devices with their start and end apart: 5, of which 4 were waited for; matrix products, arithmetic and copies ran while one was open for 0% of the time, Pallas kernels for 8%

profile of v7, /device:TPU:56, one launch (start us, length us, event | category | flops | bytes accessed | tf_op | source)
XLA Modules:
  0.0 66.4 jit_solution(11615820881135111720)
XLA Ops:
  0.6 0.0 copy-start
  0.6 0.8 %collective-permute-start = (bf16[256,1024]{1,0:T(8,128)(2,1)}, bf16[256,1024]{1,0:T(8,128)(2,1)S(1)}, u32[]{:S(2)}, u32[]{:S(2)}) collective-permute-start(bf16[256,1024]{1,0:T(8,128)(2,1)} %bitcast.16), channel_id=1, source_target_pairs={{0,480},{32,0},{64,32},{96,64},{128,96},{160,128},{192,160},{224,1... | collective-permute-start | bytes 1572872 | tf_op jit(solution)/shard_map/ppermute | solution.py:440
  1.4 0.0 copy-start.1
  1.4 1.4 %to_spectral.1.spec_ref = bf16[32,32,128]{2,1,0:T(8,128)(2,1)S(1)} custom-call(bf16[128,256]{1,0:T(8,128)(2,1)} %constant.50.clone.t_hbm, bf16[256,1024]{1,0:T(8,128)(2,1)} %bitcast.15), custom_call_target="tpu_custom_call" | custom-call | tf_op jit(solution)/shard_map/to_spectral/pallas_call | solution.py:87
  2.8 5.8 %collective-permute-done.received_ref = bf16[256,1024]{1,0:T(8,128)(2,1)S(1)} collective-permute-done((bf16[256,1024]{1,0:T(8,128)(2,1)}, bf16[256,1024]{1,0:T(8,128)(2,1)S(1)}, u32[]{:S(2)}, u32[]{:S(2)}) %collective-permute-start) | collective-permute-done | bytes 524320 | tf_op jit(solution)/shard_map/ppermute | solution.py:440
  8.6 0.0 copy-done.1
  8.6 1.1 %to_spectral_joined.1 = (bf16[32,64,128]{2,1,0:T(8,128)(2,1)}, bf16[256,1024]{1,0:T(8,128)(2,1)S(1)}) custom-call(s32[1]{0:T(128)} %bitcast.3.s_ref, bf16[128,256]{1,0:T(8,128)(2,1)S(1)} %copy-done.1, bf16[32,32,128]{2,1,0:T(8,128)(2,1)S(1)} %to_spectral.1.spec_ref, bf16[256,1024]{1,0:T(8,128)(2,1)S(1)} %collective-permute-done.received_ref, ...), custom_call_target="tpu_custom_call" | custom-call | tf_op jit(solution)/shard_map/to_spectral_joined/pallas_call | solution.py:146
  9.7 13.0 %all-to-all-start = ((bf16[32,64,128]{2,1,0:T(8,128)(2,1)}), bf16[32,64,128]{2,1,0:T(8,128)(2,1)S(1)}, u32[]{:S(2)}, u32[]{:S(2)}) async-start(bf16[32,64,128]{2,1,0:T(8,128)(2,1)} %get-tuple-element.14), calls=%async_computation | async-start | bytes 1048576 | tf_op jit(solution)/shard_map/all_to_all | solution.py:446
  22.7 0.0 copy-start.3
  22.8 0.0 copy-done
  22.8 0.2 dynamic-slice_reduce_fusion
  23.0 0.1 pad_add_fusion.s_ref
  23.0 0.4 copy-done.3
  23.5 0.0 copy-start.5
  23.5 1.6 %block_params.1 = (bf16[4,256,256]{2,1,0:T(8,128)(2,1)S(1)}, f32[4,1,256]{2,1,0:T(1,128)S(1)}) custom-call(s32[5]{0:T(128)S(1)} %pad_add_fusion.s_ref, bf16[1,2,2,1024,128]{4,3,2,1,0:T(8,128)(2,1)} %w1_hbm.1, bf16[1,2,2,1024,128]{4,3,2,1,0:T(8,128)(2,1)} %w2_hbm.1, f32[1,2,2,2,1024]{4,3,2,1,0:T(2,128)S(1)} %copy-done.3), custom_call_target="tpu_custom_call" | custom-call | tf_op jit(solution)/shard_map/block_params/pallas_call | solution.py:225
  25.1 14.1 %all-to-all-done.parts_ref = bf16[32,64,128]{2,1,0:T(8,128)(2,1)S(1)} async-done(((bf16[32,64,128]{2,1,0:T(8,128)(2,1)}), bf16[32,64,128]{2,1,0:T(8,128)(2,1)S(1)}, u32[]{:S(2)}, u32[]{:S(2)}) %all-to-all-start) | async-done | bytes 524320 | tf_op jit(solution)/shard_map/all_to_all | solution.py:446
  39.2 0.0 copy-done.5
  39.2 0.0 copy-start.4
  39.2 2.4 %spectral_chain.1 = (bf16[512,256]{1,0:T(8,128)(2,1)S(1)}, f32[2,272,128]{2,1,0:T(8,128)S(1)}, bf16[2,272,128]{2,1,0:T(8,128)(2,1)S(1)}) custom-call(s32[5]{0:T(128)S(1)} %pad_add_fusion.s_ref, bf16[32,64,128]{2,1,0:T(8,128)(2,1)S(1)} %all-to-all-done.parts_ref, bf16[128,128]{1,0:T(8,128)(2,1)S(1)} %copy-done.5, ...), custom_call_target="tpu_custom_call" | custom-call | tf_op jit(solution)/shard_map/spectral_chain/pallas_call | solution.py:334
  41.6 3.5 %collective-permute-start.1 = (bf16[2,272,128]{2,1,0:T(8,128)(2,1)S(1)}, bf16[2,272,128]{2,1,0:T(8,128)(2,1)S(1)}, u32[]{:S(2)}, u32[]{:S(2)}) collective-permute-start(bf16[2,272,128]{2,1,0:T(8,128)(2,1)S(1)} %get-tuple-element.20), channel_id=1, source_target_pairs={{0,1},{1,0},{2,3},{3,2},{4,5},{5,4},{6,7},{7,6},{8,9},{9,8},{10,11... | collective-permute-start | bytes 417800 | tf_op jit(solution)/shard_map/ppermute | solution.py:453
  45.1 0.0 copy-done.4
  45.1 1.0 %to_bands.1 = bf16[32,32,128]{2,1,0:T(8,128)(2,1)} custom-call(bf16[512,256]{1,0:T(8,128)(2,1)S(1)} %get-tuple-element.17.dz_ref, bf16[128,128]{1,0:T(8,128)(2,1)S(1)} %copy-done.4), custom_call_target="tpu_custom_call" | custom-call | tf_op jit(solution)/shard_map/to_bands/pallas_call | solution.py:364
  46.0 5.8 %all-to-all-start.1 = ((bf16[32,32,128]{2,1,0:T(8,128)(2,1)}), bf16[32,32,128]{2,1,0:T(8,128)(2,1)S(1)}, u32[]{:S(2)}, u32[]{:S(2)}) async-start(bf16[32,32,128]{2,1,0:T(8,128)(2,1)} %to_bands.1), calls=%async_computation.1 | async-start | bytes 524288 | tf_op jit(solution)/shard_map/all_to_all | solution.py:457
  51.8 0.0 collective-permute-done.1.n_ref
  51.9 0.0 copy-start.2
  51.9 5.3 %collective-permute-start.2 = (bf16[272,128]{1,0:T(8,128)(2,1)S(1)}, bf16[272,128]{1,0:T(8,128)(2,1)S(1)}, u32[]{:S(2)}, u32[]{:S(2)}) collective-permute-start(bf16[272,128]{1,0:T(8,128)(2,1)S(1)} %fusion), channel_id=1, source_target_pairs={{0,2},{1,3},{2,0},{3,1},{4,6},{5,7},{6,4},{7,5},{8,10},{9,11},{10,... | collective-permute-start | bytes 208904 | tf_op jit(solution)/shard_map/ppermute | solution.py:453
  57.2 3.3 %collective-permute-done.2.f_ref = bf16[272,128]{1,0:T(8,128)(2,1)S(1)} collective-permute-done((bf16[272,128]{1,0:T(8,128)(2,1)S(1)}, bf16[272,128]{1,0:T(8,128)(2,1)S(1)}, u32[]{:S(2)}, u32[]{:S(2)}) %collective-permute-start.2) | collective-permute-done | bytes 69664 | tf_op jit(solution)/shard_map/ppermute | solution.py:453
  60.5 1.5 %gradient_sum.1 = (f32[128,128]{1,0:T(8,128)}, f32[128,128]{1,0:T(8,128)}, f32[8,32]{1,0:T(8,128)}) custom-call(s32[5]{0:T(128)S(1)} %pad_add_fusion.s_ref, f32[2,272,128]{2,1,0:T(8,128)S(1)} %get-tuple-element.19.m_ref, bf16[2,272,128]{2,1,0:T(8,128)(2,1)S(1)} %collective-permute-done.1.n_ref, bf16[272,128]{1,0:T(8,128)(2,1)S(1)} %collective-permute-done.2.f_ref), custom_call_target="tpu_custom_call" | custom-call | flops 2000000000 | bytes 1048576 | tf_op jit(solution)/shard_map/gradient_sum/pallas_call | solution.py:401
  62.0 3.3 %all-to-all-done.1.p_ref = bf16[32,32,128]{2,1,0:T(8,128)(2,1)S(1)} async-done(((bf16[32,32,128]{2,1,0:T(8,128)(2,1)}), bf16[32,32,128]{2,1,0:T(8,128)(2,1)S(1)}, u32[]{:S(2)}, u32[]{:S(2)}) %all-to-all-start.1) | async-done | bytes 262176 | tf_op jit(solution)/shard_map/all_to_all | solution.py:457
  65.4 0.0 copy-done.2
  65.4 1.0 %to_cells.1 = bf16[256,1024]{1,0:T(8,128)(2,1)} custom-call(bf16[256,128]{1,0:T(8,128)(2,1)S(1)} %copy-done.2, bf16[32,32,128]{2,1,0:T(8,128)(2,1)S(1)} %all-to-all-done.1.p_ref, bf16[256,1024]{1,0:T(8,128)(2,1)S(1)} %get-tuple-element.18.g_ref), custom_call_target="tpu_custom_call" | custom-call | tf_op jit(solution)/shard_map/to_cells/pallas_call | solution.py:187
  (1 shorter events, 0.0 us)
Async XLA Ops:
  0.6 22.1 %copy-start = (s32[1,2,8]{2,1,0:T(2,128)S(1)}, s32[1,2,8]{2,1,0:T(2,128)}, u32[]{:S(2)}) copy-start(s32[1,2,8]{2,1,0:T(2,128)} %param.18) | copy-start | bytes 196
  0.6 8.0 %collective-permute-start = (bf16[256,1024]{1,0:T(8,128)(2,1)}, bf16[256,1024]{1,0:T(8,128)(2,1)S(1)}, u32[]{:S(2)}, u32[]{:S(2)}) collective-permute-start(bf16[256,1024]{1,0:T(8,128)(2,1)} %bitcast.16), channel_id=1, source_target_pairs={{0,480},{32,0},{64,32},{96,64},{128,96},{160,128},{192,160},{224,1... | collective-permute-start | bytes 1572872 | tf_op jit(solution)/shard_map/ppermute | solution.py:440
  1.4 7.2 %copy-start.1 = (bf16[128,256]{1,0:T(8,128)(2,1)S(1)}, bf16[128,256]{1,0:T(8,128)(2,1)}, u32[]{:S(2)}) copy-start(bf16[128,256]{1,0:T(8,128)(2,1)} %constant.51.clone.t_ref) | copy-start | bytes 196612
  9.7 29.4 %all-to-all-start = ((bf16[32,64,128]{2,1,0:T(8,128)(2,1)}), bf16[32,64,128]{2,1,0:T(8,128)(2,1)S(1)}, u32[]{:S(2)}, u32[]{:S(2)}) async-start(bf16[32,64,128]{2,1,0:T(8,128)(2,1)} %get-tuple-element.14), calls=%async_computation | async-start | bytes 1048576 | tf_op jit(solution)/shard_map/all_to_all | solution.py:446
  22.7 0.8 %copy-start.3 = (f32[1,2,2,2,1024]{4,3,2,1,0:T(2,128)S(1)}, f32[1,2,2,2,1024]{4,3,2,1,0:T(2,128)}, u32[]{:S(2)}) copy-start(f32[1,2,2,2,1024]{4,3,2,1,0:T(2,128)} %b_ref.1) | copy-start | bytes 98308
  23.5 15.7 %copy-start.5 = (bf16[128,128]{1,0:T(8,128)(2,1)S(1)}, bf16[128,128]{1,0:T(8,128)(2,1)}, u32[]{:S(2)}) copy-start(bf16[128,128]{1,0:T(8,128)(2,1)} %constant.52.clone.l_ref) | copy-start | bytes 98308
  39.2 5.9 %copy-start.4 = (bf16[128,128]{1,0:T(8,128)(2,1)S(1)}, bf16[128,128]{1,0:T(8,128)(2,1)}, u32[]{:S(2)}) copy-start(bf16[128,128]{1,0:T(8,128)(2,1)} %constant.53.clone.lt_ref) | copy-start | bytes 98308
  41.6 10.2 %collective-permute-start.1 = (bf16[2,272,128]{2,1,0:T(8,128)(2,1)S(1)}, bf16[2,272,128]{2,1,0:T(8,128)(2,1)S(1)}, u32[]{:S(2)}, u32[]{:S(2)}) collective-permute-start(bf16[2,272,128]{2,1,0:T(8,128)(2,1)S(1)} %get-tuple-element.20), channel_id=1, source_target_pairs={{0,1},{1,0},{2,3},{3,2},{4,5},{5,4},{6,7},{7,6},{8,9},{9,8},{10,11... | collective-permute-start | bytes 417800 | tf_op jit(solution)/shard_map/ppermute | solution.py:453
  46.0 19.3 %all-to-all-start.1 = ((bf16[32,32,128]{2,1,0:T(8,128)(2,1)}), bf16[32,32,128]{2,1,0:T(8,128)(2,1)S(1)}, u32[]{:S(2)}, u32[]{:S(2)}) async-start(bf16[32,32,128]{2,1,0:T(8,128)(2,1)} %to_bands.1), calls=%async_computation.1 | async-start | bytes 524288 | tf_op jit(solution)/shard_map/all_to_all | solution.py:457
  51.9 13.5 %copy-start.2 = (bf16[256,128]{1,0:T(8,128)(2,1)S(1)}, bf16[256,128]{1,0:T(8,128)(2,1)}, u32[]{:S(2)}) copy-start(bf16[256,128]{1,0:T(8,128)(2,1)} %constant.54.clone.t_ref) | copy-start | bytes 196612
  51.9 8.7 %collective-permute-start.2 = (bf16[272,128]{1,0:T(8,128)(2,1)S(1)}, bf16[272,128]{1,0:T(8,128)(2,1)S(1)}, u32[]{:S(2)}, u32[]{:S(2)}) collective-permute-start(bf16[272,128]{1,0:T(8,128)(2,1)S(1)} %fusion), channel_id=1, source_target_pairs={{0,2},{1,3},{2,0},{3,1},{4,6},{5,7},{6,4},{7,5},{8,10},{9,11},{10,... | collective-permute-start | bytes 208904 | tf_op jit(solution)/shard_map/ppermute | solution.py:453

commit v8 on v4

--- a/solution.py
+++ b/solution.py
@@ -155,9 +155,10 @@
     )(table_t, parts, grid_add)
 
 
-def block_params(scalars, w_first, w_second, bias, width):
-    def body(s_ref, w1_hbm, w2_hbm, b_ref, w_ref, rows_ref, buf, sem):
-        start = pl.multiple_of(s_ref[1] * width, width)
+def block_params(scalars, w_first, w_second, bias, lat, per, width):
+    def body(s_ref, w1_hbm, w2_hbm, b_ref, w_ref, rows_ref, mask_ref, grid_ref, buf, sem):
+        start = pl.multiple_of(s_ref[0] * width, width)
+        quarter = s_ref[1]
         copies = [
             pltpu.make_async_copy(w.at[0, :, :, pl.ds(start, width), :], buf.at[which], sem.at[which])
             for which, w in enumerate((w1_hbm, w2_hbm))
@@ -170,6 +171,15 @@
                     rows_ref[2 * layer + which, :, r * width : (r + 1) * width] = b_ref[
                         0, layer, which, pl.ds(r, 1), pl.ds(start, width)
                     ]
+            mode = quarter * per + lax.broadcasted_iota(jnp.int32, (per, 1, 2 * width), 0)
+            mask_ref[layer] = (mode < s_ref[2 + layer]).astype(F32)
+        rows = lax.broadcasted_iota(jnp.int32, (lat, lat), 0)
+        cols = lax.broadcasted_iota(jnp.int32, (lat, lat), 1)
+        eye = (rows == cols).astype(F32)
+        back = ((rows + cols) % lat == 0).astype(F32)
+        has_zero = (quarter == 0).astype(F32)
+        grid_ref[0] = (eye + 0.5 * has_zero * (back - eye)).astype(BF16)
+        grid_ref[1] = (eye - 0.5 * has_zero * (back + eye)).astype(BF16)
         for which in range(2):
             copies[which].wait()
             for layer in range(LAYERS):
@@ -182,7 +192,7 @@
     return pl.pallas_call(
         body,
         in_specs=[SMEM, HBM, HBM, VMEM],
-        out_specs=[VMEM, VMEM],
+        out_specs=[VMEM] * 4,
         scratch_shapes=[
             pltpu.VMEM((2, LAYERS, 2, width, width), BF16),
             pltpu.SemaphoreType.DMA((2,)),
@@ -190,24 +200,25 @@
         out_shape=[
             jax.ShapeDtypeStruct((2 * LAYERS, 2 * width, 2 * width), BF16),
             jax.ShapeDtypeStruct((2 * LAYERS, 1, 2 * width), F32),
+            jax.ShapeDtypeStruct((LAYERS, per, 1, 2 * width), F32),
+            jax.ShapeDtypeStruct((2, lat, lat), BF16),
         ],
         compiler_params=params(),
         name="block_params",
     )(scalars, in_hbm(w_first), in_hbm(w_second), bias)
 
 
-def spectral_chain(scalars, parts, mixer, mixer_t, weights, biases, lat, width, quarters):
+def spectral_chain(quarter, parts, mixer, mixer_t, block, lat, width, quarters):
     sources, both, _ = parts.shape
     chunk = (sources, both // 2, width)
     per = sources * (both // 2) // (2 * lat)
     tall = per * lat
-
     own = width // quarters
     count = 4 * LAYERS * own + 16
 
-    def body(s_ref, parts_ref, l_ref, lt_ref, w_ref, b_ref, da_ref, *rest):
+    def body(q_ref, parts_ref, l_ref, lt_ref, w_ref, b_ref, mask_ref, grid_ref, da_ref, *rest):
         mine_and_sent, tmp, all_ref = (rest[:quarters], rest[quarters], rest[quarters + 1])
-        quarter = s_ref[2]
+        quarter = q_ref[0]
         mix, mix_t = (l_ref[...], lt_ref[...])
 
         def mixed(slot):
@@ -220,24 +231,16 @@
                 cells.append(jnp.concatenate([z[:lat], z[lat:]], axis=1))
             return jnp.concatenate(cells, axis=0)
 
-        rows = lax.broadcasted_iota(jnp.int32, (lat, lat), 0)
-        cols = lax.broadcasted_iota(jnp.int32, (lat, lat), 1)
-        eye = (rows == cols).astype(F32)
-        back = ((rows + cols) % lat == 0).astype(F32)
-        has_zero = (quarter == 0).astype(F32)
-        even = (eye + 0.5 * has_zero * (back - eye)).astype(BF16)
-        odd = (eye - 0.5 * has_zero * (back + eye)).astype(BF16)
-
         def through_grid(v):
             first = v[:lat]
             first = jnp.concatenate(
-                [dot(even, first[:, :width]), dot(odd, first[:, width:])], axis=1
+                [dot(grid_ref[0], first[:, :width]), dot(grid_ref[1], first[:, width:])], axis=1
             )
             return jnp.concatenate([first, v[lat:].astype(F32)], axis=0)
 
-        def mask_of(layer):
-            mode = quarter * per + lax.broadcasted_iota(jnp.int32, (tall, 1), 0) // lat
-            return (mode < s_ref[3 + layer]).astype(F32)
+        def masked(v, layer):
+            split = v.reshape(per, lat, 2 * width) * mask_ref[layer]
+            return split.reshape(tall, 2 * width).astype(BF16)
 
         z = mixed(0)
         slopes = []
@@ -268,11 +271,11 @@
             slopes.append(sig * (1.0 + pre * (1.0 - sig)))
             if layer + 1 < LAYERS:
                 out = dot(hidden, w_ref[2 * layer + 1]) + b_ref[2 * layer + 1]
-                z = z + through_grid((out * mask_of(layer)).astype(BF16))
+                z = z + through_grid(masked(out, layer))
         grad = mixed(1)
         total = None
         for layer in reversed(range(LAYERS)):
-            dout = (grad * mask_of(layer)).astype(BF16)
+            dout = masked(grad, layer)
             sums = products(1, layer, dout, sums)
             dpre = (dot_rows(dout, w_ref[2 * layer + 1]) * slopes[layer]).astype(BF16)
             sums = products(0, layer, dpre, sums)
@@ -295,7 +298,7 @@
 
     return pl.pallas_call(
         body,
-        in_specs=[SMEM] + [VMEM] * 5,
+        in_specs=[SMEM] + [VMEM] * 7,
         out_specs=[VMEM] * (1 + quarters),
         scratch_shapes=[
             pltpu.VMEM((2, 2 * lat * per, width), F32),
@@ -308,15 +311,15 @@
         + [jax.ShapeDtypeStruct((count, width), BF16)] * (quarters - 1),
         compiler_params=params(),
         name="spectral_chain",
-    )(scalars, parts, mixer, mixer_t, weights, biases)
-
-
-def gradient_sum(scalars, parts, width):
+    )(quarter, parts, mixer, mixer_t, *block)
+
+
+def gradient_sum(quarter, parts, width):
     quarters = len(parts)
     own = width // quarters
     half = 2 * LAYERS * own
 
-    def body(s_ref, *refs):
+    def body(q_ref, *refs):
         first_hbm, second_hbm, bias_hbm, buf, bias_buf, sem = refs[quarters:]
 
         def added(start, size):
@@ -331,10 +334,7 @@
             pltpu.make_async_copy(buf.at[1], second_hbm, sem.at[1]),
         ]
         sums = added(2 * half, 16)[:8]
-        part = sums[:, :own]
-        for q in range(1, quarters):
-            part = jnp.where(s_ref[2] == q, sums[:, q * own : (q + 1) * own], part)
-        bias_buf[...] = part
+        bias_buf[...] = pltpu.roll(sums, (width - q_ref[0] * own) % width, 1)[:, :own]
         copies[0].start()
         for which in range(2):
             buf[which] = added(which * half, half)
@@ -358,7 +358,7 @@
         ],
         compiler_params=params(),
         name="gradient_sum",
-    )(scalars, *parts)
+    )(quarter, *parts)
 
 
 def on_device(section_input, handoff, loss_grad, w_first, w_second, bias, kept):
@@ -375,8 +375,9 @@
     place = lax.axis_index("lat")
     section = lax.axis_index("section")
     block = place // quarters
+    quarter = (place % quarters).reshape(1)
     limits = lax.dynamic_slice(kept, (0, 0, block), (1, LAYERS, 1)).reshape(-1)
-    scalars = jnp.concatenate([jnp.stack([section, block, place % quarters]), limits])
+    scalars = jnp.concatenate([jnp.stack([block, place % quarters]), limits])
     ring = [(s, (s - 1) % sections) for s in range(sections)]
     cells = (rows * lon, channels)
 
@@ -389,10 +390,11 @@
     both = lax.all_to_all(both, "lat", split_axis=0, concat_axis=0, tiled=True)
     received = lax.ppermute(later, "section", ring)
     cot = jnp.where(section == sections - 1, loss_grad, received[0]).reshape(cells)
-    weights, biases = block_params(scalars, w_first, w_second, bias, width)
+    per = MAXK // quarters
+    own_params = block_params(scalars, w_first, w_second, bias, lat, per, width)
     cot, both = lax.optimization_barrier((cot, both))
     da, *parts = spectral_chain(
-        scalars, both, mixer, mixer.T.copy(), weights, biases, lat, width, quarters
+        quarter, both, mixer, mixer.T.copy(), own_params, lat, width, quarters
     )
     da = lax.all_to_all(da, "lat", split_axis=0, concat_axis=0, tiled=True)
     for step in range(1, quarters):
@@ -404,7 +406,7 @@
         parts[step] = lax.ppermute(parts[step], "lat", pairs)
     handed = to_cells(da, forward.T.copy(), cot, quarters, width)
     handed, parts[0] = lax.optimization_barrier((handed, parts[0]))
-    first, second, biases = gradient_sum(scalars, parts, width)
+    first, second, biases = gradient_sum(quarter, parts, width)
     own = width // quarters
     return (
         handed.reshape(1, rows, lon, channels),

time: 64.2 us -> 62.9 us (0.980)
  Pallas kernels: 9.96 us -> 8.64 us
    pallas_call x1, Pallas kernels: 1.5 us -> 0.76 us  [gradient_sum(): pl.pallas_call(body, in_specs=[SMEM] + [VMEM] * quarters, out_specs=[HBM]...]
where the time goes in v8:
time: 62.9 us; the launch traced here: 62.3 us
  starting transfers between devices  32.5 us (52%)
  waiting for transfers between devices  19.2 us (31%)
  Pallas kernels  8.64 us (14%)
  other arithmetic  1 us (2%)
  between operations  0.78 us (1%)
    all_to_all x1, starting transfers between devices, on_device(): both = lax.all_to_all(both, 'lat', split_axis=0, concat_axis=0, tiled=True)  13.2 us
    ppermute x3, starting transfers between devices, on_device(): parts[step] = lax.ppermute(parts[step], 'lat', pairs)  11.7 us
    all_to_all x1, waiting for transfers between devices, on_device(): both = lax.all_to_all(both, 'lat', split_axis=0, concat_axis=0, tiled=True)  9.44 us
    all_to_all x1, starting transfers between devices, on_device(): da = lax.all_to_all(da, 'lat', split_axis=0, concat_axis=0, tiled=True)  5.19 us
    ppermute x1, waiting for transfers between devices, on_device(): received = lax.ppermute(later, 'section', ring)  4.83 us
    pallas_call x1, Pallas kernels, spectral_chain(): pl.pallas_call(body, in_specs=[SMEM] + [VMEM] * 7, out_specs=[VMEM] * (1...  2.66 us
    ppermute x1, waiting for transfers between devices, on_device(): du = lax.ppermute(du, 'section', ring)  2.65 us
    pallas_call x2, Pallas kernels, to_spectral(): pl.pallas_call(body, in_specs=[SMEM, HBM] + [HBM] * len(sources), out_spe...  2.62 us
  transfers between devices with their start and end apart: 7, of which 4 were waited for; matrix products, arithmetic and copies ran while one was open for 1% of the time, Pallas kernels for 6%

profile of v8, /device:TPU:56, one launch (start us, length us, event | category | flops | bytes accessed | tf_op | source)
XLA Modules:
  0.0 62.3 jit_solution(259028622001138920)
XLA Ops:
  0.6 0.0 copy-start
  0.7 1.3 %to_spectral.3 = bf16[32,32,128]{2,1,0:T(8,128)(2,1)S(1)} custom-call(s32[1]{0:T(128)} %bitcast.1.s_ref, bf16[128,256]{1,0:T(8,128)(2,1)} %constant.52.clone.t_hbm, bf16[256,1024]{1,0:T(8,128)(2,1)} %bitcast.15, bf16[256,1024]{1,0:T(8,128)(2,1)} %bitcast.14), custom_call_target="tpu_custom_call" | custom-call | tf_op jit(solution)/shard_map/to_spectral/pallas_call | solution.py:105
  2.0 0.8 %collective-permute-start.1 = (bf16[32,32,128]{2,1,0:T(8,128)(2,1)S(1)}, bf16[32,32,128]{2,1,0:T(8,128)(2,1)S(1)}, u32[]{:S(2)}, u32[]{:S(2)}) collective-permute-start(bf16[32,32,128]{2,1,0:T(8,128)(2,1)S(1)} %to_spectral.3), channel_id=1, source_target_pairs={{0,480},{32,0},{64,32},{96,64},{128,96},{160,128},{192,160},{224,1... | collective-permute-start | bytes 786440 | tf_op jit(solution)/shard_map/ppermute | solution.py:386
  2.8 1.3 %to_spectral.2 = bf16[32,32,128]{2,1,0:T(8,128)(2,1)S(1)} custom-call(s32[1]{0:T(128)} %bitcast.1.s_ref, bf16[128,256]{1,0:T(8,128)(2,1)} %constant.53.clone.t_hbm, bf16[256,1024]{1,0:T(8,128)(2,1)} %bitcast.16), custom_call_target="tpu_custom_call" | custom-call | tf_op jit(solution)/shard_map/to_spectral/pallas_call | solution.py:105
  4.1 2.7 %collective-permute-done.1 = bf16[32,32,128]{2,1,0:T(8,128)(2,1)S(1)} collective-permute-done((bf16[32,32,128]{2,1,0:T(8,128)(2,1)S(1)}, bf16[32,32,128]{2,1,0:T(8,128)(2,1)S(1)}, u32[]{:S(2)}, u32[]{:S(2)}) %collective-permute-start.1) | collective-permute-done | bytes 262176 | tf_op jit(solution)/shard_map/ppermute | solution.py:386
  6.7 0.9 %pad_maximum_fusion = bf16[32,64,128]{2,1,0:T(8,128)(2,1)} fusion(bf16[32,32,128]{2,1,0:T(8,128)(2,1)S(1)} %collective-permute-done.1, bf16[32,32,128]{2,1,0:T(8,128)(2,1)S(1)} %to_spectral.2), kind=kLoop, calls=%fused_computation | loop fusion | flops 1048576 | bytes 1048576 | tf_op jit(solution)/shard_map/concatenate | solution.py:389
  7.6 13.2 %all-to-all-start = ((bf16[32,64,128]{2,1,0:T(8,128)(2,1)}), bf16[32,64,128]{2,1,0:T(8,128)(2,1)S(1)}, u32[]{:S(2)}, u32[]{:S(2)}) async-start(bf16[32,64,128]{2,1,0:T(8,128)(2,1)} %pad_maximum_fusion), calls=%async_computation | async-start | bytes 1048576 | tf_op jit(solution)/shard_map/all_to_all | solution.py:390
  20.8 0.0 copy-done.6
  20.8 0.0 copy-start.2
  20.8 1.6 %collective-permute-start = (bf16[1,2,128,1024]{3,2,1,0:T(8,128)(2,1)S(1)}, bf16[1,2,128,1024]{3,2,1,0:T(8,128)(2,1)S(1)}, u32[]{:S(2)}, u32[]{:S(2)}) collective-permute-start(bf16[1,2,128,1024]{3,2,1,0:T(8,128)(2,1)S(1)} %copy-done.6), channel_id=1, source_target_pairs={{0,480},{32,0},{64,32},{96,64},{128,96},{160,128},{192,160},{224,1... | collective-permute-start | bytes 1572872 | tf_op jit(solution)/shard_map/ppermute | solution.py:391
  22.5 0.0 copy-done
  22.5 0.2 dynamic-slice_reduce_fusion
  22.7 0.1 pad_add_fusion.s_ref
  22.8 1.6 %block_params.1 = (bf16[4,256,256]{2,1,0:T(8,128)(2,1)S(1)}, f32[4,1,256]{2,1,0:T(1,128)S(1)}, f32[2,8,1,256]{3,2,1,0:T(1,128)S(1)}, bf16[2,64,64]{2,1,0:T(8,128)(2,1)S(1)}) custom-call(s32[4]{0:T(128)S(1)} %pad_add_fusion.s_ref, bf16[1,2,2,1024,128]{4,3,2,1,0:T(8,128)(2,1)} %w1_hbm.1, bf16[1,2,2,1024,128]{4,3,2,1,0:T(8,128)(2,1)} %w2_hbm.1, ...), custom_call_target="tpu_custom_call" | custom-call | tf_op jit(solution)/shard_map/block_params/pallas_call | solution.py:192
  24.3 0.0 copy-start.3
  24.3 0.0 copy-start.4
  24.4 4.8 %collective-permute-done = bf16[1,2,128,1024]{3,2,1,0:T(8,128)(2,1)S(1)} collective-permute-done((bf16[1,2,128,1024]{3,2,1,0:T(8,128)(2,1)S(1)}, bf16[1,2,128,1024]{3,2,1,0:T(8,128)(2,1)S(1)}, u32[]{:S(2)}, u32[]{:S(2)}) %collective-permute-start) | collective-permute-done | bytes 524320 | tf_op jit(solution)/shard_map/ppermute | solution.py:391
  29.2 0.0 copy-done.5
  29.2 0.1 bitcast_select_fusion
  29.2 9.4 %all-to-all-done.parts_ref = bf16[32,64,128]{2,1,0:T(8,128)(2,1)S(1)} async-done(((bf16[32,64,128]{2,1,0:T(8,128)(2,1)}), bf16[32,64,128]{2,1,0:T(8,128)(2,1)S(1)}, u32[]{:S(2)}, u32[]{:S(2)}) %all-to-all-start) | async-done | bytes 524320 | tf_op jit(solution)/shard_map/all_to_all | solution.py:390
  38.7 0.0 copy-done.4
  38.7 2.7 %spectral_chain.1 = (bf16[32,32,128]{2,1,0:T(8,128)(2,1)}, f32[272,128]{1,0:T(8,128)S(1)}, bf16[272,128]{1,0:T(8,128)(2,1)S(1)}, bf16[272,128]{1,0:T(8,128)(2,1)S(1)}, bf16[272,128]{1,0:T(8,128)(2,1)S(1)}) custom-call(s32[1]{0:T(128)} %bitcast.q_ref, bf16[32,64,128]{2,1,0:T(8,128)(2,1)S(1)} %all-to-all-done.parts_ref, bf16[128,128]{1,0:T(8,128)(2,1)S(1)} %copy-done.4, ...), custom_call_target="tpu_custom_call" | custom-call | tf_op jit(solution)/shard_map/spectral_chain/pallas_call | solution.py:299
  41.4 5.2 %all-to-all-start.1 = ((bf16[32,32,128]{2,1,0:T(8,128)(2,1)}), bf16[32,32,128]{2,1,0:T(8,128)(2,1)S(1)}, u32[]{:S(2)}, u32[]{:S(2)}) async-start(bf16[32,32,128]{2,1,0:T(8,128)(2,1)} %get-tuple-element.29), calls=%async_computation.1 | async-start | bytes 524288 | tf_op jit(solution)/shard_map/all_to_all | solution.py:399
  46.6 3.7 %collective-permute-start.2 = (bf16[272,128]{1,0:T(8,128)(2,1)S(1)}, bf16[272,128]{1,0:T(8,128)(2,1)S(1)}, u32[]{:S(2)}, u32[]{:S(2)}) collective-permute-start(bf16[272,128]{1,0:T(8,128)(2,1)S(1)} %get-tuple-element.34), channel_id=1, source_target_pairs={{0,1},{1,2},{2,3},{3,0},{4,5},{5,6},{6,7},{7,4},{8,9},{9,10},{10,1... | collective-permute-start | bytes 208904 | tf_op jit(solution)/shard_map/ppermute | solution.py:406
  50.3 4.6 %collective-permute-start.3 = (bf16[272,128]{1,0:T(8,128)(2,1)S(1)}, bf16[272,128]{1,0:T(8,128)(2,1)S(1)}, u32[]{:S(2)}, u32[]{:S(2)}) collective-permute-start(bf16[272,128]{1,0:T(8,128)(2,1)S(1)} %get-tuple-element.35), channel_id=1, source_target_pairs={{0,2},{1,3},{2,0},{3,1},{4,6},{5,7},{6,4},{7,5},{8,10},{9,11},{10,... | collective-permute-start | bytes 208904 | tf_op jit(solution)/shard_map/ppermute | solution.py:406
  54.9 3.4 %collective-permute-start.4 = (bf16[272,128]{1,0:T(8,128)(2,1)S(1)}, bf16[272,128]{1,0:T(8,128)(2,1)S(1)}, u32[]{:S(2)}, u32[]{:S(2)}) collective-permute-start(bf16[272,128]{1,0:T(8,128)(2,1)S(1)} %get-tuple-element.36), channel_id=1, source_target_pairs={{0,3},{1,0},{2,1},{3,2},{4,7},{5,4},{6,5},{7,6},{8,11},{9,8},{10,9... | collective-permute-start | bytes 208904 | tf_op jit(solution)/shard_map/ppermute | solution.py:406
  58.2 2.2 %all-to-all-done.1.p_ref = bf16[32,32,128]{2,1,0:T(8,128)(2,1)S(1)} async-done(((bf16[32,32,128]{2,1,0:T(8,128)(2,1)}), bf16[32,32,128]{2,1,0:T(8,128)(2,1)S(1)}, u32[]{:S(2)}, u32[]{:S(2)}) %all-to-all-start.1) | async-done | bytes 262176 | tf_op jit(solution)/shard_map/all_to_all | solution.py:399
  60.5 1.0 %to_cells.1 = bf16[256,1024]{1,0:T(8,128)(2,1)} custom-call(bf16[256,128]{1,0:T(8,128)(2,1)S(1)} %copy-done.1, bf16[32,32,128]{2,1,0:T(8,128)(2,1)S(1)} %all-to-all-done.1.p_ref, bf16[256,1024]{1,0:T(8,128)(2,1)S(1)} %bitcast.13), custom_call_target="tpu_custom_call" | custom-call | tf_op jit(solution)/shard_map/to_cells/pallas_call | solution.py:144
  61.5 0.0 collective-permute-done.2.refs_1_
  61.5 0.0 collective-permute-done.3.refs_2_
  61.5 0.0 collective-permute-done.4.refs_3_
  61.6 0.8 %gradient_sum.1 = (f32[128,128]{1,0:T(8,128)}, f32[128,128]{1,0:T(8,128)}, f32[8,32]{1,0:T(8,128)}) custom-call(s32[1]{0:T(128)} %bitcast.q_ref, f32[272,128]{1,0:T(8,128)S(1)} %get-tuple-element.33.refs_0_, bf16[272,128]{1,0:T(8,128)(2,1)S(1)} %collective-permute-done.2.refs_1_, bf16[272,128]{1,0:T(8,128)(2,1)S(1)} %collective-permute-done.3.refs_2_, ...), custom_call_target="tpu_custom_call" | custom-call | tf_op jit(solution)/shard_map/gradient_sum/pallas_call | solution.py:345
  (6 shorter events, 0.0 us)
Async XLA Ops:
  0.6 21.9 %copy-start = (s32[1,2,8]{2,1,0:T(2,128)S(1)}, s32[1,2,8]{2,1,0:T(2,128)}, u32[]{:S(2)}) copy-start(s32[1,2,8]{2,1,0:T(2,128)} %param.18) | copy-start | bytes 196
  2.0 4.8 %collective-permute-start.1 = (bf16[32,32,128]{2,1,0:T(8,128)(2,1)S(1)}, bf16[32,32,128]{2,1,0:T(8,128)(2,1)S(1)}, u32[]{:S(2)}, u32[]{:S(2)}) collective-permute-start(bf16[32,32,128]{2,1,0:T(8,128)(2,1)S(1)} %to_spectral.3), channel_id=1, source_target_pairs={{0,480},{32,0},{64,32},{96,64},{128,96},{160,128},{192,160},{224,1... | collective-permute-start | bytes 786440 | tf_op jit(solution)/shard_map/ppermute | solution.py:386
  7.6 13.2 %copy-start.6 = (bf16[1,2,128,1024]{3,2,1,0:T(8,128)(2,1)S(1)}, bf16[1,2,128,1024]{3,2,1,0:T(8,128)(2,1)}, u32[]{:S(2)}) copy-start(bf16[1,2,128,1024]{3,2,1,0:T(8,128)(2,1)} %param.13) | copy-start | bytes 1572868
  7.6 31.1 %all-to-all-start = ((bf16[32,64,128]{2,1,0:T(8,128)(2,1)}), bf16[32,64,128]{2,1,0:T(8,128)(2,1)S(1)}, u32[]{:S(2)}, u32[]{:S(2)}) async-start(bf16[32,64,128]{2,1,0:T(8,128)(2,1)} %pad_maximum_fusion), calls=%async_computation | async-start | bytes 1048576 | tf_op jit(solution)/shard_map/all_to_all | solution.py:390
  20.8 1.9 %copy-start.2 = (f32[1,2,2,2,1024]{4,3,2,1,0:T(2,128)S(1)}, f32[1,2,2,2,1024]{4,3,2,1,0:T(2,128)}, u32[]{:S(2)}) copy-start(f32[1,2,2,2,1024]{4,3,2,1,0:T(2,128)} %b_ref.1) | copy-start | bytes 98308
  20.8 8.3 %collective-permute-start = (bf16[1,2,128,1024]{3,2,1,0:T(8,128)(2,1)S(1)}, bf16[1,2,128,1024]{3,2,1,0:T(8,128)(2,1)S(1)}, u32[]{:S(2)}, u32[]{:S(2)}) collective-permute-start(bf16[1,2,128,1024]{3,2,1,0:T(8,128)(2,1)S(1)} %copy-done.6), channel_id=1, source_target_pairs={{0,480},{32,0},{64,32},{96,64},{128,96},{160,128},{192,160},{224,1... | collective-permute-start | bytes 1572872 | tf_op jit(solution)/shard_map/ppermute | solution.py:391
  22.8 6.4 %copy-start.5 = (bf16[2,128,1024]{2,1,0:T(8,128)(2,1)S(1)}, bf16[2,128,1024]{2,1,0:T(8,128)(2,1)}, u32[]{:S(2)}) copy-start(bf16[2,128,1024]{2,1,0:T(8,128)(2,1)} %param.14) | copy-start | bytes 1572868
  24.3 14.4 %copy-start.3 = (bf16[128,128]{1,0:T(8,128)(2,1)S(1)}, bf16[128,128]{1,0:T(8,128)(2,1)}, u32[]{:S(2)}) copy-start(bf16[128,128]{1,0:T(8,128)(2,1)} %constant.55.clone.lt_ref) | copy-start | bytes 98308
  24.3 14.4 %copy-start.4 = (bf16[128,128]{1,0:T(8,128)(2,1)S(1)}, bf16[128,128]{1,0:T(8,128)(2,1)}, u32[]{:S(2)}) copy-start(bf16[128,128]{1,0:T(8,128)(2,1)} %constant.54.clone.l_ref) | copy-start | bytes 98308
  41.4 19.1 %copy-start.1 = (bf16[256,128]{1,0:T(8,128)(2,1)S(1)}, bf16[256,128]{1,0:T(8,128)(2,1)}, u32[]{:S(2)}) copy-start(bf16[256,128]{1,0:T(8,128)(2,1)} %constant.56.clone.t_ref) | copy-start | bytes 196612
  41.4 19.1 %all-to-all-start.1 = ((bf16[32,32,128]{2,1,0:T(8,128)(2,1)}), bf16[32,32,128]{2,1,0:T(8,128)(2,1)S(1)}, u32[]{:S(2)}, u32[]{:S(2)}) async-start(bf16[32,32,128]{2,1,0:T(8,128)(2,1)} %get-tuple-element.29), calls=%async_computation.1 | async-start | bytes 524288 | tf_op jit(solution)/shard_map/all_to_all | solution.py:399
  46.6 15.0 %collective-permute-start.2 = (bf16[272,128]{1,0:T(8,128)(2,1)S(1)}, bf16[272,128]{1,0:T(8,128)(2,1)S(1)}, u32[]{:S(2)}, u32[]{:S(2)}) collective-permute-start(bf16[272,128]{1,0:T(8,128)(2,1)S(1)} %get-tuple-element.34), channel_id=1, source_target_pairs={{0,1},{1,2},{2,3},{3,0},{4,5},{5,6},{6,7},{7,4},{8,9},{9,10},{10,1... | collective-permute-start | bytes 208904 | tf_op jit(solution)/shard_map/ppermute | solution.py:406
  50.3 11.3 %collective-permute-start.3 = (bf16[272,128]{1,0:T(8,128)(2,1)S(1)}, bf16[272,128]{1,0:T(8,128)(2,1)S(1)}, u32[]{:S(2)}, u32[]{:S(2)}) collective-permute-start(bf16[272,128]{1,0:T(8,128)(2,1)S(1)} %get-tuple-element.35), channel_id=1, source_target_pairs={{0,2},{1,3},{2,0},{3,1},{4,6},{5,7},{6,4},{7,5},{8,10},{9,11},{10,... | collective-permute-start | bytes 208904 | tf_op jit(solution)/shard_map/ppermute | solution.py:406
  54.9 6.7 %collective-permute-start.4 = (bf16[272,128]{1,0:T(8,128)(2,1)S(1)}, bf16[272,128]{1,0:T(8,128)(2,1)S(1)}, u32[]{:S(2)}, u32[]{:S(2)}) collective-permute-start(bf16[272,128]{1,0:T(8,128)(2,1)S(1)} %get-tuple-element.36), channel_id=1, source_target_pairs={{0,3},{1,0},{2,1},{3,2},{4,7},{5,4},{6,5},{7,6},{8,11},{9,8},{10,9... | collective-permute-start | bytes 208904 | tf_op jit(solution)/shard_map/ppermute | solution.py:406

commit v9 on v8

--- a/solution.py
+++ b/solution.py
@@ -43,10 +43,6 @@
     return jnp.dot(left, right, preferred_element_type=F32)
 
 
-def dot_rows(left, right):
-    return lax.dot_general(left, right, (((1,), (1,)), ((), ())), preferred_element_type=F32)
-
-
 def dot_cols(left, right):
     return lax.dot_general(left, right, (((0,), (0,)), ((), ())), preferred_element_type=F32)
 
@@ -64,7 +60,7 @@
     return pltpu.with_memory_space_constraint(value, pltpu.HBM)
 
 
-def to_spectral(scalars, sources, table, quarters, width):
+def to_spectral(scalars, sources, table, quarters, width, joined):
     cells, channels = sources[0].shape
     rows = table.shape[0] // quarters
     blocks = channels // width
@@ -73,7 +69,8 @@
 
     def body(s_ref, t_hbm, *refs):
         given = refs[: len(sources)]
-        o_ref, t_buf, x_buf, t_sem, x_sem = refs[len(sources) :]
+        out, t_buf, x_buf, o_buf, t_sem, x_sem, o_sem = refs[len(sources) :]
+        o_ref = o_buf if joined else out
 
         def piece(source, cut):
             part = pl.ds(cut * span, span)
@@ -101,21 +98,47 @@
                 for q in range(quarters):
                     owner = (cut * 2 + b) * quarters + q
                     o_ref[owner] = y[q * rows : (q + 1) * rows, b * width : (b + 1) * width]
+        if joined:
+            out_copy = pltpu.make_async_copy(o_buf, out.at[:, pl.ds(0, rows), :], o_sem)
+            out_copy.start()
+            out_copy.wait()
 
     return pl.pallas_call(
         body,
         in_specs=[SMEM, HBM] + [HBM] * len(sources),
-        out_specs=VMEM,
+        out_specs=HBM if joined else VMEM,
         scratch_shapes=[
             pltpu.VMEM(table.shape, BF16),
             pltpu.VMEM((cells, channels), BF16),
+            pltpu.VMEM((blocks * quarters, rows, width), BF16),
             pltpu.SemaphoreType.DMA(()),
             pltpu.SemaphoreType.DMA((cuts,)),
-        ],
-        out_shape=jax.ShapeDtypeStruct((blocks * quarters, rows, width), BF16),
+            pltpu.SemaphoreType.DMA(()),
+        ],
+        out_shape=jax.ShapeDtypeStruct((blocks * quarters, (1 + joined) * rows, width), BF16),
         compiler_params=params(),
         name="to_spectral",
     )(scalars, in_hbm(jnp.asarray(table)), *[in_hbm(source) for source in sources])
+
+
+def lower_halves(both, du):
+    rows = du.shape[1]
+
+    def body(_, du_ref, o_hbm, sem):
+        copy = pltpu.make_async_copy(du_ref, o_hbm.at[:, pl.ds(rows, rows), :], sem)
+        copy.start()
+        copy.wait()
+
+    return pl.pallas_call(
+        body,
+        in_specs=[HBM, VMEM],
+        out_specs=HBM,
+        scratch_shapes=[pltpu.SemaphoreType.DMA(())],
+        out_shape=jax.ShapeDtypeStruct(both.shape, BF16),
+        input_output_aliases={0: 0},
+        compiler_params=params(),
+        name="lower_halves",
+    )(both, du)
 
 
 def to_cells(parts, table_t, grid_add, quarters, width):
@@ -130,10 +153,11 @@
         for cut in range(cuts):
             own = slice(cut * span, (cut + 1) * span)
             table = t_ref[own]
-            for block in range(blocks):
-                part = p_ref[block * quarters : (block + 1) * quarters]
-                part = part.reshape(quarters * rows, width)
-                lanes = slice(block * width, (block + 1) * width)
+            for block in range(0, blocks, 2):
+                part = p_ref[block * quarters : (block + 2) * quarters]
+                part = part.reshape(2, quarters * rows, width)
+                part = jnp.concatenate([part[0], part[1]], axis=1)
+                lanes = slice(block * width, (block + 2) * width)
                 mixed = g_ref[own, lanes].astype(F32) + dot(table, part)
                 buf[own, lanes] = mixed.astype(BF16)
             copies.append(pltpu.make_async_copy(buf.at[own], o_hbm.at[own], sem.at[cut]))
@@ -156,7 +180,7 @@
 
 
 def block_params(scalars, w_first, w_second, bias, lat, per, width):
-    def body(s_ref, w1_hbm, w2_hbm, b_ref, w_ref, rows_ref, mask_ref, grid_ref, buf, sem):
+    def body(s_ref, w1_hbm, w2_hbm, b_ref, w_ref, wt_ref, rows_ref, mask_ref, grid_ref, buf, sem):
         start = pl.multiple_of(s_ref[0] * width, width)
         quarter = s_ref[1]
         copies = [
@@ -188,16 +212,22 @@
                 w_ref[2 * layer + which, :width, width:] = imag
                 w_ref[2 * layer + which, width:, :width] = -imag
                 w_ref[2 * layer + which, width:, width:] = real
+                real, imag = (real.astype(F32).T.astype(BF16), imag.astype(F32).T.astype(BF16))
+                wt_ref[2 * layer + which, :width, :width] = real
+                wt_ref[2 * layer + which, :width, width:] = -imag
+                wt_ref[2 * layer + which, width:, :width] = imag
+                wt_ref[2 * layer + which, width:, width:] = real
 
     return pl.pallas_call(
         body,
         in_specs=[SMEM, HBM, HBM, VMEM],
-        out_specs=[VMEM] * 4,
+        out_specs=[VMEM] * 5,
         scratch_shapes=[
             pltpu.VMEM((2, LAYERS, 2, width, width), BF16),
             pltpu.SemaphoreType.DMA((2,)),
         ],
         out_shape=[
+            jax.ShapeDtypeStruct((2 * LAYERS, 2 * width, 2 * width), BF16),
             jax.ShapeDtypeStruct((2 * LAYERS, 2 * width, 2 * width), BF16),
             jax.ShapeDtypeStruct((2 * LAYERS, 1, 2 * width), F32),
             jax.ShapeDtypeStruct((LAYERS, per, 1, 2 * width), F32),
@@ -216,20 +246,24 @@
     own = width // quarters
     count = 4 * LAYERS * own + 16
 
-    def body(q_ref, parts_ref, l_ref, lt_ref, w_ref, b_ref, mask_ref, grid_ref, da_ref, *rest):
-        mine_and_sent, tmp, all_ref = (rest[:quarters], rest[quarters], rest[quarters + 1])
+    def body(q_ref, parts_ref, l_ref, lt_ref, w_ref, wt_ref, b_ref, mask_ref, *more):
+        grid_ref, da_ref, *mine_and_sent = more[:-2]
+        tmp, all_ref = more[-2:]
         quarter = q_ref[0]
         mix, mix_t = (l_ref[...], lt_ref[...])
 
-        def mixed(slot):
+        for slot in range(2):
             part = parts_ref[:, slot * (both // 2) : (slot + 1) * (both // 2), :]
             tmp[slot] = part.reshape(2 * lat * per, width).astype(F32)
-            cells = []
-            for k in range(per):
-                column = tmp[slot, pl.ds(k, 2 * lat, stride=per), :].astype(BF16)
-                z = dot(mix, column)
-                cells.append(jnp.concatenate([z[:lat], z[lat:]], axis=1))
-            return jnp.concatenate(cells, axis=0)
+        mixed = ([], [])
+        for k in range(per):
+            columns = [tmp[slot, pl.ds(k, 2 * lat, stride=per), :] for slot in range(2)]
+            cells = dot(mix, jnp.concatenate(columns, axis=1).astype(BF16))
+            for slot in range(2):
+                lanes = slice(slot * width, (slot + 1) * width)
+                mixed[slot].append(
+                    jnp.concatenate([cells[:lat, lanes], cells[lat:, lanes]], axis=1)
+                )
 
         def through_grid(v):
             first = v[:lat]
@@ -242,7 +276,7 @@
             split = v.reshape(per, lat, 2 * width) * mask_ref[layer]
             return split.reshape(tall, 2 * width).astype(BF16)
 
-        z = mixed(0)
+        z = jnp.concatenate(mixed[0], axis=0)
         slopes = []
         lefts = {}
         index = lax.broadcasted_iota(jnp.int32, (16, width), 0)
@@ -272,22 +306,25 @@
             if layer + 1 < LAYERS:
                 out = dot(hidden, w_ref[2 * layer + 1]) + b_ref[2 * layer + 1]
                 z = z + through_grid(masked(out, layer))
-        grad = mixed(1)
+        grad = jnp.concatenate(mixed[1], axis=0)
         total = None
         for layer in reversed(range(LAYERS)):
             dout = masked(grad, layer)
             sums = products(1, layer, dout, sums)
-            dpre = (dot_rows(dout, w_ref[2 * layer + 1]) * slopes[layer]).astype(BF16)
+            dpre = (dot(dout, wt_ref[2 * layer + 1]) * slopes[layer]).astype(BF16)
             sums = products(0, layer, dpre, sums)
-            dz = dot_rows(dpre, w_ref[2 * layer])
+            dz = dot(dpre, wt_ref[2 * layer])
             if layer:
                 grad = grad + through_grid(dz.astype(BF16))
             total = dz if total is None else total + dz
         total = total.astype(BF16)
-        for k in range(per):
-            part = total[k * lat : (k + 1) * lat]
-            part = jnp.concatenate([part[:, :width], part[:, width:]], axis=0)
-            tmp[0, pl.ds(k, 2 * lat, stride=per), :] = dot(mix_t, part)
+        for k in range(0, per, 2):
+            pair = [total[j * lat : (j + 1) * lat] for j in (k, k + 1)]
+            pair = [jnp.concatenate([v[:, :width], v[:, width:]], axis=0) for v in pair]
+            bands = dot(mix_t, jnp.concatenate(pair, axis=1))
+            for j in range(2):
+                lanes = slice(j * width, (j + 1) * width)
+                tmp[0, pl.ds(k + j, 2 * lat, stride=per), :] = bands[:, lanes]
         da_ref[...] = tmp[0].astype(BF16).reshape(chunk)
         for step, o_ref in enumerate(mine_and_sent):
             start = pl.multiple_of((quarter + step) % quarters * own, own)
@@ -298,7 +335,7 @@
 
     return pl.pallas_call(
         body,
-        in_specs=[SMEM] + [VMEM] * 7,
+        in_specs=[SMEM] + [VMEM] * 8,
         out_specs=[VMEM] * (1 + quarters),
         scratch_shapes=[
             pltpu.VMEM((2, 2 * lat * per, width), F32),
@@ -382,11 +419,12 @@
     cells = (rows * lon, channels)
 
     handed_du = (handoff.reshape(cells), loss_grad.reshape(cells))
-    du = to_spectral(section.reshape(1), handed_du, inverse, quarters, width)
+    du = to_spectral(section.reshape(1), handed_du, inverse, quarters, width, False)
     du = lax.ppermute(du, "section", ring)
-    spec = to_spectral(section.reshape(1), (section_input.reshape(cells),), forward, quarters, width)
-    later, spec = lax.optimization_barrier((handoff, spec))
-    both = jnp.concatenate([spec, du], axis=1)
+    x = section_input.reshape(cells)
+    both = to_spectral(section.reshape(1), (x,), forward, quarters, width, True)
+    later, both = lax.optimization_barrier((handoff, both))
+    both = lower_halves(both, du)
     both = lax.all_to_all(both, "lat", split_axis=0, concat_axis=0, tiled=True)
     received = lax.ppermute(later, "section", ring)
     cot = jnp.where(section == sections - 1, loss_grad, received[0]).reshape(cells)
@@ -397,7 +435,7 @@
         quarter, both, mixer, mixer.T.copy(), own_params, lat, width, quarters
     )
     da = lax.all_to_all(da, "lat", split_axis=0, concat_axis=0, tiled=True)
-    for step in range(1, quarters):
+    for step in (2, 1, 3):
         pairs = [
             (b * quarters + q, b * quarters + (q + step) % quarters)
             for b in range(blocks)

time: 62.9 us -> 62.9 us (level)
  Pallas kernels: 8.64 us -> 10.2 us
  waiting for transfers between devices: 19.2 us -> 18.3 us
  other arithmetic: 1 us -> 0.13 us
    concatenate x1 -> x0, other arithmetic: 0.86 us -> none  [on_device(): both = jnp.concatenate([spec, du], axis=1)]
    pallas_call x2, Pallas kernels: 2.62 us -> 3.34 us  [to_spectral(): pl.pallas_call(body, in_specs=[SMEM, HBM] + [HBM] * len(sources), out_spe...]
    ppermute x1, waiting for transfers between devices: 2.65 us -> 1.94 us  [on_device(): du = lax.ppermute(du, 'section', ring)]
    pallas_call x1 -> x2, Pallas kernels: 2.66 us -> 3.35 us  [the longest x1 2.64 us: spectral_chain(): pl.pallas_call(body, in_specs=[SMEM] + [VMEM] * 8, out_specs=[VMEM] * (1...]
  transfers between devices with their start and end apart: 7 -> 7, of which waited for: 4 -> 4; matrix products, arithmetic and copies ran while one was open for 1% -> 1% of each run, Pallas kernels for 6% -> 8%
where the time goes in v9:
time: 62.9 us; the launch traced here: 62.1 us
  starting transfers between devices  32.5 us (52%)
  waiting for transfers between devices  18.3 us (29%)
  Pallas kernels  10.2 us (16%)
  between operations  0.78 us (1%)
    all_to_all x1, starting transfers between devices, on_device(): both = lax.all_to_all(both, 'lat', split_axis=0, concat_axis=0, tiled=True)  13.2 us
    ppermute x3, starting transfers between devices, on_device(): parts[step] = lax.ppermute(parts[step], 'lat', pairs)  11.7 us
    all_to_all x1, waiting for transfers between devices, on_device(): both = lax.all_to_all(both, 'lat', split_axis=0, concat_axis=0, tiled=True)  9.43 us
    all_to_all x1, starting transfers between devices, on_device(): da = lax.all_to_all(da, 'lat', split_axis=0, concat_axis=0, tiled=True)  5.18 us
    ppermute x1, waiting for transfers between devices, on_device(): received = lax.ppermute(later, 'section', ring)  4.72 us
    pallas_call x2, Pallas kernels, to_spectral(): pl.pallas_call(body, in_specs=[SMEM, HBM] + [HBM] * len(sources), out_spe...  3.34 us
    pallas_call x1, Pallas kernels, spectral_chain(): pl.pallas_call(body, in_specs=[SMEM] + [VMEM] * 8, out_specs=[VMEM] * (1...  2.64 us
    all_to_all x1, waiting for transfers between devices, on_device(): da = lax.all_to_all(da, 'lat', split_axis=0, concat_axis=0, tiled=True)  2.24 us
  transfers between devices with their start and end apart: 7, of which 4 were waited for; matrix products, arithmetic and copies ran while one was open for 1% of the time, Pallas kernels for 8%

profile of v9, /device:TPU:56, one launch (start us, length us, event | category | flops | bytes accessed | tf_op | source)
XLA Modules:
  0.0 62.1 jit_solution(14661883913510529447)
XLA Ops:
  0.6 0.0 copy-start
  0.7 1.3 %to_spectral.3 = bf16[32,32,128]{2,1,0:T(8,128)(2,1)S(1)} custom-call(s32[1]{0:T(128)} %bitcast.1.s_ref, bf16[128,256]{1,0:T(8,128)(2,1)} %constant.52.clone.t_hbm, bf16[256,1024]{1,0:T(8,128)(2,1)} %bitcast.15, bf16[256,1024]{1,0:T(8,128)(2,1)} %bitcast.14), custom_call_target="tpu_custom_call" | custom-call | tf_op jit(solution)/shard_map/to_spectral/pallas_call | solution.py:106
  2.0 0.8 %collective-permute-start.1 = (bf16[32,32,128]{2,1,0:T(8,128)(2,1)S(1)}, bf16[32,32,128]{2,1,0:T(8,128)(2,1)S(1)}, u32[]{:S(2)}, u32[]{:S(2)}) collective-permute-start(bf16[32,32,128]{2,1,0:T(8,128)(2,1)S(1)} %to_spectral.3), channel_id=1, source_target_pairs={{0,480},{32,0},{64,32},{96,64},{128,96},{160,128},{192,160},{224,1... | collective-permute-start | bytes 786440 | tf_op jit(solution)/shard_map/ppermute | solution.py:423
  2.8 2.0 %to_spectral.2._ = bf16[32,64,128]{2,1,0:T(8,128)(2,1)} custom-call(s32[1]{0:T(128)} %bitcast.1.s_ref, bf16[128,256]{1,0:T(8,128)(2,1)} %constant.53.clone.t_hbm, bf16[256,1024]{1,0:T(8,128)(2,1)} %bitcast.16), custom_call_target="tpu_custom_call" | custom-call | tf_op jit(solution)/shard_map/to_spectral/pallas_call | solution.py:106
  4.8 1.9 %collective-permute-done.1.du_ref = bf16[32,32,128]{2,1,0:T(8,128)(2,1)S(1)} collective-permute-done((bf16[32,32,128]{2,1,0:T(8,128)(2,1)S(1)}, bf16[32,32,128]{2,1,0:T(8,128)(2,1)S(1)}, u32[]{:S(2)}, u32[]{:S(2)}) %collective-permute-start.1) | collective-permute-done | bytes 262176 | tf_op jit(solution)/shard_map/ppermute | solution.py:423
  6.7 0.7 %lower_halves.1 = bf16[32,64,128]{2,1,0:T(8,128)(2,1)} custom-call(bf16[32,64,128]{2,1,0:T(8,128)(2,1)} %to_spectral.2._, bf16[32,32,128]{2,1,0:T(8,128)(2,1)S(1)} %collective-permute-done.1.du_ref), custom_call_target="tpu_custom_call", output_to_operand_aliasing={{}: (0, {})} | custom-call | tf_op jit(solution)/shard_map/lower_halves/pallas_call | solution.py:132
  7.5 0.0 copy-start.6
  7.5 13.2 %all-to-all-start = ((bf16[32,64,128]{2,1,0:T(8,128)(2,1)}), bf16[32,64,128]{2,1,0:T(8,128)(2,1)S(1)}, u32[]{:S(2)}, u32[]{:S(2)}) async-start(bf16[32,64,128]{2,1,0:T(8,128)(2,1)} %lower_halves.1), calls=%async_computation | async-start | bytes 1048576 | tf_op jit(solution)/shard_map/all_to_all | solution.py:428
  20.7 0.0 copy-done.6
  20.7 0.0 copy-start.2
  20.7 1.6 %collective-permute-start = (bf16[1,2,128,1024]{3,2,1,0:T(8,128)(2,1)S(1)}, bf16[1,2,128,1024]{3,2,1,0:T(8,128)(2,1)S(1)}, u32[]{:S(2)}, u32[]{:S(2)}) collective-permute-start(bf16[1,2,128,1024]{3,2,1,0:T(8,128)(2,1)S(1)} %copy-done.6), channel_id=1, source_target_pairs={{0,480},{32,0},{64,32},{96,64},{128,96},{160,128},{192,160},{224,1... | collective-permute-start | bytes 1572872 | tf_op jit(solution)/shard_map/ppermute | solution.py:429
  22.4 0.0 copy-done
  22.4 0.2 dynamic-slice_reduce_fusion
  22.6 0.1 pad_add_fusion.s_ref
  22.6 0.0 copy-done.2
  22.6 1.7 %block_params.1 = (bf16[4,256,256]{2,1,0:T(8,128)(2,1)S(1)}, bf16[4,256,256]{2,1,0:T(8,128)(2,1)S(1)}, f32[4,1,256]{2,1,0:T(1,128)S(1)}, f32[2,8,1,256]{3,2,1,0:T(1,128)S(1)}, bf16[2,64,64]{2,1,0:T(8,128)(2,1)S(1)}) custom-call(s32[4]{0:T(128)S(1)} %pad_add_fusion.s_ref, bf16[1,2,2,1024,128]{4,3,2,1,0:T(8,128)(2,1)} %w1_hbm.1, ...), custom_call_target="tpu_custom_call" | custom-call | tf_op jit(solution)/shard_map/block_params/pallas_call | solution.py:221
  24.3 4.7 %collective-permute-done = bf16[1,2,128,1024]{3,2,1,0:T(8,128)(2,1)S(1)} collective-permute-done((bf16[1,2,128,1024]{3,2,1,0:T(8,128)(2,1)S(1)}, bf16[1,2,128,1024]{3,2,1,0:T(8,128)(2,1)S(1)}, u32[]{:S(2)}, u32[]{:S(2)}) %collective-permute-start) | collective-permute-done | bytes 524320 | tf_op jit(solution)/shard_map/ppermute | solution.py:429
  29.1 0.0 copy-done.5
  29.1 0.1 bitcast_select_fusion
  29.1 9.4 %all-to-all-done.parts_ref = bf16[32,64,128]{2,1,0:T(8,128)(2,1)S(1)} async-done(((bf16[32,64,128]{2,1,0:T(8,128)(2,1)}), bf16[32,64,128]{2,1,0:T(8,128)(2,1)S(1)}, u32[]{:S(2)}, u32[]{:S(2)}) %all-to-all-start) | async-done | bytes 524320 | tf_op jit(solution)/shard_map/all_to_all | solution.py:428
  38.6 0.0 copy-done.3
  38.6 2.6 %spectral_chain.1 = (bf16[32,32,128]{2,1,0:T(8,128)(2,1)}, f32[272,128]{1,0:T(8,128)S(1)}, bf16[272,128]{1,0:T(8,128)(2,1)S(1)}, bf16[272,128]{1,0:T(8,128)(2,1)S(1)}, bf16[272,128]{1,0:T(8,128)(2,1)S(1)}) custom-call(s32[1]{0:T(128)} %bitcast.q_ref, bf16[32,64,128]{2,1,0:T(8,128)(2,1)S(1)} %all-to-all-done.parts_ref, bf16[128,128]{1,0:T(8,128)(2,1)S(1)} %copy-done.4, ...), custom_call_target="tpu_custom_call" | custom-call | tf_op jit(solution)/shard_map/spectral_chain/pallas_call | solution.py:336
  41.2 5.2 %all-to-all-start.1 = ((bf16[32,32,128]{2,1,0:T(8,128)(2,1)}), bf16[32,32,128]{2,1,0:T(8,128)(2,1)S(1)}, u32[]{:S(2)}, u32[]{:S(2)}) async-start(bf16[32,32,128]{2,1,0:T(8,128)(2,1)} %get-tuple-element.31), calls=%async_computation.1 | async-start | bytes 524288 | tf_op jit(solution)/shard_map/all_to_all | solution.py:437
  46.4 3.7 %collective-permute-start.2 = (bf16[272,128]{1,0:T(8,128)(2,1)S(1)}, bf16[272,128]{1,0:T(8,128)(2,1)S(1)}, u32[]{:S(2)}, u32[]{:S(2)}) collective-permute-start(bf16[272,128]{1,0:T(8,128)(2,1)S(1)} %get-tuple-element.36), channel_id=1, source_target_pairs={{0,1},{1,2},{2,3},{3,0},{4,5},{5,6},{6,7},{7,4},{8,9},{9,10},{10,1... | collective-permute-start | bytes 208904 | tf_op jit(solution)/shard_map/ppermute | solution.py:444
  50.1 4.6 %collective-permute-start.3 = (bf16[272,128]{1,0:T(8,128)(2,1)S(1)}, bf16[272,128]{1,0:T(8,128)(2,1)S(1)}, u32[]{:S(2)}, u32[]{:S(2)}) collective-permute-start(bf16[272,128]{1,0:T(8,128)(2,1)S(1)} %get-tuple-element.37), channel_id=1, source_target_pairs={{0,2},{1,3},{2,0},{3,1},{4,6},{5,7},{6,4},{7,5},{8,10},{9,11},{10,... | collective-permute-start | bytes 208904 | tf_op jit(solution)/shard_map/ppermute | solution.py:444
  54.7 3.4 %collective-permute-start.4 = (bf16[272,128]{1,0:T(8,128)(2,1)S(1)}, bf16[272,128]{1,0:T(8,128)(2,1)S(1)}, u32[]{:S(2)}, u32[]{:S(2)}) collective-permute-start(bf16[272,128]{1,0:T(8,128)(2,1)S(1)} %get-tuple-element.38), channel_id=1, source_target_pairs={{0,3},{1,0},{2,1},{3,2},{4,7},{5,4},{6,5},{7,6},{8,11},{9,8},{10,9... | collective-permute-start | bytes 208904 | tf_op jit(solution)/shard_map/ppermute | solution.py:444
  58.1 2.2 %all-to-all-done.1.p_ref = bf16[32,32,128]{2,1,0:T(8,128)(2,1)S(1)} async-done(((bf16[32,32,128]{2,1,0:T(8,128)(2,1)}), bf16[32,32,128]{2,1,0:T(8,128)(2,1)S(1)}, u32[]{:S(2)}, u32[]{:S(2)}) %all-to-all-start.1) | async-done | bytes 262176 | tf_op jit(solution)/shard_map/all_to_all | solution.py:437
  60.3 1.0 %to_cells.1 = bf16[256,1024]{1,0:T(8,128)(2,1)} custom-call(bf16[256,128]{1,0:T(8,128)(2,1)S(1)} %copy-done.1, bf16[32,32,128]{2,1,0:T(8,128)(2,1)S(1)} %all-to-all-done.1.p_ref, bf16[256,1024]{1,0:T(8,128)(2,1)S(1)} %bitcast.13), custom_call_target="tpu_custom_call" | custom-call | tf_op jit(solution)/shard_map/to_cells/pallas_call | solution.py:168
  61.4 0.0 collective-permute-done.2.refs_1_
  61.4 0.0 collective-permute-done.3.refs_2_
  61.4 0.0 collective-permute-done.4.refs_3_
  61.4 0.8 %gradient_sum.1 = (f32[128,128]{1,0:T(8,128)}, f32[128,128]{1,0:T(8,128)}, f32[8,32]{1,0:T(8,128)}) custom-call(s32[1]{0:T(128)} %bitcast.q_ref, f32[272,128]{1,0:T(8,128)S(1)} %get-tuple-element.35.refs_0_, bf16[272,128]{1,0:T(8,128)(2,1)S(1)} %collective-permute-done.2.refs_1_, bf16[272,128]{1,0:T(8,128)(2,1)S(1)} %collective-permute-done.3.refs_2_, ...), custom_call_target="tpu_custom_call" | custom-call | tf_op jit(solution)/shard_map/gradient_sum/pallas_call | solution.py:382
  (6 shorter events, 0.0 us)
Async XLA Ops:
  0.6 21.7 %copy-start = (s32[1,2,8]{2,1,0:T(2,128)S(1)}, s32[1,2,8]{2,1,0:T(2,128)}, u32[]{:S(2)}) copy-start(s32[1,2,8]{2,1,0:T(2,128)} %param.18) | copy-start | bytes 196
  2.0 4.8 %collective-permute-start.1 = (bf16[32,32,128]{2,1,0:T(8,128)(2,1)S(1)}, bf16[32,32,128]{2,1,0:T(8,128)(2,1)S(1)}, u32[]{:S(2)}, u32[]{:S(2)}) collective-permute-start(bf16[32,32,128]{2,1,0:T(8,128)(2,1)S(1)} %to_spectral.3), channel_id=1, source_target_pairs={{0,480},{32,0},{64,32},{96,64},{128,96},{160,128},{192,160},{224,1... | collective-permute-start | bytes 786440 | tf_op jit(solution)/shard_map/ppermute | solution.py:423
  7.5 13.2 %copy-start.6 = (bf16[1,2,128,1024]{3,2,1,0:T(8,128)(2,1)S(1)}, bf16[1,2,128,1024]{3,2,1,0:T(8,128)(2,1)}, u32[]{:S(2)}) copy-start(bf16[1,2,128,1024]{3,2,1,0:T(8,128)(2,1)} %param.13) | copy-start | bytes 1572868
  7.5 31.1 %all-to-all-start = ((bf16[32,64,128]{2,1,0:T(8,128)(2,1)}), bf16[32,64,128]{2,1,0:T(8,128)(2,1)S(1)}, u32[]{:S(2)}, u32[]{:S(2)}) async-start(bf16[32,64,128]{2,1,0:T(8,128)(2,1)} %lower_halves.1), calls=%async_computation | async-start | bytes 1048576 | tf_op jit(solution)/shard_map/all_to_all | solution.py:428
  20.7 1.9 %copy-start.2 = (f32[1,2,2,2,1024]{4,3,2,1,0:T(2,128)S(1)}, f32[1,2,2,2,1024]{4,3,2,1,0:T(2,128)}, u32[]{:S(2)}) copy-start(f32[1,2,2,2,1024]{4,3,2,1,0:T(2,128)} %b_ref.1) | copy-start | bytes 98308
  20.7 8.3 %collective-permute-start = (bf16[1,2,128,1024]{3,2,1,0:T(8,128)(2,1)S(1)}, bf16[1,2,128,1024]{3,2,1,0:T(8,128)(2,1)S(1)}, u32[]{:S(2)}, u32[]{:S(2)}) collective-permute-start(bf16[1,2,128,1024]{3,2,1,0:T(8,128)(2,1)S(1)} %copy-done.6), channel_id=1, source_target_pairs={{0,480},{32,0},{64,32},{96,64},{128,96},{160,128},{192,160},{224,1... | collective-permute-start | bytes 1572872 | tf_op jit(solution)/shard_map/ppermute | solution.py:429
  22.6 6.4 %copy-start.5 = (bf16[2,128,1024]{2,1,0:T(8,128)(2,1)S(1)}, bf16[2,128,1024]{2,1,0:T(8,128)(2,1)}, u32[]{:S(2)}) copy-start(bf16[2,128,1024]{2,1,0:T(8,128)(2,1)} %param.14) | copy-start | bytes 1572868
  29.1 9.5 %copy-start.3 = (bf16[128,128]{1,0:T(8,128)(2,1)S(1)}, bf16[128,128]{1,0:T(8,128)(2,1)}, u32[]{:S(2)}) copy-start(bf16[128,128]{1,0:T(8,128)(2,1)} %constant.55.clone.lt_ref) | copy-start | bytes 98308
  29.1 9.5 %copy-start.4 = (bf16[128,128]{1,0:T(8,128)(2,1)S(1)}, bf16[128,128]{1,0:T(8,128)(2,1)}, u32[]{:S(2)}) copy-start(bf16[128,128]{1,0:T(8,128)(2,1)} %constant.54.clone.l_ref) | copy-start | bytes 98308
  41.2 19.1 %copy-start.1 = (bf16[256,128]{1,0:T(8,128)(2,1)S(1)}, bf16[256,128]{1,0:T(8,128)(2,1)}, u32[]{:S(2)}) copy-start(bf16[256,128]{1,0:T(8,128)(2,1)} %constant.56.clone.t_ref) | copy-start | bytes 196612
  41.2 19.1 %all-to-all-start.1 = ((bf16[32,32,128]{2,1,0:T(8,128)(2,1)}), bf16[32,32,128]{2,1,0:T(8,128)(2,1)S(1)}, u32[]{:S(2)}, u32[]{:S(2)}) async-start(bf16[32,32,128]{2,1,0:T(8,128)(2,1)} %get-tuple-element.31), calls=%async_computation.1 | async-start | bytes 524288 | tf_op jit(solution)/shard_map/all_to_all | solution.py:437
  46.4 15.0 %collective-permute-start.2 = (bf16[272,128]{1,0:T(8,128)(2,1)S(1)}, bf16[272,128]{1,0:T(8,128)(2,1)S(1)}, u32[]{:S(2)}, u32[]{:S(2)}) collective-permute-start(bf16[272,128]{1,0:T(8,128)(2,1)S(1)} %get-tuple-element.36), channel_id=1, source_target_pairs={{0,1},{1,2},{2,3},{3,0},{4,5},{5,6},{6,7},{7,4},{8,9},{9,10},{10,1... | collective-permute-start | bytes 208904 | tf_op jit(solution)/shard_map/ppermute | solution.py:444
  50.1 11.3 %collective-permute-start.3 = (bf16[272,128]{1,0:T(8,128)(2,1)S(1)}, bf16[272,128]{1,0:T(8,128)(2,1)S(1)}, u32[]{:S(2)}, u32[]{:S(2)}) collective-permute-start(bf16[272,128]{1,0:T(8,128)(2,1)S(1)} %get-tuple-element.37), channel_id=1, source_target_pairs={{0,2},{1,3},{2,0},{3,1},{4,6},{5,7},{6,4},{7,5},{8,10},{9,11},{10,... | collective-permute-start | bytes 208904 | tf_op jit(solution)/shard_map/ppermute | solution.py:444
  54.7 6.7 %collective-permute-start.4 = (bf16[272,128]{1,0:T(8,128)(2,1)S(1)}, bf16[272,128]{1,0:T(8,128)(2,1)S(1)}, u32[]{:S(2)}, u32[]{:S(2)}) collective-permute-start(bf16[272,128]{1,0:T(8,128)(2,1)S(1)} %get-tuple-element.38), channel_id=1, source_target_pairs={{0,3},{1,0},{2,1},{3,2},{4,7},{5,4},{6,5},{7,6},{8,11},{9,8},{10,9... | collective-permute-start | bytes 208904 | tf_op jit(solution)/shard_map/ppermute | solution.py:444

commit v10 on v9

--- a/solution.py
+++ b/solution.py
@@ -234,6 +234,7 @@
             jax.ShapeDtypeStruct((2, lat, lat), BF16),
         ],
         compiler_params=params(),
+        cost_estimate=pl.CostEstimate(flops=2 * 10**10, transcendentals=0, bytes_accessed=1 << 20),
         name="block_params",
     )(scalars, in_hbm(w_first), in_hbm(w_second), bias)
 

time: 62.9 us -> 62.7 us (level)
  starting transfers between devices: 32.5 us -> 31.4 us
  other arithmetic: 0.13 us -> 1.18 us
    all_to_all x1, waiting for transfers between devices: 9.43 us -> 15 us  [on_device(): both = lax.all_to_all(both, 'lat', split_axis=0, concat_axis=0, tiled=True)]
    ppermute x1, waiting for transfers between devices: 4.72 us -> 0.01 us  [on_device(): received = lax.ppermute(later, 'section', ring)]
    select_n x1, other arithmetic: 0.06 us -> 1.11 us  [on_device(): jnp.where(section == sections - 1, loss_grad, received[0]).reshape(cells)]
    ppermute x1, waiting for transfers between devices: 1.94 us -> 0.92 us  [on_device(): du = lax.ppermute(du, 'section', ring)]
    ppermute x1, starting transfers between devices: 1.64 us -> 0.69 us  [on_device(): received = lax.ppermute(later, 'section', ring)]
  transfers between devices with their start and end apart: 7 -> 7, of which waited for: 4 -> 3; matrix products, arithmetic and copies ran while one was open for 1% -> 2% of each run, Pallas kernels for 8% -> 9%
where the time goes in v10:
time: 62.7 us; the launch traced here: 62 us
  starting transfers between devices  31.4 us (50%)
  waiting for transfers between devices  18.1 us (29%)
  Pallas kernels  10.2 us (16%)
  other arithmetic  1.18 us (2%)
  between operations  0.83 us (1%)
    all_to_all x1, waiting for transfers between devices, on_device(): both = lax.all_to_all(both, 'lat', split_axis=0, concat_axis=0, tiled=True)  15 us
    all_to_all x1, starting transfers between devices, on_device(): both = lax.all_to_all(both, 'lat', split_axis=0, concat_axis=0, tiled=True)  13.1 us
    ppermute x3, starting transfers between devices, on_device(): parts[step] = lax.ppermute(parts[step], 'lat', pairs)  11.7 us
    all_to_all x1, starting transfers between devices, on_device(): da = lax.all_to_all(da, 'lat', split_axis=0, concat_axis=0, tiled=True)  5.17 us
    pallas_call x2, Pallas kernels, to_spectral(): pl.pallas_call(body, in_specs=[SMEM, HBM] + [HBM] * len(sources), out_spe...  3.39 us
    pallas_call x1, Pallas kernels, spectral_chain(): pl.pallas_call(body, in_specs=[SMEM] + [VMEM] * 8, out_specs=[VMEM] * (1...  2.64 us
    all_to_all x1, waiting for transfers between devices, on_device(): da = lax.all_to_all(da, 'lat', split_axis=0, concat_axis=0, tiled=True)  2.24 us
    pallas_call x1, Pallas kernels, block_params(): pl.pallas_call(body, in_specs=[SMEM, HBM, HBM, VMEM], out_specs=[VMEM] *...  1.7 us
  transfers between devices with their start and end apart: 7, of which 3 were waited for; matrix products, arithmetic and copies ran while one was open for 2% of the time, Pallas kernels for 9%

profile of v10, /device:TPU:56, one launch (start us, length us, event | category | flops | bytes accessed | tf_op | source)
XLA Modules:
  0.0 62.0 jit_solution(3433961950850999168)
XLA Ops:
  0.6 0.0 copy-start
  0.7 1.3 %to_spectral.3 = bf16[32,32,128]{2,1,0:T(8,128)(2,1)S(1)} custom-call(s32[1]{0:T(128)} %bitcast.1.s_ref, bf16[128,256]{1,0:T(8,128)(2,1)} %constant.52.clone.t_hbm, bf16[256,1024]{1,0:T(8,128)(2,1)} %bitcast.15, bf16[256,1024]{1,0:T(8,128)(2,1)} %bitcast.14), custom_call_target="tpu_custom_call" | custom-call | tf_op jit(solution)/shard_map/to_spectral/pallas_call | solution.py:106
  2.0 0.8 %collective-permute-start.1 = (bf16[32,32,128]{2,1,0:T(8,128)(2,1)S(1)}, bf16[32,32,128]{2,1,0:T(8,128)(2,1)S(1)}, u32[]{:S(2)}, u32[]{:S(2)}) collective-permute-start(bf16[32,32,128]{2,1,0:T(8,128)(2,1)S(1)} %to_spectral.3), channel_id=1, source_target_pairs={{0,480},{32,0},{64,32},{96,64},{128,96},{160,128},{192,160},{224,1... | collective-permute-start | bytes 786440 | tf_op jit(solution)/shard_map/ppermute | solution.py:424
  2.8 2.1 %to_spectral.2._ = bf16[32,64,128]{2,1,0:T(8,128)(2,1)} custom-call(s32[1]{0:T(128)} %bitcast.1.s_ref, bf16[128,256]{1,0:T(8,128)(2,1)} %constant.53.clone.t_hbm, bf16[256,1024]{1,0:T(8,128)(2,1)} %bitcast.16), custom_call_target="tpu_custom_call" | custom-call | tf_op jit(solution)/shard_map/to_spectral/pallas_call | solution.py:106
  4.9 0.7 %collective-permute-start = (bf16[1,2,128,1024]{3,2,1,0:T(8,128)(2,1)S(1)}, bf16[1,2,128,1024]{3,2,1,0:T(8,128)(2,1)}, u32[]{:S(2)}, u32[]{:S(2)}) collective-permute-start(bf16[1,2,128,1024]{3,2,1,0:T(8,128)(2,1)S(1)} %copy-done.6), channel_id=1, source_target_pairs={{0,480},{32,0},{64,32},{96,64},{128,96},{160,128},{192,160},{224,1... | collective-permute-start | bytes 1572872 | tf_op jit(solution)/shard_map/ppermute | solution.py:430
  5.6 0.2 dynamic-slice_reduce_fusion
  5.7 0.1 pad_add_fusion.s_ref
  5.8 0.9 %collective-permute-done.1.du_ref = bf16[32,32,128]{2,1,0:T(8,128)(2,1)S(1)} collective-permute-done((bf16[32,32,128]{2,1,0:T(8,128)(2,1)S(1)}, bf16[32,32,128]{2,1,0:T(8,128)(2,1)S(1)}, u32[]{:S(2)}, u32[]{:S(2)}) %collective-permute-start.1) | collective-permute-done | bytes 262176 | tf_op jit(solution)/shard_map/ppermute | solution.py:424
  6.7 0.7 %lower_halves.1 = bf16[32,64,128]{2,1,0:T(8,128)(2,1)} custom-call(bf16[32,64,128]{2,1,0:T(8,128)(2,1)} %to_spectral.2._, bf16[32,32,128]{2,1,0:T(8,128)(2,1)S(1)} %collective-permute-done.1.du_ref), custom_call_target="tpu_custom_call", output_to_operand_aliasing={{}: (0, {})} | custom-call | tf_op jit(solution)/shard_map/lower_halves/pallas_call | solution.py:132
  7.5 0.0 copy-start.4
  7.5 13.1 %all-to-all-start = ((bf16[32,64,128]{2,1,0:T(8,128)(2,1)}), bf16[32,64,128]{2,1,0:T(8,128)(2,1)S(1)}, u32[]{:S(2)}, u32[]{:S(2)}) async-start(bf16[32,64,128]{2,1,0:T(8,128)(2,1)} %lower_halves.1), calls=%async_computation | async-start | bytes 1048576 | tf_op jit(solution)/shard_map/all_to_all | solution.py:429
  20.6 0.0 copy-done.4
  20.6 0.0 copy-start.5
  20.6 1.7 %block_params.1 = (bf16[4,256,256]{2,1,0:T(8,128)(2,1)S(1)}, bf16[4,256,256]{2,1,0:T(8,128)(2,1)S(1)}, f32[4,1,256]{2,1,0:T(1,128)S(1)}, f32[2,8,1,256]{3,2,1,0:T(1,128)S(1)}, bf16[2,64,64]{2,1,0:T(8,128)(2,1)S(1)}) custom-call(s32[4]{0:T(128)S(1)} %pad_add_fusion.s_ref, bf16[1,2,2,1024,128]{4,3,2,1,0:T(8,128)(2,1)} %w1_hbm.1, ...), custom_call_target="tpu_custom_call" | custom-call | flops 20000000000 | bytes 1048576 | tf_op jit(solution)/shard_map/block_params/pallas_call | solution.py:221
  22.3 0.0 collective-permute-done
  22.3 0.0 copy-done.5
  22.3 0.0 copy-start.2
  22.3 0.0 copy-start.3
  22.3 1.1 %bitcast_select_fusion = bf16[2,128,1024]{2,1,0:T(8,128)(2,1)S(1)} fusion(bf16[2,128,1024]{2,1,0:T(8,128)(2,1)S(1)} %copy-done.5, bf16[1,2,128,1024]{3,2,1,0:T(8,128)(2,1)} %collective-permute-done, pred[]{:T(512)S(6)} %eq.6), kind=kLoop, calls=%fused_computation | loop fusion | flops 262144 | bytes 1572865 | tf_op jit(solution)/shard_map/jit(_where)/select_n | solution.py:431
  23.5 15.0 %all-to-all-done.parts_ref = bf16[32,64,128]{2,1,0:T(8,128)(2,1)S(1)} async-done(((bf16[32,64,128]{2,1,0:T(8,128)(2,1)}), bf16[32,64,128]{2,1,0:T(8,128)(2,1)S(1)}, u32[]{:S(2)}, u32[]{:S(2)}) %all-to-all-start) | async-done | bytes 524320 | tf_op jit(solution)/shard_map/all_to_all | solution.py:429
  38.4 2.6 %spectral_chain.1 = (bf16[32,32,128]{2,1,0:T(8,128)(2,1)}, f32[272,128]{1,0:T(8,128)S(1)}, bf16[272,128]{1,0:T(8,128)(2,1)S(1)}, bf16[272,128]{1,0:T(8,128)(2,1)S(1)}, bf16[272,128]{1,0:T(8,128)(2,1)S(1)}) custom-call(s32[1]{0:T(128)} %bitcast.q_ref, bf16[32,64,128]{2,1,0:T(8,128)(2,1)S(1)} %all-to-all-done.parts_ref, bf16[128,128]{1,0:T(8,128)(2,1)S(1)} %copy-done.3, ...), custom_call_target="tpu_custom_call" | custom-call | tf_op jit(solution)/shard_map/spectral_chain/pallas_call | solution.py:337
  41.1 5.2 %all-to-all-start.1 = ((bf16[32,32,128]{2,1,0:T(8,128)(2,1)}), bf16[32,32,128]{2,1,0:T(8,128)(2,1)S(1)}, u32[]{:S(2)}, u32[]{:S(2)}) async-start(bf16[32,32,128]{2,1,0:T(8,128)(2,1)} %get-tuple-element.31), calls=%async_computation.1 | async-start | bytes 524288 | tf_op jit(solution)/shard_map/all_to_all | solution.py:438
  46.3 3.7 %collective-permute-start.2 = (bf16[272,128]{1,0:T(8,128)(2,1)S(1)}, bf16[272,128]{1,0:T(8,128)(2,1)S(1)}, u32[]{:S(2)}, u32[]{:S(2)}) collective-permute-start(bf16[272,128]{1,0:T(8,128)(2,1)S(1)} %get-tuple-element.36), channel_id=1, source_target_pairs={{0,1},{1,2},{2,3},{3,0},{4,5},{5,6},{6,7},{7,4},{8,9},{9,10},{10,1... | collective-permute-start | bytes 208904 | tf_op jit(solution)/shard_map/ppermute | solution.py:445
  50.0 4.6 %collective-permute-start.3 = (bf16[272,128]{1,0:T(8,128)(2,1)S(1)}, bf16[272,128]{1,0:T(8,128)(2,1)S(1)}, u32[]{:S(2)}, u32[]{:S(2)}) collective-permute-start(bf16[272,128]{1,0:T(8,128)(2,1)S(1)} %get-tuple-element.37), channel_id=1, source_target_pairs={{0,2},{1,3},{2,0},{3,1},{4,6},{5,7},{6,4},{7,5},{8,10},{9,11},{10,... | collective-permute-start | bytes 208904 | tf_op jit(solution)/shard_map/ppermute | solution.py:445
  54.6 3.4 %collective-permute-start.4 = (bf16[272,128]{1,0:T(8,128)(2,1)S(1)}, bf16[272,128]{1,0:T(8,128)(2,1)S(1)}, u32[]{:S(2)}, u32[]{:S(2)}) collective-permute-start(bf16[272,128]{1,0:T(8,128)(2,1)S(1)} %get-tuple-element.38), channel_id=1, source_target_pairs={{0,3},{1,0},{2,1},{3,2},{4,7},{5,4},{6,5},{7,6},{8,11},{9,8},{10,9... | collective-permute-start | bytes 208904 | tf_op jit(solution)/shard_map/ppermute | solution.py:445
  57.9 2.2 %all-to-all-done.1.p_ref = bf16[32,32,128]{2,1,0:T(8,128)(2,1)S(1)} async-done(((bf16[32,32,128]{2,1,0:T(8,128)(2,1)}), bf16[32,32,128]{2,1,0:T(8,128)(2,1)S(1)}, u32[]{:S(2)}, u32[]{:S(2)}) %all-to-all-start.1) | async-done | bytes 262176 | tf_op jit(solution)/shard_map/all_to_all | solution.py:438
  60.2 0.0 copy-done.1
  60.2 1.0 %to_cells.1 = bf16[256,1024]{1,0:T(8,128)(2,1)} custom-call(bf16[256,128]{1,0:T(8,128)(2,1)S(1)} %copy-done.1, bf16[32,32,128]{2,1,0:T(8,128)(2,1)S(1)} %all-to-all-done.1.p_ref, bf16[256,1024]{1,0:T(8,128)(2,1)S(1)} %bitcast.13), custom_call_target="tpu_custom_call" | custom-call | tf_op jit(solution)/shard_map/to_cells/pallas_call | solution.py:168
  61.2 0.0 collective-permute-done.2.refs_1_
  61.2 0.0 collective-permute-done.3.refs_2_
  61.2 0.0 collective-permute-done.4.refs_3_
  61.3 0.8 %gradient_sum.1 = (f32[128,128]{1,0:T(8,128)}, f32[128,128]{1,0:T(8,128)}, f32[8,32]{1,0:T(8,128)}) custom-call(s32[1]{0:T(128)} %bitcast.q_ref, f32[272,128]{1,0:T(8,128)S(1)} %get-tuple-element.35.refs_0_, bf16[272,128]{1,0:T(8,128)(2,1)S(1)} %collective-permute-done.2.refs_1_, bf16[272,128]{1,0:T(8,128)(2,1)S(1)} %collective-permute-done.3.refs_2_, ...), custom_call_target="tpu_custom_call" | custom-call | tf_op jit(solution)/shard_map/gradient_sum/pallas_call | solution.py:383
  (6 shorter events, 0.0 us)
Async XLA Ops:
  0.6 4.9 %copy-start = (s32[1,2,8]{2,1,0:T(2,128)S(1)}, s32[1,2,8]{2,1,0:T(2,128)}, u32[]{:S(2)}) copy-start(s32[1,2,8]{2,1,0:T(2,128)} %param.18) | copy-start | bytes 196
  2.0 4.8 %collective-permute-start.1 = (bf16[32,32,128]{2,1,0:T(8,128)(2,1)S(1)}, bf16[32,32,128]{2,1,0:T(8,128)(2,1)S(1)}, u32[]{:S(2)}, u32[]{:S(2)}) collective-permute-start(bf16[32,32,128]{2,1,0:T(8,128)(2,1)S(1)} %to_spectral.3), channel_id=1, source_target_pairs={{0,480},{32,0},{64,32},{96,64},{128,96},{160,128},{192,160},{224,1... | collective-permute-start | bytes 786440 | tf_op jit(solution)/shard_map/ppermute | solution.py:424
  2.8 2.1 %copy-start.6 = (bf16[1,2,128,1024]{3,2,1,0:T(8,128)(2,1)S(1)}, bf16[1,2,128,1024]{3,2,1,0:T(8,128)(2,1)}, u32[]{:S(2)}) copy-start(bf16[1,2,128,1024]{3,2,1,0:T(8,128)(2,1)} %param.13) | copy-start | bytes 1572868
  4.9 17.4 %collective-permute-start = (bf16[1,2,128,1024]{3,2,1,0:T(8,128)(2,1)S(1)}, bf16[1,2,128,1024]{3,2,1,0:T(8,128)(2,1)}, u32[]{:S(2)}, u32[]{:S(2)}) collective-permute-start(bf16[1,2,128,1024]{3,2,1,0:T(8,128)(2,1)S(1)} %copy-done.6), channel_id=1, source_target_pairs={{0,480},{32,0},{64,32},{96,64},{128,96},{160,128},{192,160},{224,1... | collective-permute-start | bytes 1572872 | tf_op jit(solution)/shard_map/ppermute | solution.py:430
  7.5 13.1 %copy-start.4 = (f32[1,2,2,2,1024]{4,3,2,1,0:T(2,128)S(1)}, f32[1,2,2,2,1024]{4,3,2,1,0:T(2,128)}, u32[]{:S(2)}) copy-start(f32[1,2,2,2,1024]{4,3,2,1,0:T(2,128)} %b_ref.1) | copy-start | bytes 98308
  7.5 31.0 %all-to-all-start = ((bf16[32,64,128]{2,1,0:T(8,128)(2,1)}), bf16[32,64,128]{2,1,0:T(8,128)(2,1)S(1)}, u32[]{:S(2)}, u32[]{:S(2)}) async-start(bf16[32,64,128]{2,1,0:T(8,128)(2,1)} %lower_halves.1), calls=%async_computation | async-start | bytes 1048576 | tf_op jit(solution)/shard_map/all_to_all | solution.py:429
  20.6 1.7 %copy-start.5 = (bf16[2,128,1024]{2,1,0:T(8,128)(2,1)S(1)}, bf16[2,128,1024]{2,1,0:T(8,128)(2,1)}, u32[]{:S(2)}) copy-start(bf16[2,128,1024]{2,1,0:T(8,128)(2,1)} %param.14) | copy-start | bytes 1572868
  22.3 16.1 %copy-start.2 = (bf16[128,128]{1,0:T(8,128)(2,1)S(1)}, bf16[128,128]{1,0:T(8,128)(2,1)}, u32[]{:S(2)}) copy-start(bf16[128,128]{1,0:T(8,128)(2,1)} %constant.55.clone.lt_ref) | copy-start | bytes 98308
  22.3 16.1 %copy-start.3 = (bf16[128,128]{1,0:T(8,128)(2,1)S(1)}, bf16[128,128]{1,0:T(8,128)(2,1)}, u32[]{:S(2)}) copy-start(bf16[128,128]{1,0:T(8,128)(2,1)} %constant.54.clone.l_ref) | copy-start | bytes 98308
  41.1 19.1 %copy-start.1 = (bf16[256,128]{1,0:T(8,128)(2,1)S(1)}, bf16[256,128]{1,0:T(8,128)(2,1)}, u32[]{:S(2)}) copy-start(bf16[256,128]{1,0:T(8,128)(2,1)} %constant.56.clone.t_ref) | copy-start | bytes 196612
  41.1 19.1 %all-to-all-start.1 = ((bf16[32,32,128]{2,1,0:T(8,128)(2,1)}), bf16[32,32,128]{2,1,0:T(8,128)(2,1)S(1)}, u32[]{:S(2)}, u32[]{:S(2)}) async-start(bf16[32,32,128]{2,1,0:T(8,128)(2,1)} %get-tuple-element.31), calls=%async_computation.1 | async-start | bytes 524288 | tf_op jit(solution)/shard_map/all_to_all | solution.py:438
  46.3 15.0 %collective-permute-start.2 = (bf16[272,128]{1,0:T(8,128)(2,1)S(1)}, bf16[272,128]{1,0:T(8,128)(2,1)S(1)}, u32[]{:S(2)}, u32[]{:S(2)}) collective-permute-start(bf16[272,128]{1,0:T(8,128)(2,1)S(1)} %get-tuple-element.36), channel_id=1, source_target_pairs={{0,1},{1,2},{2,3},{3,0},{4,5},{5,6},{6,7},{7,4},{8,9},{9,10},{10,1... | collective-permute-start | bytes 208904 | tf_op jit(solution)/shard_map/ppermute | solution.py:445
  50.0 11.3 %collective-permute-start.3 = (bf16[272,128]{1,0:T(8,128)(2,1)S(1)}, bf16[272,128]{1,0:T(8,128)(2,1)S(1)}, u32[]{:S(2)}, u32[]{:S(2)}) collective-permute-start(bf16[272,128]{1,0:T(8,128)(2,1)S(1)} %get-tuple-element.37), channel_id=1, source_target_pairs={{0,2},{1,3},{2,0},{3,1},{4,6},{5,7},{6,4},{7,5},{8,10},{9,11},{10,... | collective-permute-start | bytes 208904 | tf_op jit(solution)/shard_map/ppermute | solution.py:445
  54.6 6.7 %collective-permute-start.4 = (bf16[272,128]{1,0:T(8,128)(2,1)S(1)}, bf16[272,128]{1,0:T(8,128)(2,1)S(1)}, u32[]{:S(2)}, u32[]{:S(2)}) collective-permute-start(bf16[272,128]{1,0:T(8,128)(2,1)S(1)} %get-tuple-element.38), channel_id=1, source_target_pairs={{0,3},{1,0},{2,1},{3,2},{4,7},{5,4},{6,5},{7,6},{8,11},{9,8},{10,9... | collective-permute-start | bytes 208904 | tf_op jit(solution)/shard_map/ppermute | solution.py:445

commit v11 on v9

--- a/solution.py
+++ b/solution.py
@@ -327,7 +327,7 @@
                 tmp[0, pl.ds(k + j, 2 * lat, stride=per), :] = bands[:, lanes]
         da_ref[...] = tmp[0].astype(BF16).reshape(chunk)
         for step, o_ref in enumerate(mine_and_sent):
-            start = pl.multiple_of((quarter + step) % quarters * own, own)
+            start = pl.multiple_of((quarter ^ step) * own, own)
             for square in range(4 * LAYERS):
                 part = all_ref[square, pl.ds(start, own), :]
                 o_ref[square * own : (square + 1) * own] = part.astype(o_ref.dtype)
@@ -435,12 +435,8 @@
         quarter, both, mixer, mixer.T.copy(), own_params, lat, width, quarters
     )
     da = lax.all_to_all(da, "lat", split_axis=0, concat_axis=0, tiled=True)
-    for step in (2, 1, 3):
-        pairs = [
-            (b * quarters + q, b * quarters + (q + step) % quarters)
-            for b in range(blocks)
-            for q in range(quarters)
-        ]
+    for step in range(1, quarters):
+        pairs = [(d, d ^ step) for d in range(lat_count)]
         parts[step] = lax.ppermute(parts[step], "lat", pairs)
     handed = to_cells(da, forward.T.copy(), cot, quarters, width)
     handed, parts[0] = lax.optimization_barrier((handed, parts[0]))

time: 62.9 us -> 64 us (1.017)
  waiting for transfers between devices: 18.3 us -> 20.3 us
  starting transfers between devices: 32.5 us -> 31.3 us
    all_to_all x1, waiting for transfers between devices: 2.24 us -> 3.47 us  [on_device(): da = lax.all_to_all(da, 'lat', split_axis=0, concat_axis=0, tiled=True)]
    ppermute x3, starting transfers between devices: 11.7 us -> 10.4 us  [on_device(): parts[step] = lax.ppermute(parts[step], 'lat', pairs)]
    ppermute x3, waiting for transfers between devices: 0.01 us -> 0.74 us  [on_device(): parts[step] = lax.ppermute(parts[step], 'lat', pairs)]
  transfers between devices with their start and end apart: 7 -> 7, of which waited for: 4 -> 5; matrix products, arithmetic and copies ran while one was open for 1% -> 1% of each run, Pallas kernels for 8% -> 8%
where the time goes in v11:
time: 64 us; the launch traced here: 62.9 us
  starting transfers between devices  31.3 us (49%)
  waiting for transfers between devices  20.3 us (32%)
  Pallas kernels  10.2 us (16%)
  between operations  0.78 us (1%)
    all_to_all x1, starting transfers between devices, on_device(): both = lax.all_to_all(both, 'lat', split_axis=0, concat_axis=0, tiled=True)  13.2 us
    ppermute x3, starting transfers between devices, on_device(): parts[step] = lax.ppermute(parts[step], 'lat', pairs)  10.4 us
    all_to_all x1, waiting for transfers between devices, on_device(): both = lax.all_to_all(both, 'lat', split_axis=0, concat_axis=0, tiled=True)  9.43 us
    all_to_all x1, starting transfers between devices, on_device(): da = lax.all_to_all(da, 'lat', split_axis=0, concat_axis=0, tiled=True)  5.18 us
    ppermute x1, waiting for transfers between devices, on_device(): received = lax.ppermute(later, 'section', ring)  4.72 us
    all_to_all x1, waiting for transfers between devices, on_device(): da = lax.all_to_all(da, 'lat', split_axis=0, concat_axis=0, tiled=True)  3.47 us
    pallas_call x2, Pallas kernels, to_spectral(): pl.pallas_call(body, in_specs=[SMEM, HBM] + [HBM] * len(sources), out_spe...  3.34 us
    pallas_call x1, Pallas kernels, spectral_chain(): pl.pallas_call(body, in_specs=[SMEM] + [VMEM] * 8, out_specs=[VMEM] * (1...  2.64 us
  transfers between devices with their start and end apart: 7, of which 5 were waited for; matrix products, arithmetic and copies ran while one was open for 1% of the time, Pallas kernels for 8%

profile of v11, /device:TPU:56, one launch (start us, length us, event | category | flops | bytes accessed | tf_op | source)
XLA Modules:
  0.0 62.9 jit_solution(17959113831518909278)
XLA Ops:
  0.6 0.0 copy-start
  0.7 1.3 %to_spectral.3 = bf16[32,32,128]{2,1,0:T(8,128)(2,1)S(1)} custom-call(s32[1]{0:T(128)} %bitcast.1.s_ref, bf16[128,256]{1,0:T(8,128)(2,1)} %constant.52.clone.t_hbm, bf16[256,1024]{1,0:T(8,128)(2,1)} %bitcast.15, bf16[256,1024]{1,0:T(8,128)(2,1)} %bitcast.14), custom_call_target="tpu_custom_call" | custom-call | tf_op jit(solution)/shard_map/to_spectral/pallas_call | solution.py:106
  2.0 0.8 %collective-permute-start.1 = (bf16[32,32,128]{2,1,0:T(8,128)(2,1)S(1)}, bf16[32,32,128]{2,1,0:T(8,128)(2,1)S(1)}, u32[]{:S(2)}, u32[]{:S(2)}) collective-permute-start(bf16[32,32,128]{2,1,0:T(8,128)(2,1)S(1)} %to_spectral.3), channel_id=1, source_target_pairs={{0,480},{32,0},{64,32},{96,64},{128,96},{160,128},{192,160},{224,1... | collective-permute-start | bytes 786440 | tf_op jit(solution)/shard_map/ppermute | solution.py:423
  2.8 2.0 %to_spectral.2._ = bf16[32,64,128]{2,1,0:T(8,128)(2,1)} custom-call(s32[1]{0:T(128)} %bitcast.1.s_ref, bf16[128,256]{1,0:T(8,128)(2,1)} %constant.53.clone.t_hbm, bf16[256,1024]{1,0:T(8,128)(2,1)} %bitcast.16), custom_call_target="tpu_custom_call" | custom-call | tf_op jit(solution)/shard_map/to_spectral/pallas_call | solution.py:106
  4.8 1.9 %collective-permute-done.1.du_ref = bf16[32,32,128]{2,1,0:T(8,128)(2,1)S(1)} collective-permute-done((bf16[32,32,128]{2,1,0:T(8,128)(2,1)S(1)}, bf16[32,32,128]{2,1,0:T(8,128)(2,1)S(1)}, u32[]{:S(2)}, u32[]{:S(2)}) %collective-permute-start.1) | collective-permute-done | bytes 262176 | tf_op jit(solution)/shard_map/ppermute | solution.py:423
  6.7 0.7 %lower_halves.1 = bf16[32,64,128]{2,1,0:T(8,128)(2,1)} custom-call(bf16[32,64,128]{2,1,0:T(8,128)(2,1)} %to_spectral.2._, bf16[32,32,128]{2,1,0:T(8,128)(2,1)S(1)} %collective-permute-done.1.du_ref), custom_call_target="tpu_custom_call", output_to_operand_aliasing={{}: (0, {})} | custom-call | tf_op jit(solution)/shard_map/lower_halves/pallas_call | solution.py:132
  7.5 0.0 copy-start.6
  7.5 13.2 %all-to-all-start = ((bf16[32,64,128]{2,1,0:T(8,128)(2,1)}), bf16[32,64,128]{2,1,0:T(8,128)(2,1)S(1)}, u32[]{:S(2)}, u32[]{:S(2)}) async-start(bf16[32,64,128]{2,1,0:T(8,128)(2,1)} %lower_halves.1), calls=%async_computation | async-start | bytes 1048576 | tf_op jit(solution)/shard_map/all_to_all | solution.py:428
  20.7 0.0 copy-done.6
  20.7 0.0 copy-start.2
  20.7 1.6 %collective-permute-start = (bf16[1,2,128,1024]{3,2,1,0:T(8,128)(2,1)S(1)}, bf16[1,2,128,1024]{3,2,1,0:T(8,128)(2,1)S(1)}, u32[]{:S(2)}, u32[]{:S(2)}) collective-permute-start(bf16[1,2,128,1024]{3,2,1,0:T(8,128)(2,1)S(1)} %copy-done.6), channel_id=1, source_target_pairs={{0,480},{32,0},{64,32},{96,64},{128,96},{160,128},{192,160},{224,1... | collective-permute-start | bytes 1572872 | tf_op jit(solution)/shard_map/ppermute | solution.py:429
  22.4 0.0 copy-done
  22.4 0.2 dynamic-slice_reduce_fusion
  22.6 0.1 pad_add_fusion.s_ref
  22.6 0.0 copy-done.2
  22.6 1.7 %block_params.1 = (bf16[4,256,256]{2,1,0:T(8,128)(2,1)S(1)}, bf16[4,256,256]{2,1,0:T(8,128)(2,1)S(1)}, f32[4,1,256]{2,1,0:T(1,128)S(1)}, f32[2,8,1,256]{3,2,1,0:T(1,128)S(1)}, bf16[2,64,64]{2,1,0:T(8,128)(2,1)S(1)}) custom-call(s32[4]{0:T(128)S(1)} %pad_add_fusion.s_ref, bf16[1,2,2,1024,128]{4,3,2,1,0:T(8,128)(2,1)} %w1_hbm.1, ...), custom_call_target="tpu_custom_call" | custom-call | tf_op jit(solution)/shard_map/block_params/pallas_call | solution.py:221
  24.3 4.7 %collective-permute-done = bf16[1,2,128,1024]{3,2,1,0:T(8,128)(2,1)S(1)} collective-permute-done((bf16[1,2,128,1024]{3,2,1,0:T(8,128)(2,1)S(1)}, bf16[1,2,128,1024]{3,2,1,0:T(8,128)(2,1)S(1)}, u32[]{:S(2)}, u32[]{:S(2)}) %collective-permute-start) | collective-permute-done | bytes 524320 | tf_op jit(solution)/shard_map/ppermute | solution.py:429
  29.1 0.0 copy-done.5
  29.1 0.1 bitcast_select_fusion
  29.1 9.4 %all-to-all-done.parts_ref = bf16[32,64,128]{2,1,0:T(8,128)(2,1)S(1)} async-done(((bf16[32,64,128]{2,1,0:T(8,128)(2,1)}), bf16[32,64,128]{2,1,0:T(8,128)(2,1)S(1)}, u32[]{:S(2)}, u32[]{:S(2)}) %all-to-all-start) | async-done | bytes 524320 | tf_op jit(solution)/shard_map/all_to_all | solution.py:428
  38.6 0.0 copy-done.3
  38.6 2.6 %spectral_chain.1 = (bf16[32,32,128]{2,1,0:T(8,128)(2,1)}, f32[272,128]{1,0:T(8,128)S(1)}, bf16[272,128]{1,0:T(8,128)(2,1)S(1)}, bf16[272,128]{1,0:T(8,128)(2,1)S(1)}, bf16[272,128]{1,0:T(8,128)(2,1)S(1)}) custom-call(s32[1]{0:T(128)} %bitcast.q_ref, bf16[32,64,128]{2,1,0:T(8,128)(2,1)S(1)} %all-to-all-done.parts_ref, bf16[128,128]{1,0:T(8,128)(2,1)S(1)} %copy-done.4, ...), custom_call_target="tpu_custom_call" | custom-call | tf_op jit(solution)/shard_map/spectral_chain/pallas_call | solution.py:336
  41.2 5.2 %all-to-all-start.1 = ((bf16[32,32,128]{2,1,0:T(8,128)(2,1)}), bf16[32,32,128]{2,1,0:T(8,128)(2,1)S(1)}, u32[]{:S(2)}, u32[]{:S(2)}) async-start(bf16[32,32,128]{2,1,0:T(8,128)(2,1)} %get-tuple-element.31), calls=%async_computation.1 | async-start | bytes 524288 | tf_op jit(solution)/shard_map/all_to_all | solution.py:437
  46.4 3.7 %collective-permute-start.2 = (bf16[272,128]{1,0:T(8,128)(2,1)S(1)}, bf16[272,128]{1,0:T(8,128)(2,1)S(1)}, u32[]{:S(2)}, u32[]{:S(2)}) collective-permute-start(bf16[272,128]{1,0:T(8,128)(2,1)S(1)} %get-tuple-element.36), channel_id=1, source_target_pairs={{0,1},{1,0},{2,3},{3,2},{4,5},{5,4},{6,7},{7,6},{8,9},{9,8},{10,11... | collective-permute-start | bytes 208904 | tf_op jit(solution)/shard_map/ppermute | solution.py:440
  50.1 4.6 %collective-permute-start.3 = (bf16[272,128]{1,0:T(8,128)(2,1)S(1)}, bf16[272,128]{1,0:T(8,128)(2,1)S(1)}, u32[]{:S(2)}, u32[]{:S(2)}) collective-permute-start(bf16[272,128]{1,0:T(8,128)(2,1)S(1)} %get-tuple-element.37), channel_id=1, source_target_pairs={{0,2},{1,3},{2,0},{3,1},{4,6},{5,7},{6,4},{7,5},{8,10},{9,11},{10,... | collective-permute-start | bytes 208904 | tf_op jit(solution)/shard_map/ppermute | solution.py:440
  54.7 2.1 %collective-permute-start.4 = (bf16[272,128]{1,0:T(8,128)(2,1)S(1)}, bf16[272,128]{1,0:T(8,128)(2,1)S(1)}, u32[]{:S(2)}, u32[]{:S(2)}) collective-permute-start(bf16[272,128]{1,0:T(8,128)(2,1)S(1)} %get-tuple-element.38), channel_id=1, source_target_pairs={{0,3},{1,2},{2,1},{3,0},{4,7},{5,6},{6,5},{7,4},{8,11},{9,10},{10,... | collective-permute-start | bytes 208904 | tf_op jit(solution)/shard_map/ppermute | solution.py:440
  56.8 3.5 %all-to-all-done.1.p_ref = bf16[32,32,128]{2,1,0:T(8,128)(2,1)S(1)} async-done(((bf16[32,32,128]{2,1,0:T(8,128)(2,1)}), bf16[32,32,128]{2,1,0:T(8,128)(2,1)S(1)}, u32[]{:S(2)}, u32[]{:S(2)}) %all-to-all-start.1) | async-done | bytes 262176 | tf_op jit(solution)/shard_map/all_to_all | solution.py:437
  60.3 1.0 %to_cells.1 = bf16[256,1024]{1,0:T(8,128)(2,1)} custom-call(bf16[256,128]{1,0:T(8,128)(2,1)S(1)} %copy-done.1, bf16[32,32,128]{2,1,0:T(8,128)(2,1)S(1)} %all-to-all-done.1.p_ref, bf16[256,1024]{1,0:T(8,128)(2,1)S(1)} %bitcast.13), custom_call_target="tpu_custom_call" | custom-call | tf_op jit(solution)/shard_map/to_cells/pallas_call | solution.py:168
  61.4 0.0 collective-permute-done.2.refs_1_
  61.4 0.0 collective-permute-done.3.refs_2_
  61.4 0.7 %collective-permute-done.4.refs_3_ = bf16[272,128]{1,0:T(8,128)(2,1)S(1)} collective-permute-done((bf16[272,128]{1,0:T(8,128)(2,1)S(1)}, bf16[272,128]{1,0:T(8,128)(2,1)S(1)}, u32[]{:S(2)}, u32[]{:S(2)}) %collective-permute-start.4) | collective-permute-done | bytes 69664 | tf_op jit(solution)/shard_map/ppermute | solution.py:440
  62.1 0.8 %gradient_sum.1 = (f32[128,128]{1,0:T(8,128)}, f32[128,128]{1,0:T(8,128)}, f32[8,32]{1,0:T(8,128)}) custom-call(s32[1]{0:T(128)} %bitcast.q_ref, f32[272,128]{1,0:T(8,128)S(1)} %get-tuple-element.35.refs_0_, bf16[272,128]{1,0:T(8,128)(2,1)S(1)} %collective-permute-done.2.refs_1_, bf16[272,128]{1,0:T(8,128)(2,1)S(1)} %collective-permute-done.3.refs_2_, ...), custom_call_target="tpu_custom_call" | custom-call | tf_op jit(solution)/shard_map/gradient_sum/pallas_call | solution.py:382
  (6 shorter events, 0.0 us)
Async XLA Ops:
  0.6 21.7 %copy-start = (s32[1,2,8]{2,1,0:T(2,128)S(1)}, s32[1,2,8]{2,1,0:T(2,128)}, u32[]{:S(2)}) copy-start(s32[1,2,8]{2,1,0:T(2,128)} %param.18) | copy-start | bytes 196
  2.0 4.8 %collective-permute-start.1 = (bf16[32,32,128]{2,1,0:T(8,128)(2,1)S(1)}, bf16[32,32,128]{2,1,0:T(8,128)(2,1)S(1)}, u32[]{:S(2)}, u32[]{:S(2)}) collective-permute-start(bf16[32,32,128]{2,1,0:T(8,128)(2,1)S(1)} %to_spectral.3), channel_id=1, source_target_pairs={{0,480},{32,0},{64,32},{96,64},{128,96},{160,128},{192,160},{224,1... | collective-permute-start | bytes 786440 | tf_op jit(solution)/shard_map/ppermute | solution.py:423
  7.5 13.2 %copy-start.6 = (bf16[1,2,128,1024]{3,2,1,0:T(8,128)(2,1)S(1)}, bf16[1,2,128,1024]{3,2,1,0:T(8,128)(2,1)}, u32[]{:S(2)}) copy-start(bf16[1,2,128,1024]{3,2,1,0:T(8,128)(2,1)} %param.13) | copy-start | bytes 1572868
  7.5 31.1 %all-to-all-start = ((bf16[32,64,128]{2,1,0:T(8,128)(2,1)}), bf16[32,64,128]{2,1,0:T(8,128)(2,1)S(1)}, u32[]{:S(2)}, u32[]{:S(2)}) async-start(bf16[32,64,128]{2,1,0:T(8,128)(2,1)} %lower_halves.1), calls=%async_computation | async-start | bytes 1048576 | tf_op jit(solution)/shard_map/all_to_all | solution.py:428
  20.7 1.9 %copy-start.2 = (f32[1,2,2,2,1024]{4,3,2,1,0:T(2,128)S(1)}, f32[1,2,2,2,1024]{4,3,2,1,0:T(2,128)}, u32[]{:S(2)}) copy-start(f32[1,2,2,2,1024]{4,3,2,1,0:T(2,128)} %b_ref.1) | copy-start | bytes 98308
  20.7 8.3 %collective-permute-start = (bf16[1,2,128,1024]{3,2,1,0:T(8,128)(2,1)S(1)}, bf16[1,2,128,1024]{3,2,1,0:T(8,128)(2,1)S(1)}, u32[]{:S(2)}, u32[]{:S(2)}) collective-permute-start(bf16[1,2,128,1024]{3,2,1,0:T(8,128)(2,1)S(1)} %copy-done.6), channel_id=1, source_target_pairs={{0,480},{32,0},{64,32},{96,64},{128,96},{160,128},{192,160},{224,1... | collective-permute-start | bytes 1572872 | tf_op jit(solution)/shard_map/ppermute | solution.py:429
  22.6 6.4 %copy-start.5 = (bf16[2,128,1024]{2,1,0:T(8,128)(2,1)S(1)}, bf16[2,128,1024]{2,1,0:T(8,128)(2,1)}, u32[]{:S(2)}) copy-start(bf16[2,128,1024]{2,1,0:T(8,128)(2,1)} %param.14) | copy-start | bytes 1572868
  29.1 9.5 %copy-start.3 = (bf16[128,128]{1,0:T(8,128)(2,1)S(1)}, bf16[128,128]{1,0:T(8,128)(2,1)}, u32[]{:S(2)}) copy-start(bf16[128,128]{1,0:T(8,128)(2,1)} %constant.55.clone.lt_ref) | copy-start | bytes 98308
  29.1 9.5 %copy-start.4 = (bf16[128,128]{1,0:T(8,128)(2,1)S(1)}, bf16[128,128]{1,0:T(8,128)(2,1)}, u32[]{:S(2)}) copy-start(bf16[128,128]{1,0:T(8,128)(2,1)} %constant.54.clone.l_ref) | copy-start | bytes 98308
  41.2 19.1 %copy-start.1 = (bf16[256,128]{1,0:T(8,128)(2,1)S(1)}, bf16[256,128]{1,0:T(8,128)(2,1)}, u32[]{:S(2)}) copy-start(bf16[256,128]{1,0:T(8,128)(2,1)} %constant.56.clone.t_ref) | copy-start | bytes 196612
  41.2 19.1 %all-to-all-start.1 = ((bf16[32,32,128]{2,1,0:T(8,128)(2,1)}), bf16[32,32,128]{2,1,0:T(8,128)(2,1)S(1)}, u32[]{:S(2)}, u32[]{:S(2)}) async-start(bf16[32,32,128]{2,1,0:T(8,128)(2,1)} %get-tuple-element.31), calls=%async_computation.1 | async-start | bytes 524288 | tf_op jit(solution)/shard_map/all_to_all | solution.py:437
  46.4 15.0 %collective-permute-start.2 = (bf16[272,128]{1,0:T(8,128)(2,1)S(1)}, bf16[272,128]{1,0:T(8,128)(2,1)S(1)}, u32[]{:S(2)}, u32[]{:S(2)}) collective-permute-start(bf16[272,128]{1,0:T(8,128)(2,1)S(1)} %get-tuple-element.36), channel_id=1, source_target_pairs={{0,1},{1,0},{2,3},{3,2},{4,5},{5,4},{6,7},{7,6},{8,9},{9,8},{10,11... | collective-permute-start | bytes 208904 | tf_op jit(solution)/shard_map/ppermute | solution.py:440
  50.1 11.3 %collective-permute-start.3 = (bf16[272,128]{1,0:T(8,128)(2,1)S(1)}, bf16[272,128]{1,0:T(8,128)(2,1)S(1)}, u32[]{:S(2)}, u32[]{:S(2)}) collective-permute-start(bf16[272,128]{1,0:T(8,128)(2,1)S(1)} %get-tuple-element.37), channel_id=1, source_target_pairs={{0,2},{1,3},{2,0},{3,1},{4,6},{5,7},{6,4},{7,5},{8,10},{9,11},{10,... | collective-permute-start | bytes 208904 | tf_op jit(solution)/shard_map/ppermute | solution.py:440
  54.7 7.4 %collective-permute-start.4 = (bf16[272,128]{1,0:T(8,128)(2,1)S(1)}, bf16[272,128]{1,0:T(8,128)(2,1)S(1)}, u32[]{:S(2)}, u32[]{:S(2)}) collective-permute-start(bf16[272,128]{1,0:T(8,128)(2,1)S(1)} %get-tuple-element.38), channel_id=1, source_target_pairs={{0,3},{1,2},{2,1},{3,0},{4,7},{5,6},{6,5},{7,4},{8,11},{9,10},{10,... | collective-permute-start | bytes 208904 | tf_op jit(solution)/shard_map/ppermute | solution.py:440
